TPU v7x, 32 devices: a whole 2x2x4 slice. The times are simulated.
32 devices in a mesh: dom: 8 (over z, y), col: 4 (over x, core).
Axes of the slice: x: 2, y: 2, z: 4, core: 2. Of those that a mesh axis runs over, the one named last changes fastest.
Arguments:
- margin: bfloat16 [64, 27, 128, 128], P(('dom', 'col')), may hold values from -0.05 to 1.05
- neighbours: int32 [64, 27], P('dom'), may hold values from 0 to 9, as said below
- pattern: int32 [64, 27], P('dom'), may hold values from 0 to 1, as said below
- colour: int32 [64], replicated, may hold values from 0 to 3
- send_list: int32 [8, 2, 1], replicated, may hold values from 0 to 7
Outputs:
- probe_images: float32 [8192, 512], P('dom', 'col')
Inputs may be any that keep to these rules, and one draw needn't show every extreme that they name: `neighbours`: slot 13 of every block row names the block itself. `pattern`: slot 13 of every block row is present.
All inputs are finite; a program needn't handle non-finite values.
Results may differ from a plain program's by a relative error of at most 0.0011.
Values may be sent and summed in bfloat16 or wider, within the bound.
No kernel may reach another device: no remote copies, remote signals or barrier semaphores. Data moves between devices by JAX's collectives and lax.ppermute only.
A program may use at most 128 MiB of HBM per device.

v0:
```python
import math

import jax
import jax.numpy as jnp
from jax import lax
from jax.sharding import PartitionSpec as P

CENTRE = 1.0
HALF_WIDTH = 0.9


def padded(value, sides, width):
    for axis, dim in sides:
        size, length = (lax.axis_size(axis), value.shape[dim])
        up = [(i, (i + 1) % size) for i in range(size)]
        down = [(j, i) for i, j in up]
        last = lax.slice_in_dim(value, length - width, length, axis=dim)
        first = lax.slice_in_dim(value, 0, width, axis=dim)
        before = lax.ppermute(last, axis, up)
        after = lax.ppermute(first, axis, down)
        value = jnp.concatenate([before, value, after], axis=dim)
    return value


def cheb_coefficients():
    samples = []
    for index_k in range(3):
        angle_value = math.pi * (index_k + 0.5) / 3.0
        samples.append((angle_value, (CENTRE + HALF_WIDTH * math.cos(angle_value)) ** (-0.5)))
    coeffs = []
    for order in range(3):
        coeffs.append(
            2.0
            / 3.0
            * sum((value * math.cos(order * angle_value) for angle_value, value in samples))
        )
    coeffs[0] = 0.5 * coeffs[0]
    return coeffs


def combine_terms(coeffs, product, first, probe):
    applied = (product - CENTRE * first) / HALF_WIDTH
    return coeffs[0] * probe + coeffs[1] * first + coeffs[2] * (2.0 * applied - probe)


def per_device(margin, neighbours, pattern, colour, send_list):
    coeffs = cheb_coefficients()
    rows_dev = margin.shape[0]
    orbits = margin.shape[2]
    dom_count = neighbours.shape[0]
    ncolour = lax.axis_size("col")
    ndomain = lax.axis_size("dom")
    domain = lax.axis_index("dom")
    shade = lax.axis_index("col")
    lower = (domain + ndomain - 1) % ndomain
    upper = (domain + 1) % ndomain
    own_ids = domain * dom_count + jnp.arange(dom_count, dtype=jnp.int32)
    low_ids = lower * dom_count + send_list[lower, 1]
    high_ids = upper * dom_count + send_list[upper, 0]
    ext_ids = jnp.concatenate([own_ids, low_ids, high_ids], axis=0)
    slot_colour = colour[ext_ids][neighbours]
    dom_colour = colour[own_ids]
    row_start = shade * rows_dev
    my_live = lax.dynamic_slice_in_dim(pattern, row_start, rows_dev, 0)
    my_slot_colour = lax.dynamic_slice_in_dim(slot_colour, row_start, rows_dev, 0)
    my_colour = lax.dynamic_slice_in_dim(dom_colour, row_start, rows_dev, 0)
    identity = jnp.eye(orbits, dtype=jnp.float32)
    shades = jnp.arange(ncolour, dtype=jnp.int32)
    onehot = (
        (my_slot_colour[:, :, None] == shades[None, None, :]) & (my_live[:, :, None] == 1)
    ).astype(jnp.bfloat16)
    spread = jnp.einsum("bkc,bkij->bicj", onehot, margin, preferred_element_type=jnp.float32)
    spread = spread.reshape(rows_dev, orbits, ncolour * orbits)
    hits = (my_colour[:, None] == shades[None, :]).astype(jnp.float32)
    probe_all = (hits[:, None, :, None] * identity[None, :, None, :]).reshape(
        rows_dev, orbits, ncolour * orbits
    )
    first_all = ((spread - CENTRE * probe_all) / HALF_WIDTH).astype(jnp.bfloat16)
    first_own = lax.all_to_all(first_all, "col", split_axis=2, concat_axis=0, tiled=True)
    outgoing = first_own[send_list[domain]]
    bordered = padded(outgoing, (("dom", 0),), 1)
    extended = jnp.concatenate([first_own, bordered[0], bordered[3]], axis=0)
    own_hit = (dom_colour == shade).astype(jnp.float32)
    fetched = jnp.where(
        pattern[:, :, None, None] == 1, extended[neighbours], jnp.zeros((), jnp.bfloat16)
    )
    product = jnp.einsum(
        "bkij,bkjl->bil",
        lax.all_gather(margin, "col", axis=0, tiled=True),
        fetched,
        preferred_element_type=jnp.float32,
    )
    first = first_own.astype(jnp.float32)
    probe = own_hit[:, None, None] * identity[None, :, :]
    images = combine_terms(coeffs, product, first, probe)
    return images.reshape(dom_count * orbits, orbits)


def solution(mesh):
    placed = (P(("dom", "col"), None, None, None), P("dom", None), P("dom", None), P(), P())
    return jax.shard_map(
        per_device, mesh=mesh, in_specs=placed, out_specs=P("dom", "col"), check_vma=False
    )
```

profile of v0, /device:TPU:0, one launch (start us, length us, event | category | flops | bytes accessed | tf_op | source)
XLA Modules:
  0.0 80.1 jit_solution(2779056784277049401)
XLA Ops:
  6.6 0.7 all-gather.2.cloned.1.call-update
  7.3 0.6 gather_fusion
  8.2 1.3 %constant_dynamic-slice_fusion.4 = (s32[1,1,1]{0,2,1:T(1,128)}, s32[1,1,1]{0,2,1:T(1,128)}) fusion(s32[8,2,1]{0,2,1:T(1,128)} %param.9, s32[]{:T(128)S(6)} %select_n.67, s32[]{:T(128)S(6)} %select_n.69), kind=kLoop, calls=%fused_computation.50 | loop fusion | bytes 24 | tf_op jit(solution)/shard_map/dynamic_slice | solution.py:58
  10.9 0.1 fusion.37
  11.0 0.7 gather_fusion.1
  11.6 0.7 compare_select_fusion
  12.3 0.1 reshape.235
  12.4 1.9 %gather_fusion.2 = s32[216]{0:T(256)S(1)} fusion(s32[10]{0:T(128)S(1)} %gather_fusion.1, s32[1024]{0:T(1024)S(1)} %pad_clamp_fusion.1), kind=kCustom, calls=%fused_computation.2 | custom fusion | bytes 2592 | tf_op jit(solution)/shard_map/gather | solution.py:61
  14.3 0.1 reshape.234
  14.5 1.1 %fusion.6 = f32[2,128,4,128]{3,2,1,0:T(4,128)S(1)} fusion(bf16[2,27,128,128]{3,2,1,0:T(8,128)(2,1)S(1)} %copy-done.1, s32[2,27]{1,0:T(2,128)S(1)} %constant_dynamic-slice_fusion.2, pred[2,27]{1,0:T(4,128)(4,1)S(1)} %fusion.34), kind=kOutput, calls=%fused_computation.11 | convolution fusion | flops 7078320 | bytes 2294030 | tf_op jit(solution)/shard_map/bkc,bkij->bicj/dot_general | solution.py:72
  15.6 0.2 reshape.215
  15.8 0.1 multiply_convert_fusion
  15.9 0.9 %copy.15 = bf16[2,128,512]{1,0,2:T(2,128)(2,1)} copy(bf16[2,128,512]{2,1,0:T(8,128)(2,1)S(1)} %multiply_convert_fusion) | data formatting | bytes 524288 | tf_op jit(solution)/shard_map/convert_element_type | solution.py:78
  16.8 4.2 %all-to-all-start = ((bf16[2,128,512]{1,0,2:T(2,128)(2,1)}), bf16[2,128,512]{1,0,2:T(2,128)(2,1)S(1)}, u32[]{:S(2)}, u32[]{:S(2)}) async-start(bf16[2,128,512]{1,0,2:T(2,128)(2,1)} %copy.15), calls=%async_computation | async-start | bytes 524288 | tf_op jit(solution)/shard_map/all_to_all | solution.py:79
  21.0 0.2 fusion.35
  21.2 8.9 %all-to-all-done = bf16[2,128,512]{1,0,2:T(2,128)(2,1)S(1)} async-done(((bf16[2,128,512]{1,0,2:T(2,128)(2,1)}), bf16[2,128,512]{1,0,2:T(2,128)(2,1)S(1)}, u32[]{:S(2)}, u32[]{:S(2)}) %all-to-all-start) | async-done | bytes 262176 | tf_op jit(solution)/shard_map/all_to_all | solution.py:79
  30.2 0.2 copy.16
  30.3 0.6 gather_fusion.3
  30.9 2.2 %collective-permute-start = (bf16[1,1,128,128]{3,2,1,0:T(8,128)(2,1)S(1)}, bf16[1,1,128,128]{3,2,1,0:T(8,128)(2,1)S(1)}, u32[]{:S(2)}, u32[]{:S(2)}) collective-permute-start(bf16[1,1,128,128]{3,2,1,0:T(8,128)(2,1)S(1)} %get-tuple-element.5), channel_id=1, source_target_pairs={{0,4},{4,8},{8,12},{12,16},{16,20},{20,24},{24,28},{28,0},{1,5},{5... | collective-permute-start | bytes 98312 | tf_op jit(solution)/shard_map/ppermute | solution.py:19
  33.1 3.1 %collective-permute-start.1 = (bf16[1,1,128,128]{3,2,1,0:T(8,128)(2,1)S(1)}, bf16[1,1,128,128]{3,2,1,0:T(8,128)(2,1)S(1)}, u32[]{:S(2)}, u32[]{:S(2)}) collective-permute-start(bf16[1,1,128,128]{3,2,1,0:T(8,128)(2,1)S(1)} %get-tuple-element.6), channel_id=1, source_target_pairs={{4,0},{8,4},{12,8},{16,12},{20,16},{24,20},{28,24},{0,28},{5,1},{9... | collective-permute-start | bytes 98312 | tf_op jit(solution)/shard_map/ppermute | solution.py:20
  36.2 1.8 %collective-permute-done = bf16[1,1,128,128]{3,2,1,0:T(8,128)(2,1)S(1)} collective-permute-done((bf16[1,1,128,128]{3,2,1,0:T(8,128)(2,1)S(1)}, bf16[1,1,128,128]{3,2,1,0:T(8,128)(2,1)S(1)}, u32[]{:S(2)}, u32[]{:S(2)}) %collective-permute-start) | collective-permute-done | bytes 32800 | tf_op jit(solution)/shard_map/ppermute | solution.py:19
  38.1 8.4 %gather_fusion.4 = bf16[216,128,128]{2,1,0:T(8,128)(2,1)} fusion(bf16[10,128,128]{2,1,0:T(8,128)(2,1)S(1)} %pad_maximum_fusion, s32[1024]{0:T(1024)S(1)} %pad_clamp_fusion.1), kind=kCustom, calls=%fused_computation.4 | custom fusion | bytes 14156640 | tf_op jit(solution)/shard_map/gather | solution.py:85
  46.5 18.8 %all-gather.2.cloned.1.call-done = bf16[8,27,128,128]{3,2,1,0:T(8,128)(2,1)} async-done(((bf16[2,27,128,128]{3,2,1,0:T(8,128)(2,1)}), bf16[8,27,128,128]{3,2,1,0:T(8,128)(2,1)}) %all-gather.2.cloned.1.call-update) | async-done | bytes 7077904 | tf_op jit(solution)/shard_map/all_gather | solution.py:89
  65.3 7.9 %fusion.24 = f32[8,128,128]{2,1,0:T(8,128)} fusion(bf16[8,27,128,128]{3,2,1,0:T(8,128)(2,1)} %all-gather.2.cloned.1.call-done, bf16[8,27,128,128]{3,2,1,0:T(8,128)(2,1)} %bitcast.60, pred[8,27]{1,0:T(8,128)(4,1)S(1)} %broadcast_compare_fusion, bf16[8,128,128]{2,1,0:T(8,128)(2,1)S(1)} %bitcast.63, f32[128,128]{1,0:T(8,128)S(1)} %fusion.28, ...), kind=kOutput, calls=%fused_computation.17 | convolution fusion | flops 910819328 | bytes 15007992 | tf_op jit(solution)/shard_map/bkij,bkjl->bil/dot_general | solution.py:87
  (30 shorter events, 0.5 us)
Async XLA Ops:
  6.5 0.8 copy-start
  6.5 8.0 %copy-start.1 = (bf16[2,27,128,128]{3,2,1,0:T(8,128)(2,1)S(1)}, bf16[2,27,128,128]{3,2,1,0:T(8,128)(2,1)}, u32[]{:S(2)}) copy-start(bf16[2,27,128,128]{3,2,1,0:T(8,128)(2,1)} %param.5) | copy-start | bytes 5308420
  6.5 14.5 %copy-start.3 = (s32[8,2,1]{0,2,1:T(1,128)S(1)}, s32[8,2,1]{0,2,1:T(1,128)}, u32[]{:S(2)}) copy-start(s32[8,2,1]{0,2,1:T(1,128)} %param.9) | copy-start | bytes 196
  6.5 7.9 %copy-start.2 = (s32[8,27]{1,0:T(8,128)S(1)}, s32[8,27]{1,0:T(8,128)}, u32[]{:S(2)}) copy-start(s32[8,27]{1,0:T(8,128)} %param.7) | copy-start | bytes 2596
  6.5 58.8 %all-gather.2.cloned.1.call-start = ((), (), s32[]{:S(2)}) async-start(), calls=%async_computation.1 | async-start | bytes 8847360 | tf_op jit(solution)/shard_map/all_gather | solution.py:89
  16.8 13.4 %all-to-all-start = ((bf16[2,128,512]{1,0,2:T(2,128)(2,1)}), bf16[2,128,512]{1,0,2:T(2,128)(2,1)S(1)}, u32[]{:S(2)}, u32[]{:S(2)}) async-start(bf16[2,128,512]{1,0,2:T(2,128)(2,1)} %copy.15), calls=%async_computation | async-start | bytes 524288 | tf_op jit(solution)/shard_map/all_to_all | solution.py:79
  30.9 7.1 %collective-permute-start = (bf16[1,1,128,128]{3,2,1,0:T(8,128)(2,1)S(1)}, bf16[1,1,128,128]{3,2,1,0:T(8,128)(2,1)S(1)}, u32[]{:S(2)}, u32[]{:S(2)}) collective-permute-start(bf16[1,1,128,128]{3,2,1,0:T(8,128)(2,1)S(1)} %get-tuple-element.5), channel_id=1, source_target_pairs={{0,4},{4,8},{8,12},{12,16},{16,20},{20,24},{24,28},{28,0},{1,5},{5... | collective-permute-start | bytes 98312 | tf_op jit(solution)/shard_map/ppermute | solution.py:19
  33.1 4.9 %collective-permute-start.1 = (bf16[1,1,128,128]{3,2,1,0:T(8,128)(2,1)S(1)}, bf16[1,1,128,128]{3,2,1,0:T(8,128)(2,1)S(1)}, u32[]{:S(2)}, u32[]{:S(2)}) collective-permute-start(bf16[1,1,128,128]{3,2,1,0:T(8,128)(2,1)S(1)} %get-tuple-element.6), channel_id=1, source_target_pairs={{4,0},{8,4},{12,8},{16,12},{20,16},{24,20},{28,24},{0,28},{5,1},{9... | collective-permute-start | bytes 98312 | tf_op jit(solution)/shard_map/ppermute | solution.py:20
Sparse Core Ops, SparseCore 0:
  8.9 56.3 all-gather.1
where the time goes:
time: 80.3 us; the launch traced here: 80.1 us
  waiting for transfers between devices  30.3 us (38%)
  local copies, waits for them, and re-layouts  15.3 us (19%)
  between operations  14.9 us (19%)
  starting transfers between devices  9.55 us (12%)
  matrix products  8.98 us (11%)
  other arithmetic  1.07 us (1%)
    all_gather x1, waiting for transfers between devices, per_device(): lax.all_gather(margin, 'col', axis=0, tiled=True)  18.8 us
    all_to_all x1, waiting for transfers between devices, per_device(): lax.all_to_all(first_all, 'col', split_axis=2, concat_axis=0, tiled=True)  8.94 us
    gather x1, local copies, waits for them, and re-layouts, per_device(): extended[neighbours]  8.36 us
    dot_general x1, matrix products, per_device(): jnp.einsum('bkij,bkjl->bil', lax.all_gather(margin, 'col', axis=0, tiled=...  7.9 us
    all_to_all x1, starting transfers between devices, per_device(): lax.all_to_all(first_all, 'col', split_axis=2, concat_axis=0, tiled=True)  4.21 us
    ppermute x1, starting transfers between devices, padded(): after = lax.ppermute(first, axis, down)  3.11 us
    gather x3, local copies, waits for them, and re-layouts, per_device(): slot_colour = colour[ext_ids][neighbours]  2.61 us
    ppermute x1, starting transfers between devices, padded(): before = lax.ppermute(last, axis, up)  2.2 us
  transfers between devices with their start and end apart: 4, of which 3 were waited for; matrix products, arithmetic and copies ran while one was open for 22% of the time, Pallas kernels for 0%

commit v1 on v0

v1 whole, which is shorter than its diff:
```python
import functools
import math

import jax
import jax.numpy as jnp
from jax import lax
from jax.experimental import pallas as pl
from jax.experimental.pallas import tpu as pltpu
from jax.sharding import PartitionSpec as P

CENTRE = 1.0
HALF_WIDTH = 0.9
ANY = pl.BlockSpec(memory_space=pl.ANY)
SMEM = pl.BlockSpec(memory_space=pltpu.SMEM)
VMEM = pl.BlockSpec(memory_space=pltpu.VMEM)


def cheb_coefficients():
    samples = []
    for index_k in range(3):
        angle_value = math.pi * (index_k + 0.5) / 3.0
        samples.append((angle_value, (CENTRE + HALF_WIDTH * math.cos(angle_value)) ** (-0.5)))
    coeffs = []
    for order in range(3):
        coeffs.append(
            2.0
            / 3.0
            * sum((value * math.cos(order * angle_value) for angle_value, value in samples))
        )
    coeffs[0] = 0.5 * coeffs[0]
    return coeffs


def first_kernel(
    ndomain, ncolour, neighbours, pattern, colour, send_list, margin, first, blocks, sums, table, sems
):
    domain = lax.axis_index("dom")
    shade = lax.axis_index("col")
    rows, slots = margin.shape[:2]
    own = neighbours.shape[0]
    width = send_list.shape[2]
    copies = [
        pltpu.make_async_copy(margin.at[row], blocks.at[row], sems.at[row]) for row in range(rows)
    ]
    for copy in copies:
        copy.start()
    lower = lax.rem(domain + ndomain - 1, ndomain)
    upper = lax.rem(domain + 1, ndomain)

    @pl.loop(0, own)
    def _(i):
        table[i] = colour[domain * own + i]

    for i in range(width):
        table[own + i] = colour[lower * own + send_list[lower, 1, i]]
        table[own + width + i] = colour[upper * own + send_list[upper, 0, i]]
    sums[...] = jnp.zeros_like(sums)
    orbits = margin.shape[2]
    eye = (
        lax.broadcasted_iota(jnp.int32, (orbits, orbits), 0)
        == lax.broadcasted_iota(jnp.int32, (orbits, orbits), 1)
    ).astype(jnp.float32)
    for row in range(rows):
        block = shade * rows + row
        copies[row].wait()

        @pl.loop(0, slots)
        def _(k):
            live = pattern[block, k] == 1
            where = jnp.where(live, table[neighbours[block, k]], ncolour)
            sums[row, where] += blocks[row, k].astype(jnp.float32)

        sums[row, table[block]] -= CENTRE * eye
        for c in range(ncolour):
            first[row, :, c * orbits : (c + 1) * orbits] = (sums[row, c] / HALF_WIDTH).astype(
                jnp.bfloat16
            )


def first_terms(ndomain, ncolour, neighbours, pattern, colour, send_list, margin):
    rows, slots, orbits, _ = margin.shape
    ext = neighbours.shape[0] + 2 * send_list.shape[2]
    return pl.pallas_call(
        functools.partial(first_kernel, ndomain, ncolour),
        out_shape=jax.ShapeDtypeStruct((rows, orbits, ncolour * orbits), jnp.bfloat16),
        in_specs=[SMEM] * 4 + [ANY],
        out_specs=VMEM,
        scratch_shapes=[
            pltpu.VMEM(margin.shape, jnp.bfloat16),
            pltpu.VMEM((rows, ncolour + 1, orbits, orbits), jnp.float32),
            pltpu.SMEM((ext,), jnp.int32),
            pltpu.SemaphoreType.DMA((rows,)),
        ],
        name="first_terms",
    )(neighbours, pattern, colour, send_list, margin)


def place(entry, shade, rows, own):
    owner = lax.div(entry, rows)
    return jnp.where(entry < own, (owner ^ shade) * rows + lax.rem(entry, rows), entry)


def border_kernel(own, send_list, *refs):
    pieces, (up, down, sems) = refs[:-3], refs[-3:]
    domain = lax.axis_index("dom")
    shade = lax.axis_index("col")
    rows = pieces[0].shape[0]
    copies = []
    for side, out in ((1, up), (0, down)):
        for i in range(send_list.shape[2]):
            entry = send_list[domain, side, i]
            relative = lax.div(entry, rows) ^ shade
            for piece in range(len(pieces)):

                @pl.when(relative == piece)
                def _():
                    pltpu.make_async_copy(
                        pieces[piece].at[lax.rem(entry, rows)], out.at[i], sems.at[side, i]
                    ).start()

            copies.append(pltpu.make_async_copy(pieces[0].at[0], out.at[i], sems.at[side, i]))
    for copy in copies:
        copy.wait()


def borders(own, send_list, pieces):
    shape = jax.ShapeDtypeStruct((send_list.shape[2],) + pieces[0].shape[1:], jnp.bfloat16)
    return pl.pallas_call(
        functools.partial(border_kernel, own),
        out_shape=(shape, shape),
        in_specs=[SMEM] + [ANY] * len(pieces),
        out_specs=(ANY, ANY),
        scratch_shapes=[pltpu.SemaphoreType.DMA((2, send_list.shape[2]))],
        name="borders",
    )(send_list, *pieces)


def image_kernel(coeffs, ncolour, neighbours, pattern, colour, margin, *refs):
    pieces, (images, blocks, ext, sems) = refs[:-4], refs[-4:]
    domain = lax.axis_index("dom")
    shade = lax.axis_index("col")
    rows, slots, orbits, _ = margin.shape
    own = neighbours.shape[0]
    copies = []
    for row in range(rows):
        copies.append(pltpu.make_async_copy(margin.at[row], blocks.at[row], sems.at[row]))
    at = 0
    for i, piece in enumerate(pieces):
        size = piece.shape[0]
        copies.append(
            pltpu.make_async_copy(piece, ext.at[pl.ds(at, size)], sems.at[rows + i])
        )
        at += size
    for copy in copies:
        copy.start()
    ext[at] = jnp.zeros(ext.shape[1:], jnp.bfloat16)
    for copy in copies:
        copy.wait()
    half = 2 * orbits
    eye = (
        lax.broadcasted_iota(jnp.int32, (orbits, orbits), 0)
        == lax.broadcasted_iota(jnp.int32, (orbits, orbits), 1)
    ).astype(jnp.float32)
    for row in range(rows):
        block = shade * rows + row
        mine = colour[domain * own + block]
        spots = []
        for k in range(slots):
            spot = place(neighbours[block, k], shade, rows, own)
            spots.append(jnp.where(pattern[block, k] == 1, spot, at))
        for h in range(ncolour // 2):
            lanes = slice(h * half, (h + 1) * half)
            total = jnp.zeros((orbits, half), jnp.float32)
            for k in range(0, slots, 2):
                ks = range(k, min(k + 2, slots))
                left = jnp.concatenate([blocks[row, j] for j in ks], axis=1)
                right = jnp.concatenate([ext[spots[j], :, lanes] for j in ks], axis=0)
                total += jnp.dot(left, right, preferred_element_type=jnp.float32)
            for c in range(2):
                cut = slice(c * orbits, (c + 1) * orbits)
                first = ext[row, :, h * half + c * orbits : h * half + (c + 1) * orbits]
                first = first.astype(jnp.float32)
                probe = jnp.where(mine == 2 * h + c, eye, 0.0)
                applied = (total[:, cut] - CENTRE * first) / HALF_WIDTH
                images[2 * h + c, row] = (
                    coeffs[0] * probe + coeffs[1] * first + coeffs[2] * (2.0 * applied - probe)
                )


def image_terms(coeffs, ncolour, neighbours, pattern, colour, margin, pieces):
    rows, slots, orbits, _ = margin.shape
    total = sum(piece.shape[0] for piece in pieces)
    return pl.pallas_call(
        functools.partial(image_kernel, coeffs, ncolour),
        out_shape=jax.ShapeDtypeStruct((ncolour, rows, orbits, orbits), jnp.float32),
        in_specs=[SMEM] * 3 + [ANY] * (1 + len(pieces)),
        out_specs=VMEM,
        scratch_shapes=[
            pltpu.VMEM(margin.shape, jnp.bfloat16),
            pltpu.VMEM((total + 1,) + pieces[0].shape[1:], jnp.bfloat16),
            pltpu.SemaphoreType.DMA((rows + len(pieces),)),
        ],
        compiler_params=pltpu.CompilerParams(vmem_limit_bytes=56 << 20),
        name="image_terms",
    )(neighbours, pattern, colour, margin, *pieces)


def per_device(ndomain, ncolour, margin, neighbours, pattern, colour, send_list):
    coeffs = cheb_coefficients()
    rows, _, orbits, _ = margin.shape
    own = neighbours.shape[0]
    pieces = {0: first_terms(ndomain, ncolour, neighbours, pattern, colour, send_list, margin)}
    step = ncolour // 2
    while step:
        pairs = [(i, i ^ step) for i in range(ncolour)]
        for held in list(pieces):
            pieces[held ^ step] = lax.ppermute(pieces[held], "col", pairs)
        step //= 2
    pieces = [pieces[i] for i in range(ncolour)]
    up, down = borders(own, send_list, pieces)
    onward = [(i, (i + 1) % ndomain) for i in range(ndomain)]
    before = lax.ppermute(up, "dom", onward)
    after = lax.ppermute(down, "dom", [(j, i) for i, j in onward])
    images = image_terms(
        coeffs, ncolour, neighbours, pattern, colour, margin, pieces + [before, after]
    )
    images = lax.all_to_all(images, "col", split_axis=0, concat_axis=0, tiled=True)
    return images.reshape(own * orbits, orbits)


def solution(mesh):
    placed = (P(("dom", "col"), None, None, None), P("dom", None), P("dom", None), P(), P())
    return jax.shard_map(
        functools.partial(per_device, mesh.shape["dom"], mesh.shape["col"]),
        mesh=mesh,
        in_specs=placed,
        out_specs=P("dom", "col"),
        check_vma=False,
    )
```

time: 80.3 us -> 55.7 us (0.69)
  Pallas kernels: 0 us -> 18.3 us
  waiting for transfers between devices: 30.3 us -> 13.2 us
  between operations: 14.9 us -> 0.05 us
  blocking collectives: 0 us -> 12.3 us
  local copies, waits for them, and re-layouts: 15.3 us -> 3.52 us
  matrix products: 8.98 us -> 0 us
  starting transfers between devices: 9.55 us -> 7.93 us
  other arithmetic: 1.07 us -> 0 us
    all_gather x1 -> x0, waiting for transfers between devices: 18.8 us -> none  [per_device(): lax.all_gather(margin, 'col', axis=0, tiled=True)]
    pallas_call x0 -> x3, Pallas kernels: none -> 18.3 us  [the longest x1 9.86 us: borders(): pl.pallas_call(functools.partial(border_kernel, own), out_shape=(shape, s...]
    all_to_all x0 -> x1, blocking collectives: none -> 12.3 us  [per_device(): lax.all_to_all(images, 'col', split_axis=0, concat_axis=0, tiled=True)]
    gather x6 -> x0, local copies, waits for them, and re-layouts: 12.2 us -> none  [the longest x1 8.36 us: per_device(): extended[neighbours]]
    ppermute x2 -> x5, waiting for transfers between devices: 1.83 us -> 13.2 us  [the longest x3 8.03 us: per_device(): pieces[held ^ step] = lax.ppermute(pieces[held], 'col', pairs)]
    dot_general x2 -> x0, matrix products: 8.98 us -> none  [the longest x1 7.9 us: per_device(): jnp.einsum('bkij,bkjl->bil', lax.all_gather(margin, 'col', axis=0, tiled=...]
    all_to_all x1 -> x0, waiting for transfers between devices: 8.94 us -> none  [per_device(): lax.all_to_all(first_all, 'col', split_axis=2, concat_axis=0, tiled=True)]
    all_to_all x1 -> x0, starting transfers between devices: 4.21 us -> none  [per_device(): lax.all_to_all(first_all, 'col', split_axis=2, concat_axis=0, tiled=True)]
  transfers between devices with their start and end apart: 4 -> 5, of which waited for: 3 -> 4; matrix products, arithmetic and copies ran while one was open for 22% -> 0% of each run, Pallas kernels for 0% -> 0%
where the time goes in v1:
time: 55.7 us; the launch traced here: 55.3 us
  Pallas kernels  18.3 us (33%)
  waiting for transfers between devices  13.2 us (24%)
  blocking collectives  12.3 us (22%)
  starting transfers between devices  7.93 us (14%)
  local copies, waits for them, and re-layouts  3.52 us (6%)
    all_to_all x1, blocking collectives, per_device(): lax.all_to_all(images, 'col', split_axis=0, concat_axis=0, tiled=True)  12.3 us
    pallas_call x1, Pallas kernels, borders(): pl.pallas_call(functools.partial(border_kernel, own), out_shape=(shape, s...  9.86 us
    ppermute x3, waiting for transfers between devices, per_device(): pieces[held ^ step] = lax.ppermute(pieces[held], 'col', pairs)  8.03 us
    pallas_call x1, Pallas kernels, image_terms(): pl.pallas_call(functools.partial(image_kernel, coeffs, ncolour), out_shap...  4.67 us
    ppermute x1, waiting for transfers between devices, per_device(): before = lax.ppermute(up, 'dom', onward)  4.05 us
    pallas_call x1, Pallas kernels, first_terms(): pl.pallas_call(functools.partial(first_kernel, ndomain, ncolour), out_sha...  3.77 us
    unnamed x12, local copies, waits for them, and re-layouts  3.52 us
    ppermute x1, starting transfers between devices, per_device(): after = lax.ppermute(down, 'dom', [(j, i) for i, j in onward])  3.11 us
  transfers between devices with their start and end apart: 5, of which 4 were waited for; matrix products, arithmetic and copies ran while one was open for 0% of the time, Pallas kernels for 0%

profile of v1, /device:TPU:0, one launch (start us, length us, event | category | flops | bytes accessed | tf_op | source)
XLA Modules:
  0.0 55.3 jit_solution(16914228169596646120)
XLA Ops:
  0.0 1.3 %copy.6.send_list = s32[8,2,1]{2,1,0:T(2,128)} copy(s32[8,2,1]{0,2,1:T(1,128)} %param.9) | data formatting | bytes 128 | tf_op args[4]
  1.4 3.8 %first_terms.1.refs_0_ = bf16[2,128,512]{2,1,0:T(8,128)(2,1)} custom-call(s32[8,27]{1,0:T(8,128)} %neighbours.3, s32[8,27]{1,0:T(8,128)} %pattern.3, s32[64]{0:T(128)} %colour.3, s32[8,2,1]{2,1,0:T(2,128)} %copy.6.send_list, bf16[2,27,128,128]{3,2,1,0:T(8,128)(2,1)} %margin.3), custom_call_target="tpu_custom_call" | custom-call | tf_op jit(solution)/shard_map/first_terms/pallas_call | solution.py:83
  5.1 3.0 %collective-permute-start.1 = (bf16[2,128,512]{2,1,0:T(8,128)(2,1)}, bf16[2,128,512]{2,1,0:T(8,128)(2,1)S(1)}, u32[]{:S(2)}, u32[]{:S(2)}) collective-permute-start(bf16[2,128,512]{2,1,0:T(8,128)(2,1)} %first_terms.1.refs_0_), channel_id=1, source_target_pairs={{0,2},{1,3},{2,0},{3,1},{4,6},{5,7},{6,4},{7,5},{8,10},{9,11},{10,... | collective-permute-start | bytes 786440 | tf_op jit(solution)/shard_map/ppermute | solution.py:217
  8.1 0.0 collective-permute-start
  8.1 6.5 %collective-permute-done.1.refs_2_ = bf16[2,128,512]{2,1,0:T(8,128)(2,1)S(1)} collective-permute-done((bf16[2,128,512]{2,1,0:T(8,128)(2,1)}, bf16[2,128,512]{2,1,0:T(8,128)(2,1)S(1)}, u32[]{:S(2)}, u32[]{:S(2)}) %collective-permute-start.1) | collective-permute-done | bytes 262176 | tf_op jit(solution)/shard_map/ppermute | solution.py:217
  14.7 0.0 copy-start
  14.7 0.0 collective-permute-start.2
  14.7 0.0 collective-permute-done.refs_1_
  14.7 0.0 copy-start.1
  14.7 1.5 %collective-permute-done.2.refs_3_ = bf16[2,128,512]{2,1,0:T(8,128)(2,1)S(1)} collective-permute-done((bf16[2,128,512]{2,1,0:T(8,128)(2,1)S(1)}, bf16[2,128,512]{2,1,0:T(8,128)(2,1)S(1)}, u32[]{:S(2)}, u32[]{:S(2)}) %collective-permute-start.2) | collective-permute-done | bytes 262176 | tf_op jit(solution)/shard_map/ppermute | solution.py:217
  16.2 0.0 copy-done
  16.2 0.0 copy-done.1
  16.2 0.0 copy-start.2
  16.2 0.7 %copy-done.2 = bf16[2,128,512]{2,1,0:T(8,128)(2,1)} copy-done((bf16[2,128,512]{2,1,0:T(8,128)(2,1)}, bf16[2,128,512]{2,1,0:T(8,128)(2,1)S(1)}, u32[]{:S(2)}) %copy-start.2) | copy-done | bytes 262168
  16.9 9.9 %borders.1 = (bf16[1,128,512]{2,1,0:T(8,128)(2,1)}, bf16[1,128,512]{2,1,0:T(8,128)(2,1)}) custom-call(s32[8,2,1]{2,1,0:T(2,128)} %copy.6.send_list, bf16[2,128,512]{2,1,0:T(8,128)(2,1)} %first_terms.1.refs_0_, bf16[2,128,512]{2,1,0:T(8,128)(2,1)} %copy-done.1, bf16[2,128,512]{2,1,0:T(8,128)(2,1)} %copy-done, bf16[2,128,512]{2,1,0:T(8,128)(2,1)} %copy-done.2), custom_call_target="tpu_custom_call" | custom-call | tf_op jit(solution)/shard_map/borders/pallas_call | solution.py:128
  26.8 1.8 %collective-permute-start.3 = (bf16[1,128,512]{2,1,0:T(8,128)(2,1)}, bf16[1,128,512]{2,1,0:T(8,128)(2,1)S(1)}, u32[]{:S(2)}, u32[]{:S(2)}) collective-permute-start(bf16[1,128,512]{2,1,0:T(8,128)(2,1)} %get-tuple-element.7), channel_id=1, source_target_pairs={{0,4},{4,8},{8,12},{12,16},{16,20},{20,24},{24,28},{28,0},{1,5},{5... | collective-permute-start | bytes 393224 | tf_op jit(solution)/shard_map/ppermute | solution.py:222
  28.6 3.1 %collective-permute-start.4 = (bf16[1,128,512]{2,1,0:T(8,128)(2,1)}, bf16[1,128,512]{2,1,0:T(8,128)(2,1)S(1)}, u32[]{:S(2)}, u32[]{:S(2)}) collective-permute-start(bf16[1,128,512]{2,1,0:T(8,128)(2,1)} %get-tuple-element.8), channel_id=1, source_target_pairs={{4,0},{8,4},{12,8},{16,12},{20,16},{24,20},{28,24},{0,28},{5,1},{9... | collective-permute-start | bytes 393224 | tf_op jit(solution)/shard_map/ppermute | solution.py:223
  31.7 4.1 %collective-permute-done.3.refs_4_ = bf16[1,128,512]{2,1,0:T(8,128)(2,1)S(1)} collective-permute-done((bf16[1,128,512]{2,1,0:T(8,128)(2,1)}, bf16[1,128,512]{2,1,0:T(8,128)(2,1)S(1)}, u32[]{:S(2)}, u32[]{:S(2)}) %collective-permute-start.3) | collective-permute-done | bytes 131104 | tf_op jit(solution)/shard_map/ppermute | solution.py:222
  35.7 1.1 %collective-permute-done.4.refs_5_ = bf16[1,128,512]{2,1,0:T(8,128)(2,1)S(1)} collective-permute-done((bf16[1,128,512]{2,1,0:T(8,128)(2,1)}, bf16[1,128,512]{2,1,0:T(8,128)(2,1)S(1)}, u32[]{:S(2)}, u32[]{:S(2)}) %collective-permute-start.4) | collective-permute-done | bytes 131104 | tf_op jit(solution)/shard_map/ppermute | solution.py:223
  36.9 0.0 copy-done.3
  36.9 0.7 %copy-done.4 = bf16[1,128,512]{2,1,0:T(8,128)(2,1)} copy-done((bf16[1,128,512]{2,1,0:T(8,128)(2,1)}, bf16[1,128,512]{2,1,0:T(8,128)(2,1)S(1)}, u32[]{:S(2)}) %copy-start.4) | copy-done | bytes 131096
  37.5 4.7 %image_terms.1 = f32[4,2,128,128]{3,2,1,0:T(8,128)} custom-call(s32[8,27]{1,0:T(8,128)} %neighbours.3, s32[8,27]{1,0:T(8,128)} %pattern.3, s32[64]{0:T(128)} %colour.3, bf16[2,27,128,128]{3,2,1,0:T(8,128)(2,1)} %margin.3, bf16[2,128,512]{2,1,0:T(8,128)(2,1)} %first_terms.1.refs_0_, bf16[2,128,512]{2,1,0:T(8,128)(2,1)} %copy-done.1, ...), custom_call_target="tpu_custom_call" | custom-call | tf_op jit(solution)/shard_map/image_terms/pallas_call | solution.py:193
  42.2 12.3 %all_to_all.5 = f32[4,2,128,128]{3,2,1,0:T(8,128)S(1)} all-to-all(f32[4,2,128,128]{3,2,1,0:T(8,128)} %image_terms.1), channel_id=1, replica_groups=mesh['dom'=8,'col'=4] {'col'}, dimensions={0} | all-to-all | bytes 1048576 | tf_op jit(solution)/shard_map/all_to_all | solution.py:227
  54.5 0.8 %copy.9 = f32[1024,128]{1,0:T(8,128)} copy(f32[1024,128]{1,0:T(8,128)S(1)} %bitcast.1) | data formatting | bytes 1048576
  (2 shorter events, 0.0 us)
Async XLA Ops:
  5.1 9.5 %collective-permute-start.1 = (bf16[2,128,512]{2,1,0:T(8,128)(2,1)}, bf16[2,128,512]{2,1,0:T(8,128)(2,1)S(1)}, u32[]{:S(2)}, u32[]{:S(2)}) collective-permute-start(bf16[2,128,512]{2,1,0:T(8,128)(2,1)} %first_terms.1.refs_0_), channel_id=1, source_target_pairs={{0,2},{1,3},{2,0},{3,1},{4,6},{5,7},{6,4},{7,5},{8,10},{9,11},{10,... | collective-permute-start | bytes 786440 | tf_op jit(solution)/shard_map/ppermute | solution.py:217
  8.1 6.5 %collective-permute-start = (bf16[2,128,512]{2,1,0:T(8,128)(2,1)}, bf16[2,128,512]{2,1,0:T(8,128)(2,1)S(1)}, u32[]{:S(2)}, u32[]{:S(2)}) collective-permute-start(bf16[2,128,512]{2,1,0:T(8,128)(2,1)} %first_terms.1.refs_0_), channel_id=1, source_target_pairs={{0,1},{1,0},{2,3},{3,2},{4,5},{5,4},{6,7},{7,6},{8,9},{9,8},{10,11... | collective-permute-start | bytes 786440 | tf_op jit(solution)/shard_map/ppermute | solution.py:217
  14.7 1.5 %copy-start = (bf16[2,128,512]{2,1,0:T(8,128)(2,1)}, bf16[2,128,512]{2,1,0:T(8,128)(2,1)S(1)}, u32[]{:S(2)}) copy-start(bf16[2,128,512]{2,1,0:T(8,128)(2,1)S(1)} %collective-permute-done.1.refs_2_) | copy-start | bytes 786436
  14.7 1.5 %collective-permute-start.2 = (bf16[2,128,512]{2,1,0:T(8,128)(2,1)S(1)}, bf16[2,128,512]{2,1,0:T(8,128)(2,1)S(1)}, u32[]{:S(2)}, u32[]{:S(2)}) collective-permute-start(bf16[2,128,512]{2,1,0:T(8,128)(2,1)S(1)} %collective-permute-done.1.refs_2_), channel_id=1, source_target_pairs={{0,1},{1,0},{2,3},{3,2},{4,5},{5,4},{6,7},{7,6},{8,9},{9,8},{10,11... | collective-permute-start | bytes 786440 | tf_op jit(solution)/shard_map/ppermute | solution.py:217
  14.7 1.5 %copy-start.1 = (bf16[2,128,512]{2,1,0:T(8,128)(2,1)}, bf16[2,128,512]{2,1,0:T(8,128)(2,1)S(1)}, u32[]{:S(2)}) copy-start(bf16[2,128,512]{2,1,0:T(8,128)(2,1)S(1)} %collective-permute-done.refs_1_) | copy-start | bytes 786436
  16.2 0.7 %copy-start.2 = (bf16[2,128,512]{2,1,0:T(8,128)(2,1)}, bf16[2,128,512]{2,1,0:T(8,128)(2,1)S(1)}, u32[]{:S(2)}) copy-start(bf16[2,128,512]{2,1,0:T(8,128)(2,1)S(1)} %collective-permute-done.2.refs_3_) | copy-start | bytes 786436
  26.8 9.0 %collective-permute-start.3 = (bf16[1,128,512]{2,1,0:T(8,128)(2,1)}, bf16[1,128,512]{2,1,0:T(8,128)(2,1)S(1)}, u32[]{:S(2)}, u32[]{:S(2)}) collective-permute-start(bf16[1,128,512]{2,1,0:T(8,128)(2,1)} %get-tuple-element.7), channel_id=1, source_target_pairs={{0,4},{4,8},{8,12},{12,16},{16,20},{20,24},{24,28},{28,0},{1,5},{5... | collective-permute-start | bytes 393224 | tf_op jit(solution)/shard_map/ppermute | solution.py:222
  28.6 8.3 %collective-permute-start.4 = (bf16[1,128,512]{2,1,0:T(8,128)(2,1)}, bf16[1,128,512]{2,1,0:T(8,128)(2,1)S(1)}, u32[]{:S(2)}, u32[]{:S(2)}) collective-permute-start(bf16[1,128,512]{2,1,0:T(8,128)(2,1)} %get-tuple-element.8), channel_id=1, source_target_pairs={{4,0},{8,4},{12,8},{16,12},{20,16},{24,20},{28,24},{0,28},{5,1},{9... | collective-permute-start | bytes 393224 | tf_op jit(solution)/shard_map/ppermute | solution.py:223
  35.7 1.1 %copy-start.3 = (bf16[1,128,512]{2,1,0:T(8,128)(2,1)}, bf16[1,128,512]{2,1,0:T(8,128)(2,1)S(1)}, u32[]{:S(2)}) copy-start(bf16[1,128,512]{2,1,0:T(8,128)(2,1)S(1)} %collective-permute-done.3.refs_4_) | copy-start | bytes 393220
  36.9 0.7 %copy-start.4 = (bf16[1,128,512]{2,1,0:T(8,128)(2,1)}, bf16[1,128,512]{2,1,0:T(8,128)(2,1)S(1)}, u32[]{:S(2)}) copy-start(bf16[1,128,512]{2,1,0:T(8,128)(2,1)S(1)} %collective-permute-done.4.refs_5_) | copy-start | bytes 393220

commit v2 on v0

v2 whole, which is shorter than its diff:
```python
import functools
import math

import jax
import jax.numpy as jnp
from jax import lax
from jax.experimental import pallas as pl
from jax.experimental.pallas import tpu as pltpu
from jax.sharding import PartitionSpec as P

CENTRE = 1.0
HALF_WIDTH = 0.9
HBM = pl.BlockSpec(memory_space=pltpu.HBM)
SMEM = pl.BlockSpec(memory_space=pltpu.SMEM)
VMEM = pl.BlockSpec(memory_space=pltpu.VMEM)
WIRE = jnp.float16
WIRE_SCALE = 0.5


def cheb_coefficients():
    samples = []
    for index_k in range(3):
        angle_value = math.pi * (index_k + 0.5) / 3.0
        samples.append((angle_value, (CENTRE + HALF_WIDTH * math.cos(angle_value)) ** (-0.5)))
    coeffs = []
    for order in range(3):
        coeffs.append(
            2.0
            / 3.0
            * sum((value * math.cos(order * angle_value) for angle_value, value in samples))
        )
    coeffs[0] = 0.5 * coeffs[0]
    return coeffs


def unit(orbits):
    down = lax.broadcasted_iota(jnp.int32, (orbits, orbits), 0)
    along = lax.broadcasted_iota(jnp.int32, (orbits, orbits), 1)
    return (down == along).astype(jnp.float32)


def limit(shapes, extra=2 << 20):
    total = sum(math.prod(s.shape) * jnp.dtype(s.dtype).itemsize for s in shapes)
    return int(total + extra)


def like(shape, dtype):
    return jax.ShapeDtypeStruct(shape, dtype)


def first_kernel(ndomain, ncolour, chunk, *refs):
    tables, margin = refs[:4], refs[4]
    near, far, border, blocks, sums = refs[5:10]
    neighbours, pattern, colour, sends, table, sems, small = refs[10:]
    domain = lax.axis_index("dom")
    shade = lax.axis_index("col")
    rows, slots, orbits, _ = margin.shape
    own = neighbours.shape[0]
    width = sends.shape[1]
    loads = [
        pltpu.make_async_copy(source, target, small.at[i])
        for i, (source, target) in enumerate(zip(tables, (neighbours, pattern, colour, sends)))
    ]
    for load in loads:
        load.start()
    copies = []
    for row in range(rows):
        for i, k in enumerate(range(0, slots, chunk)):
            part = pl.ds(k, min(chunk, slots - k))
            copies.append(
                pltpu.make_async_copy(margin.at[row, part], blocks.at[row, part], sems.at[row, i])
            )
    for copy in copies:
        copy.start()
    sums[...] = jnp.zeros_like(sums)
    border[...] = jnp.zeros_like(border)
    base = shade - lax.rem(shade, 2)
    lower = lax.rem(domain + ndomain - 1, ndomain)
    upper = lax.rem(domain + 1, ndomain)
    for load in loads:
        load.wait()
    for i in range(own):
        table[i] = colour[domain * own + i] ^ base
    for i in range(width):
        table[own + i] = colour[lower * own + sends[1, i, lower]] ^ base
        table[own + width + i] = colour[upper * own + sends[0, i, upper]] ^ base
    eye = unit(orbits)
    half = ncolour // 4
    for row in range(rows):
        block = shade * rows + row
        sums[row, table[block]] = (-CENTRE) * eye
        for k0 in range(0, slots, chunk):
            copies.pop(0).wait()

            @pl.loop(k0, min(k0 + chunk, slots))
            def _(k):
                entry = neighbours[block, k]
                live = pattern[block, k] == 1
                value = blocks[row, k].astype(jnp.float32)
                sums[row, jnp.where(live, table[entry], ncolour)] += value

                @pl.when(jnp.logical_and(live, entry >= own))
                def _():
                    border[row, entry - own] += value

        for c in range(ncolour):
            r = c // 2
            lanes = slice((c % 2) * orbits, (c % 2 + 1) * orbits)
            (near if r < half else far)[r % half, row, :, lanes] = (
                sums[row, c] * (1.0 / HALF_WIDTH)
            ).astype(jnp.bfloat16)


def first_terms(ndomain, ncolour, neighbours, pattern, colour, sends, margin):
    rows, slots, orbits, _ = margin.shape
    width = sends.shape[1]
    ext = neighbours.shape[0] + 2 * width
    half = like((ncolour // 4, rows, orbits, 2 * orbits), jnp.bfloat16)
    border = like((rows, 2 * width, orbits, orbits), jnp.float32)
    sums = like((rows, ncolour + 1, orbits, orbits), jnp.float32)
    chunk = 9
    tables = [neighbours, pattern, colour, sends]
    return pl.pallas_call(
        functools.partial(first_kernel, ndomain, ncolour, chunk),
        out_shape=(half, half, border),
        in_specs=[HBM] * 5,
        out_specs=(VMEM, VMEM, VMEM),
        scratch_shapes=[
            pltpu.VMEM(margin.shape, jnp.bfloat16),
            pltpu.VMEM(sums.shape, jnp.float32),
            *[pltpu.SMEM(t.shape, jnp.int32) for t in tables],
            pltpu.SMEM((ext,), jnp.int32),
            pltpu.SemaphoreType.DMA((rows, pl.cdiv(slots, chunk))),
            pltpu.SemaphoreType.DMA((4,)),
        ],
        compiler_params=pltpu.CompilerParams(
            vmem_limit_bytes=limit([half, half, border, margin, sums])
        ),
        name="first_terms",
    )(*[pltpu.with_memory_space_constraint(t, pltpu.HBM) for t in tables + [margin]])


def border_kernel(sends, near0, far0, near1, far1, up, down):
    domain = lax.axis_index("dom")
    shade = lax.axis_index("col")
    parity = lax.rem(shade, 2)
    half, rows, orbits, _ = near0.shape
    lanes = pl.ds(pl.multiple_of(parity * orbits, orbits), orbits)
    for side, out in ((1, up), (0, down)):
        for i in range(sends.shape[1]):
            entry = sends[side, i, domain]
            relative = lax.div(entry, rows) ^ shade
            row = lax.rem(entry, rows)
            for s in range(2 * half):
                mine, other = (near0, near1) if s < half else (far0, far1)

                @pl.when(relative == 0)
                def _():
                    out[s, i] = mine[s % half, row, :, lanes]

                @pl.when(relative == 1)
                def _():
                    out[s, i] = other[s % half, row, :, lanes]

                @pl.when(relative > 1)
                def _():
                    out[s, i] = jnp.zeros(out.shape[2:], out.dtype)


def borders(sends, near0, far0, near1, far1):
    half, _, orbits, _ = near0.shape
    out = like((2 * half, sends.shape[1], orbits, orbits), jnp.bfloat16)
    return pl.pallas_call(
        border_kernel,
        out_shape=(out, out),
        in_specs=[SMEM] + [VMEM] * 4,
        out_specs=(VMEM, VMEM),
        compiler_params=pltpu.CompilerParams(
            vmem_limit_bytes=limit([near0, far0, near1, far1, out, out])
        ),
        name="borders",
    )(sends, near0, far0, near1, far1)


def image_kernel(coeffs, upper_half, neighbours, pattern, colour, margin, *refs):
    pieces, (images, ext) = refs[:-2], refs[-2:]
    domain = lax.axis_index("dom")
    shade = lax.axis_index("col")
    parity = lax.rem(shade, 2)
    base = shade - parity
    rows, slots, orbits, _ = margin.shape
    own = neighbours.shape[0]
    half = pieces[0].shape[0]
    for r in range(half):
        for relative, piece in enumerate(pieces):
            turn = ((relative // 2) % half) ^ r
            for row in range(rows):
                ext[r, relative * rows + row] = piece[turn, row]
        ext[r, own] = jnp.zeros(ext.shape[2:], ext.dtype)
    eye = unit(orbits)
    for row in range(rows):
        block = shade * rows + row
        mine = colour[domain * own + block] ^ base
        spots = []
        for k in range(slots):
            entry = neighbours[block, k]
            spot = (lax.div(entry, rows) ^ shade) * rows + lax.rem(entry, rows)
            live = jnp.logical_and(pattern[block, k] == 1, entry < own)
            spots.append(jnp.where(live, spot, own))
        for r in range(half):
            total = jnp.zeros((orbits, 2 * orbits), jnp.float32)
            for k in range(0, slots, 2):
                ks = range(k, min(k + 2, slots))
                left = jnp.concatenate([margin[row, j] for j in ks], axis=1)
                right = jnp.concatenate([ext[r, spots[j]] for j in ks], axis=0)
                total += jnp.dot(left, right, preferred_element_type=jnp.float32)
            for q in range(2):
                cut = slice(q * orbits, (q + 1) * orbits)
                first = ext[r, row, :, cut].astype(jnp.float32)
                relative = 2 * (r + (half if upper_half else 0)) + q
                probe = jnp.where(mine == relative, eye, 0.0)
                applied = (total[:, cut] - CENTRE * first) * (1.0 / HALF_WIDTH)
                images[2 * r + (parity ^ q), row] = (
                    coeffs[0] * probe + coeffs[1] * first + coeffs[2] * (2.0 * applied - probe)
                )


def image_terms(coeffs, upper_half, neighbours, pattern, colour, margin, pieces):
    rows, slots, orbits, _ = margin.shape
    half = pieces[0].shape[0]
    images = like((2 * half, rows, orbits, orbits), jnp.float32)
    ext = like((half, neighbours.shape[0] + 1, orbits, 2 * orbits), jnp.bfloat16)
    return pl.pallas_call(
        functools.partial(image_kernel, coeffs, upper_half),
        out_shape=images,
        in_specs=[SMEM] * 3 + [VMEM] * (1 + len(pieces)),
        out_specs=VMEM,
        scratch_shapes=[pltpu.VMEM(ext.shape, ext.dtype)],
        compiler_params=pltpu.CompilerParams(
            vmem_limit_bytes=limit([margin, images, ext, *pieces], 4 << 20)
        ),
        name="image_terms",
    )(neighbours, pattern, colour, margin, *pieces)


def final_kernel(scale, count, mine, *refs):
    images, refs = refs[: count - 1], refs[count - 1 :]
    blocks, refs = refs[:count], refs[count:]
    firsts, out = refs[:-1], refs[-1]
    shade = lax.axis_index("col")
    rows, wide, orbits, _ = blocks[0].shape
    width = wide // 2
    right = []
    for e in range(wide):
        side, i = divmod(e, width)
        value = firsts[side][0, i].astype(jnp.float32)
        for other in firsts[2:]:
            value += other[side, i].astype(jnp.float32)
        right.append(value.astype(jnp.bfloat16))
    right = jnp.concatenate(right + right, axis=0)
    for relative in range(count):
        for row in range(rows):
            left = jnp.concatenate([blocks[relative][row, e] for e in range(wide)], axis=1)
            high = left.astype(jnp.bfloat16)
            low = (left - high.astype(jnp.float32)).astype(jnp.bfloat16)
            extra = jnp.dot(
                jnp.concatenate([high, low], axis=1), right, preferred_element_type=jnp.float32
            )
            if relative == 0:
                value = mine[0, row]
            else:
                value = images[relative - 1][0, row] * (1.0 / WIRE_SCALE)
            at = (shade ^ relative) * rows + row
            out[pl.ds(pl.multiple_of(at * orbits, orbits), orbits), :] = value + scale * extra


def final_images(scale, mine, images, blocks, firsts):
    count = len(blocks)
    rows, _, orbits, _ = blocks[0].shape
    out = like((count * rows * orbits, orbits), jnp.float32)
    return pl.pallas_call(
        functools.partial(final_kernel, scale, count),
        out_shape=out,
        in_specs=[VMEM] * (1 + len(images) + len(blocks) + len(firsts)),
        out_specs=VMEM,
        compiler_params=pltpu.CompilerParams(
            vmem_limit_bytes=limit([mine, *images, *blocks, *firsts, out], 4 << 20)
        ),
        name="final_images",
    )(mine, *images, *blocks, *firsts)


def per_device(ndomain, ncolour, margin, neighbours, pattern, colour, send_list):
    coeffs = cheb_coefficients()
    pairs = ncolour // 2
    half = pairs // 2
    sends = jnp.transpose(send_list, (1, 2, 0))

    def across(value, step):
        return lax.ppermute(value, "col", [(i, i ^ step) for i in range(ncolour)])

    near, far, border = first_terms(ndomain, ncolour, neighbours, pattern, colour, sends, margin)
    nears, fars = {0: near}, {0: far}
    for s in range(1, pairs):
        nears[2 * s] = across(near, 2 * s)
        fars[2 * s] = across(far, 2 * s)
    nears[1] = across(near, 1)
    fars[1] = across(far, 1)
    up, down = borders(sends, near, far, nears[1], fars[1])
    onward = [(i, (i + 1) % ndomain) for i in range(ndomain)]
    before = lax.ppermute(up, "dom", onward)
    after = lax.ppermute(down, "dom", [(j, i) for i, j in onward])
    for s in range(1, pairs):
        nears[2 * s + 1] = across(nears[2 * s], 1)
        fars[2 * s + 1] = across(fars[2 * s], 1)
    wire = border.astype(WIRE)
    wires = {0: wire, 1: across(wire, 1)}
    for s in range(1, pairs):
        wires[2 * s] = across(wire, 2 * s)
        wires[2 * s + 1] = across(wires[2 * s], 1)

    def pieces(upper):
        picked = []
        for relative in range(ncolour):
            top = relative // 2 >= half
            picked.append((nears if top == upper else fars)[relative])
        return picked

    outer = image_terms(coeffs, True, neighbours, pattern, colour, margin, pieces(True))
    images = {}
    sent = (outer * WIRE_SCALE).astype(WIRE)
    for m in range(pairs, ncolour):
        images[m] = across(sent[m - pairs : m - pairs + 1], m)
    firsts = [before, after]
    for s in range(1, pairs):
        firsts.append(across(jnp.stack([before[s], after[s]]), 2 * s))
    inner = image_terms(coeffs, False, neighbours, pattern, colour, margin, pieces(False))
    sent = (inner * WIRE_SCALE).astype(WIRE)
    for m in range(1, pairs):
        images[m] = across(sent[m : m + 1], m)
    return final_images(
        2.0 * coeffs[2] / HALF_WIDTH,
        inner,
        [images[m].astype(jnp.float32) for m in range(1, ncolour)],
        [border] + [wires[m].astype(jnp.float32) for m in range(1, ncolour)],
        firsts,
    )


def solution(mesh):
    placed = (P(("dom", "col"), None, None, None), P("dom", None), P("dom", None), P(), P())
    return jax.shard_map(
        functools.partial(per_device, mesh.shape["dom"], mesh.shape["col"]),
        mesh=mesh,
        in_specs=placed,
        out_specs=P("dom", "col"),
        check_vma=False,
    )
```

time: 80.3 us -> 27 us (0.34)
  waiting for transfers between devices: 30.3 us -> 4.57 us
  local copies, waits for them, and re-layouts: 15.3 us -> 0.05 us
  between operations: 14.9 us -> 0.22 us
  matrix products: 8.98 us -> 0 us
  Pallas kernels: 0 us -> 7.19 us
  starting transfers between devices: 9.55 us -> 14.7 us
  other arithmetic: 1.07 us -> 0.17 us
    all_gather x1 -> x0, waiting for transfers between devices: 18.8 us -> none  [per_device(): lax.all_gather(margin, 'col', axis=0, tiled=True)]
    gather x6 -> x0, local copies, waits for them, and re-layouts: 12.2 us -> none  [the longest x1 8.36 us: per_device(): extended[neighbours]]
    ppermute x2 -> x15, starting transfers between devices: 5.31 us -> 14.7 us  [the longest x13 9.93 us: across(): return lax.ppermute(value, 'col', [(i, i ^ step) for i in range(ncolour)])]
    dot_general x2 -> x0, matrix products: 8.98 us -> none  [the longest x1 7.9 us: per_device(): jnp.einsum('bkij,bkjl->bil', lax.all_gather(margin, 'col', axis=0, tiled=...]
    all_to_all x1 -> x0, waiting for transfers between devices: 8.94 us -> none  [per_device(): lax.all_to_all(first_all, 'col', split_axis=2, concat_axis=0, tiled=True)]
    pallas_call x0 -> x5, Pallas kernels: none -> 7.19 us  [the longest x2 2.9 us: image_terms(): pl.pallas_call(functools.partial(image_kernel, coeffs, upper_half), out_s...]
    all_to_all x1 -> x0, starting transfers between devices: 4.21 us -> none  [per_device(): lax.all_to_all(first_all, 'col', split_axis=2, concat_axis=0, tiled=True)]
    ppermute x2 -> x15, waiting for transfers between devices: 1.83 us -> 4.57 us  [the longest x13 4.14 us: across(): return lax.ppermute(value, 'col', [(i, i ^ step) for i in range(ncolour)])]
  transfers between devices with their start and end apart: 4 -> 15, of which waited for: 3 -> 4; matrix products, arithmetic and copies ran while one was open for 22% -> 1% of each run, Pallas kernels for 0% -> 13%
where the time goes in v2:
time: 27 us; the launch traced here: 26.9 us
  starting transfers between devices  14.7 us (54%)
  Pallas kernels  7.19 us (27%)
  waiting for transfers between devices  4.57 us (17%)
    ppermute x13, starting transfers between devices, across(): return lax.ppermute(value, 'col', [(i, i ^ step) for i in range(ncolour)])  9.93 us
    ppermute x13, waiting for transfers between devices, across(): return lax.ppermute(value, 'col', [(i, i ^ step) for i in range(ncolour)])  4.14 us
    ppermute x1, starting transfers between devices, per_device(): after = lax.ppermute(down, 'dom', [(j, i) for i, j in onward])  3.2 us
    pallas_call x2, Pallas kernels, image_terms(): pl.pallas_call(functools.partial(image_kernel, coeffs, upper_half), out_s...  2.9 us
    pallas_call x1, Pallas kernels, first_terms(): pl.pallas_call(functools.partial(first_kernel, ndomain, ncolour, chunk),...  2.41 us
    ppermute x1, starting transfers between devices, per_device(): before = lax.ppermute(up, 'dom', onward)  1.57 us
    pallas_call x1, Pallas kernels, final_images(): pl.pallas_call(functools.partial(final_kernel, scale, count), out_shape=o...  1.24 us
    pallas_call x1, Pallas kernels, borders(): pl.pallas_call(border_kernel, out_shape=(out, out), in_specs=[SMEM] + [VM...  0.64 us
  transfers between devices with their start and end apart: 15, of which 4 were waited for; matrix products, arithmetic and copies ran while one was open for 1% of the time, Pallas kernels for 13%

profile of v2, /device:TPU:0, one launch (start us, length us, event | category | flops | bytes accessed | tf_op | source)
XLA Modules:
  0.0 26.9 jit_solution(17332563687277333464)
XLA Ops:
  0.0 2.4 %first_terms.1 = (bf16[1,2,128,256]{3,2,1,0:T(8,128)(2,1)S(1)}, bf16[1,2,128,256]{3,2,1,0:T(8,128)(2,1)S(1)}, f32[2,2,128,128]{3,2,1,0:T(8,128)S(1)}) custom-call(s32[8,27]{1,0:T(8,128)} %neighbours.3, s32[8,27]{1,0:T(8,128)} %pattern.3, s32[64]{0:T(128)} %colour.3, s32[2,1,8]{2,1,0:T(1,128)} %bitcast.1, bf16[2,27,128,128]{3,2,1,0:T(8,128)(2,1)} %margin.3), custom_call_target="tpu_custom_call" | custom-call | tf_op jit(solution)/shard_map/first_terms/pallas_call | solution.py:123
  2.4 0.5 %collective-permute-start = (bf16[1,2,128,256]{3,2,1,0:T(8,128)(2,1)S(1)}, bf16[1,2,128,256]{3,2,1,0:T(8,128)(2,1)S(1)}, u32[]{:S(2)}, u32[]{:S(2)}) collective-permute-start(bf16[1,2,128,256]{3,2,1,0:T(8,128)(2,1)S(1)} %get-tuple-element.10.refs_0_.near0), channel_id=1, source_target_pairs={{0,1},{1,0},{2,3},{3,2},{4,5},{5,4},{6,7},{7,6},{8,9},{9,8},{10,11... | collective-permute-start | bytes 393224 | tf_op jit(solution)/shard_map/ppermute | solution.py:300
  3.0 0.1 collective-permute-start.4
  3.0 2.9 %collective-permute-start.5 = (bf16[1,2,128,256]{3,2,1,0:T(8,128)(2,1)S(1)}, bf16[1,2,128,256]{3,2,1,0:T(8,128)(2,1)S(1)}, u32[]{:S(2)}, u32[]{:S(2)}) collective-permute-start(bf16[1,2,128,256]{3,2,1,0:T(8,128)(2,1)S(1)} %get-tuple-element.10.refs_0_.near0), channel_id=1, source_target_pairs={{0,2},{1,3},{2,0},{3,1},{4,6},{5,7},{6,4},{7,5},{8,10},{9,11},{10,... | collective-permute-start | bytes 393224 | tf_op jit(solution)/shard_map/ppermute | solution.py:300
  6.0 0.1 collective-permute-start.10
  6.1 2.0 %collective-permute-start.1 = (bf16[1,2,128,256]{3,2,1,0:T(8,128)(2,1)S(1)}, bf16[1,2,128,256]{3,2,1,0:T(8,128)(2,1)S(1)}, u32[]{:S(2)}, u32[]{:S(2)}) collective-permute-start(bf16[1,2,128,256]{3,2,1,0:T(8,128)(2,1)S(1)} %get-tuple-element.11.refs_0_.far0), channel_id=1, source_target_pairs={{0,2},{1,3},{2,0},{3,1},{4,6},{5,7},{6,4},{7,5},{8,10},{9,11},{10,... | collective-permute-start | bytes 393224 | tf_op jit(solution)/shard_map/ppermute | solution.py:300
  8.1 0.0 collective-permute-done.refs_1_.near1
  8.1 0.0 collective-permute-done.4.refs_1_.far1
  8.1 0.6 %borders.1 = (bf16[2,1,128,128]{3,2,1,0:T(8,128)(2,1)S(1)}, bf16[2,1,128,128]{3,2,1,0:T(8,128)(2,1)S(1)}) custom-call(s32[2,1,8]{2,1,0:T(1,128)S(1)} %bitcast.2, bf16[1,2,128,256]{3,2,1,0:T(8,128)(2,1)S(1)} %get-tuple-element.10.refs_0_.near0, bf16[1,2,128,256]{3,2,1,0:T(8,128)(2,1)S(1)} %get-tuple-element.11.refs_0_.far0, ...), custom_call_target="tpu_custom_call" | custom-call | tf_op jit(solution)/shard_map/borders/pallas_call | solution.py:173
  8.7 1.6 %collective-permute-start.12 = (bf16[2,1,128,128]{3,2,1,0:T(8,128)(2,1)S(1)}, bf16[2,1,128,128]{3,2,1,0:T(8,128)(2,1)S(1)}, u32[]{:S(2)}, u32[]{:S(2)}) collective-permute-start(bf16[2,1,128,128]{3,2,1,0:T(8,128)(2,1)S(1)} %get-tuple-element.13), channel_id=1, source_target_pairs={{0,4},{4,8},{8,12},{12,16},{16,20},{20,24},{24,28},{28,0},{1,5},{5... | collective-permute-start | bytes 196616 | tf_op jit(solution)/shard_map/ppermute | solution.py:311
  10.3 3.2 %collective-permute-start.13 = (bf16[2,1,128,128]{3,2,1,0:T(8,128)(2,1)S(1)}, bf16[2,1,128,128]{3,2,1,0:T(8,128)(2,1)S(1)}, u32[]{:S(2)}, u32[]{:S(2)}) collective-permute-start(bf16[2,1,128,128]{3,2,1,0:T(8,128)(2,1)S(1)} %get-tuple-element.14), channel_id=1, source_target_pairs={{4,0},{8,4},{12,8},{16,12},{20,16},{24,20},{28,24},{0,28},{5,1},{9... | collective-permute-start | bytes 196616 | tf_op jit(solution)/shard_map/ppermute | solution.py:312
  13.5 0.5 %collective-permute-start.9 = (f16[2,2,128,128]{3,2,1,0:T(8,128)(2,1)S(1)}, f16[2,2,128,128]{3,2,1,0:T(8,128)(2,1)S(1)}, u32[]{:S(2)}, u32[]{:S(2)}) collective-permute-start(f16[2,2,128,128]{3,2,1,0:T(8,128)(2,1)S(1)} %convert_element_type.32), channel_id=1, source_target_pairs={{0,1},{1,0},{2,3},{3,2},{4,5},{5,4},{6,7},{7,6},{8,9},{9,8},{10,11... | collective-permute-start | bytes 393224 | tf_op jit(solution)/shard_map/ppermute | solution.py:300
  14.0 1.3 %collective-permute-done.1.refs_2_ = bf16[1,2,128,256]{3,2,1,0:T(8,128)(2,1)S(1)} collective-permute-done((bf16[1,2,128,256]{3,2,1,0:T(8,128)(2,1)S(1)}, bf16[1,2,128,256]{3,2,1,0:T(8,128)(2,1)S(1)}, u32[]{:S(2)}, u32[]{:S(2)}) %collective-permute-start.1) | collective-permute-done | bytes 131104 | tf_op jit(solution)/shard_map/ppermute | solution.py:300
  15.3 0.4 %collective-permute-done.12.refs_7_ = bf16[2,1,128,128]{3,2,1,0:T(8,128)(2,1)S(1)} collective-permute-done((bf16[2,1,128,128]{3,2,1,0:T(8,128)(2,1)S(1)}, bf16[2,1,128,128]{3,2,1,0:T(8,128)(2,1)S(1)}, u32[]{:S(2)}, u32[]{:S(2)}) %collective-permute-start.12) | collective-permute-done | bytes 65568 | tf_op jit(solution)/shard_map/ppermute | solution.py:311
  15.8 0.1 collective-permute-start.2
  15.9 1.4 %image_terms.3 = f32[2,2,128,128]{3,2,1,0:T(8,128)S(1)} custom-call(s32[8,27]{1,0:T(8,128)S(1)} %copy-done.1, s32[8,27]{1,0:T(8,128)S(1)} %copy-done.2, s32[64]{0:T(128)S(1)} %copy-done.3, bf16[2,27,128,128]{3,2,1,0:T(8,128)(2,1)S(1)} %copy-done, bf16[1,2,128,256]{3,2,1,0:T(8,128)(2,1)S(1)} %get-tuple-element.11.refs_0_.far0, ...), custom_call_target="tpu_custom_call" | custom-call | tf_op jit(solution)/shard_map/image_terms/pallas_call | solution.py:233
  17.5 1.4 %collective-permute-start.8 = (f16[1,2,128,128]{3,2,1,0:T(8,128)(2,1)S(1)}, f16[1,2,128,128]{3,2,1,0:T(8,128)(2,1)S(1)}, u32[]{:S(2)}, u32[]{:S(2)}) collective-permute-start(f16[1,2,128,128]{3,2,1,0:T(8,128)(2,1)S(1)} %get-tuple-element.15), channel_id=1, source_target_pairs={{0,3},{1,2},{2,1},{3,0},{4,7},{5,6},{6,5},{7,4},{8,11},{9,10},{10,... | collective-permute-start | bytes 196616 | tf_op jit(solution)/shard_map/ppermute | solution.py:300
  18.9 0.7 %collective-permute-start.7 = (f16[1,2,128,128]{3,2,1,0:T(8,128)(2,1)S(1)}, f16[1,2,128,128]{3,2,1,0:T(8,128)(2,1)S(1)}, u32[]{:S(2)}, u32[]{:S(2)}) collective-permute-start(f16[1,2,128,128]{3,2,1,0:T(8,128)(2,1)S(1)} %get-tuple-element.16), channel_id=1, source_target_pairs={{0,2},{1,3},{2,0},{3,1},{4,6},{5,7},{6,4},{7,5},{8,10},{9,11},{10,... | collective-permute-start | bytes 196616 | tf_op jit(solution)/shard_map/ppermute | solution.py:300
  19.6 1.4 %image_terms.2.mine = f32[2,2,128,128]{3,2,1,0:T(8,128)S(1)} custom-call(s32[8,27]{1,0:T(8,128)S(1)} %copy-done.1, s32[8,27]{1,0:T(8,128)S(1)} %copy-done.2, s32[64]{0:T(128)S(1)} %copy-done.3, bf16[2,27,128,128]{3,2,1,0:T(8,128)(2,1)S(1)} %copy-done, bf16[1,2,128,256]{3,2,1,0:T(8,128)(2,1)S(1)} %get-tuple-element.10.refs_0_.near0, ...), custom_call_target="tpu_custom_call" | custom-call | tf_op jit(solution)/shard_map/image_terms/pallas_call | solution.py:233
  21.1 0.1 collective-permute-start.3
  21.2 1.5 %collective-permute-start.14 = (bf16[2,1,128,128]{3,2,1,0:T(8,128)(2,1)S(1)}, bf16[2,1,128,128]{3,2,1,0:T(8,128)(2,1)S(1)}, u32[]{:S(2)}, u32[]{:S(2)}) collective-permute-start(bf16[2,1,128,128]{3,2,1,0:T(8,128)(2,1)S(1)} %pad_maximum_fusion), channel_id=1, source_target_pairs={{0,2},{1,3},{2,0},{3,1},{4,6},{5,7},{6,4},{7,5},{8,10},{9,11},{10,... | collective-permute-start | bytes 196616 | tf_op jit(solution)/shard_map/ppermute | solution.py:300
  22.8 0.6 %collective-permute-done.7 = f16[1,2,128,128]{3,2,1,0:T(8,128)(2,1)S(1)} collective-permute-done((f16[1,2,128,128]{3,2,1,0:T(8,128)(2,1)S(1)}, f16[1,2,128,128]{3,2,1,0:T(8,128)(2,1)S(1)}, u32[]{:S(2)}, u32[]{:S(2)}) %collective-permute-start.7) | collective-permute-done | bytes 65568 | tf_op jit(solution)/shard_map/ppermute | solution.py:300
  23.4 2.3 %collective-permute-done.14.refs_9_ = bf16[2,1,128,128]{3,2,1,0:T(8,128)(2,1)S(1)} collective-permute-done((bf16[2,1,128,128]{3,2,1,0:T(8,128)(2,1)S(1)}, bf16[2,1,128,128]{3,2,1,0:T(8,128)(2,1)S(1)}, u32[]{:S(2)}, u32[]{:S(2)}) %collective-permute-start.14) | collective-permute-done | bytes 65568 | tf_op jit(solution)/shard_map/ppermute | solution.py:300
  25.7 1.2 %final_images.1 = f32[1024,128]{1,0:T(8,128)} custom-call(f32[2,2,128,128]{3,2,1,0:T(8,128)S(1)} %image_terms.2.mine, f32[1,2,128,128]{3,2,1,0:T(8,128)S(1)} %convert_element_type.28.refs_0_, f32[1,2,128,128]{3,2,1,0:T(8,128)S(1)} %convert_element_type.30.refs_1_, f32[1,2,128,128]{3,2,1,0:T(8,128)S(1)} %convert_element_type.31.refs_2_, ...), custom_call_target="tpu_custom_call" | custom-call | tf_op jit(solution)/shard_map/final_images/pallas_call | solution.py:281
  (34 shorter events, 0.3 us)
Async XLA Ops:
  0.0 15.9 %copy-start.3 = (s32[64]{0:T(128)S(1)}, s32[64]{0:T(128)}, u32[]{:S(2)}) copy-start(s32[64]{0:T(128)} %colour.3) | copy-start | bytes 772
  0.0 15.9 %copy-start.2 = (s32[8,27]{1,0:T(8,128)S(1)}, s32[8,27]{1,0:T(8,128)}, u32[]{:S(2)}) copy-start(s32[8,27]{1,0:T(8,128)} %pattern.3) | copy-start | bytes 2596
  0.0 15.9 %copy-start.1 = (s32[8,27]{1,0:T(8,128)S(1)}, s32[8,27]{1,0:T(8,128)}, u32[]{:S(2)}) copy-start(s32[8,27]{1,0:T(8,128)} %neighbours.3) | copy-start | bytes 2596
  0.0 15.9 %copy-start = (bf16[2,27,128,128]{3,2,1,0:T(8,128)(2,1)S(1)}, bf16[2,27,128,128]{3,2,1,0:T(8,128)(2,1)}, u32[]{:S(2)}) copy-start(bf16[2,27,128,128]{3,2,1,0:T(8,128)(2,1)} %margin.3) | copy-start | bytes 5308420
  0.0 8.1 %copy-start.4 = (s32[8,2,1]{0,2,1:T(1,128)S(1)}, s32[8,2,1]{0,2,1:T(1,128)}, u32[]{:S(2)}) copy-start(s32[8,2,1]{0,2,1:T(1,128)} %param.9) | copy-start | bytes 196
  2.4 5.7 %collective-permute-start = (bf16[1,2,128,256]{3,2,1,0:T(8,128)(2,1)S(1)}, bf16[1,2,128,256]{3,2,1,0:T(8,128)(2,1)S(1)}, u32[]{:S(2)}, u32[]{:S(2)}) collective-permute-start(bf16[1,2,128,256]{3,2,1,0:T(8,128)(2,1)S(1)} %get-tuple-element.10.refs_0_.near0), channel_id=1, source_target_pairs={{0,1},{1,0},{2,3},{3,2},{4,5},{5,4},{6,7},{7,6},{8,9},{9,8},{10,11... | collective-permute-start | bytes 393224 | tf_op jit(solution)/shard_map/ppermute | solution.py:300
  3.0 5.1 %collective-permute-start.4 = (bf16[1,2,128,256]{3,2,1,0:T(8,128)(2,1)S(1)}, bf16[1,2,128,256]{3,2,1,0:T(8,128)(2,1)S(1)}, u32[]{:S(2)}, u32[]{:S(2)}) collective-permute-start(bf16[1,2,128,256]{3,2,1,0:T(8,128)(2,1)S(1)} %get-tuple-element.11.refs_0_.far0), channel_id=1, source_target_pairs={{0,1},{1,0},{2,3},{3,2},{4,5},{5,4},{6,7},{7,6},{8,9},{9,8},{10,11... | collective-permute-start | bytes 393224 | tf_op jit(solution)/shard_map/ppermute | solution.py:300
  3.0 10.5 %collective-permute-start.5 = (bf16[1,2,128,256]{3,2,1,0:T(8,128)(2,1)S(1)}, bf16[1,2,128,256]{3,2,1,0:T(8,128)(2,1)S(1)}, u32[]{:S(2)}, u32[]{:S(2)}) collective-permute-start(bf16[1,2,128,256]{3,2,1,0:T(8,128)(2,1)S(1)} %get-tuple-element.10.refs_0_.near0), channel_id=1, source_target_pairs={{0,2},{1,3},{2,0},{3,1},{4,6},{5,7},{6,4},{7,5},{8,10},{9,11},{10,... | collective-permute-start | bytes 393224 | tf_op jit(solution)/shard_map/ppermute | solution.py:300
  6.0 7.5 %collective-permute-start.10 = (f16[2,2,128,128]{3,2,1,0:T(8,128)(2,1)S(1)}, f16[2,2,128,128]{3,2,1,0:T(8,128)(2,1)S(1)}, u32[]{:S(2)}, u32[]{:S(2)}) collective-permute-start(f16[2,2,128,128]{3,2,1,0:T(8,128)(2,1)S(1)} %convert_element_type.32), channel_id=1, source_target_pairs={{0,2},{1,3},{2,0},{3,1},{4,6},{5,7},{6,4},{7,5},{8,10},{9,11},{10,... | collective-permute-start | bytes 393224 | tf_op jit(solution)/shard_map/ppermute | solution.py:300
  6.1 9.3 %collective-permute-start.1 = (bf16[1,2,128,256]{3,2,1,0:T(8,128)(2,1)S(1)}, bf16[1,2,128,256]{3,2,1,0:T(8,128)(2,1)S(1)}, u32[]{:S(2)}, u32[]{:S(2)}) collective-permute-start(bf16[1,2,128,256]{3,2,1,0:T(8,128)(2,1)S(1)} %get-tuple-element.11.refs_0_.far0), channel_id=1, source_target_pairs={{0,2},{1,3},{2,0},{3,1},{4,6},{5,7},{6,4},{7,5},{8,10},{9,11},{10,... | collective-permute-start | bytes 393224 | tf_op jit(solution)/shard_map/ppermute | solution.py:300
  8.7 7.0 %collective-permute-start.12 = (bf16[2,1,128,128]{3,2,1,0:T(8,128)(2,1)S(1)}, bf16[2,1,128,128]{3,2,1,0:T(8,128)(2,1)S(1)}, u32[]{:S(2)}, u32[]{:S(2)}) collective-permute-start(bf16[2,1,128,128]{3,2,1,0:T(8,128)(2,1)S(1)} %get-tuple-element.13), channel_id=1, source_target_pairs={{0,4},{4,8},{8,12},{12,16},{16,20},{20,24},{24,28},{28,0},{1,5},{5... | collective-permute-start | bytes 196616 | tf_op jit(solution)/shard_map/ppermute | solution.py:311
  10.3 5.5 %collective-permute-start.13 = (bf16[2,1,128,128]{3,2,1,0:T(8,128)(2,1)S(1)}, bf16[2,1,128,128]{3,2,1,0:T(8,128)(2,1)S(1)}, u32[]{:S(2)}, u32[]{:S(2)}) collective-permute-start(bf16[2,1,128,128]{3,2,1,0:T(8,128)(2,1)S(1)} %get-tuple-element.14), channel_id=1, source_target_pairs={{4,0},{8,4},{12,8},{16,12},{20,16},{24,20},{28,24},{0,28},{5,1},{9... | collective-permute-start | bytes 196616 | tf_op jit(solution)/shard_map/ppermute | solution.py:312
  13.5 2.3 %collective-permute-start.6 = (bf16[1,2,128,256]{3,2,1,0:T(8,128)(2,1)S(1)}, bf16[1,2,128,256]{3,2,1,0:T(8,128)(2,1)S(1)}, u32[]{:S(2)}, u32[]{:S(2)}) collective-permute-start(bf16[1,2,128,256]{3,2,1,0:T(8,128)(2,1)S(1)} %collective-permute-done.5.refs_2_), channel_id=1, source_target_pairs={{0,1},{1,0},{2,3},{3,2},{4,5},{5,4},{6,7},{7,6},{8,9},{9,8},{10,11... | collective-permute-start | bytes 393224 | tf_op jit(solution)/shard_map/ppermute | solution.py:300
  13.5 7.6 %collective-permute-start.9 = (f16[2,2,128,128]{3,2,1,0:T(8,128)(2,1)S(1)}, f16[2,2,128,128]{3,2,1,0:T(8,128)(2,1)S(1)}, u32[]{:S(2)}, u32[]{:S(2)}) collective-permute-start(f16[2,2,128,128]{3,2,1,0:T(8,128)(2,1)S(1)} %convert_element_type.32), channel_id=1, source_target_pairs={{0,1},{1,0},{2,3},{3,2},{4,5},{5,4},{6,7},{7,6},{8,9},{9,8},{10,11... | collective-permute-start | bytes 393224 | tf_op jit(solution)/shard_map/ppermute | solution.py:300
  15.3 7.4 %collective-permute-start.11 = (f16[2,2,128,128]{3,2,1,0:T(8,128)(2,1)S(1)}, f16[2,2,128,128]{3,2,1,0:T(8,128)(2,1)S(1)}, u32[]{:S(2)}, u32[]{:S(2)}) collective-permute-start(f16[2,2,128,128]{3,2,1,0:T(8,128)(2,1)S(1)} %collective-permute-done.10), channel_id=1, source_target_pairs={{0,1},{1,0},{2,3},{3,2},{4,5},{5,4},{6,7},{7,6},{8,9},{9,8},{10,11... | collective-permute-start | bytes 393224 | tf_op jit(solution)/shard_map/ppermute | solution.py:300
  15.8 3.8 %collective-permute-start.2 = (bf16[1,2,128,256]{3,2,1,0:T(8,128)(2,1)S(1)}, bf16[1,2,128,256]{3,2,1,0:T(8,128)(2,1)S(1)}, u32[]{:S(2)}, u32[]{:S(2)}) collective-permute-start(bf16[1,2,128,256]{3,2,1,0:T(8,128)(2,1)S(1)} %collective-permute-done.1.refs_2_), channel_id=1, source_target_pairs={{0,1},{1,0},{2,3},{3,2},{4,5},{5,4},{6,7},{7,6},{8,9},{9,8},{10,11... | collective-permute-start | bytes 393224 | tf_op jit(solution)/shard_map/ppermute | solution.py:300
  17.5 5.3 %collective-permute-start.8 = (f16[1,2,128,128]{3,2,1,0:T(8,128)(2,1)S(1)}, f16[1,2,128,128]{3,2,1,0:T(8,128)(2,1)S(1)}, u32[]{:S(2)}, u32[]{:S(2)}) collective-permute-start(f16[1,2,128,128]{3,2,1,0:T(8,128)(2,1)S(1)} %get-tuple-element.15), channel_id=1, source_target_pairs={{0,3},{1,2},{2,1},{3,0},{4,7},{5,6},{6,5},{7,4},{8,11},{9,10},{10,... | collective-permute-start | bytes 196616 | tf_op jit(solution)/shard_map/ppermute | solution.py:300
  18.9 4.5 %collective-permute-start.7 = (f16[1,2,128,128]{3,2,1,0:T(8,128)(2,1)S(1)}, f16[1,2,128,128]{3,2,1,0:T(8,128)(2,1)S(1)}, u32[]{:S(2)}, u32[]{:S(2)}) collective-permute-start(f16[1,2,128,128]{3,2,1,0:T(8,128)(2,1)S(1)} %get-tuple-element.16), channel_id=1, source_target_pairs={{0,2},{1,3},{2,0},{3,1},{4,6},{5,7},{6,4},{7,5},{8,10},{9,11},{10,... | collective-permute-start | bytes 196616 | tf_op jit(solution)/shard_map/ppermute | solution.py:300
  21.1 2.3 %collective-permute-start.3 = (f16[1,2,128,128]{3,2,1,0:T(8,128)(2,1)S(1)}, f16[1,2,128,128]{3,2,1,0:T(8,128)(2,1)S(1)}, u32[]{:S(2)}, u32[]{:S(2)}) collective-permute-start(f16[1,2,128,128]{3,2,1,0:T(8,128)(2,1)S(1)} %fusion), channel_id=1, source_target_pairs={{0,1},{1,0},{2,3},{3,2},{4,5},{5,4},{6,7},{7,6},{8,9},{9,8},{10,11... | collective-permute-start | bytes 196616 | tf_op jit(solution)/shard_map/ppermute | solution.py:300
  21.2 4.5 %collective-permute-start.14 = (bf16[2,1,128,128]{3,2,1,0:T(8,128)(2,1)S(1)}, bf16[2,1,128,128]{3,2,1,0:T(8,128)(2,1)S(1)}, u32[]{:S(2)}, u32[]{:S(2)}) collective-permute-start(bf16[2,1,128,128]{3,2,1,0:T(8,128)(2,1)S(1)} %pad_maximum_fusion), channel_id=1, source_target_pairs={{0,2},{1,3},{2,0},{3,1},{4,6},{5,7},{6,4},{7,5},{8,10},{9,11},{10,... | collective-permute-start | bytes 196616 | tf_op jit(solution)/shard_map/ppermute | solution.py:300

commit v3 on v2

v3 whole, which is shorter than its diff:
```python
import functools
import math

import jax
import jax.numpy as jnp
from jax import lax
from jax.experimental import pallas as pl
from jax.experimental.pallas import tpu as pltpu
from jax.sharding import PartitionSpec as P

CENTRE = 1.0
HALF_WIDTH = 0.9
HBM = pl.BlockSpec(memory_space=pltpu.HBM)
SMEM = pl.BlockSpec(memory_space=pltpu.SMEM)
VMEM = pl.BlockSpec(memory_space=pltpu.VMEM)
WIRE = jnp.float16
WIRE_SCALE = 0.5
CHUNK = 9


def cheb_coefficients():
    samples = []
    for index_k in range(3):
        angle_value = math.pi * (index_k + 0.5) / 3.0
        samples.append((angle_value, (CENTRE + HALF_WIDTH * math.cos(angle_value)) ** (-0.5)))
    coeffs = []
    for order in range(3):
        coeffs.append(
            2.0
            / 3.0
            * sum((value * math.cos(order * angle_value) for angle_value, value in samples))
        )
    coeffs[0] = 0.5 * coeffs[0]
    return coeffs


def unit(orbits):
    down = lax.broadcasted_iota(jnp.int32, (orbits, orbits), 0)
    along = lax.broadcasted_iota(jnp.int32, (orbits, orbits), 1)
    return (down == along).astype(jnp.float32)


def like(shape, dtype):
    return jax.ShapeDtypeStruct(shape, dtype)


def call(kernel, name, ins, outs, scratch, args, extra=2):
    held = [*outs, *(s for s in scratch if isinstance(s, jax.ShapeDtypeStruct))]
    held += [a for spec, a in zip(ins, args) if spec is VMEM]
    total = sum(math.prod(s.shape) * jnp.dtype(s.dtype).itemsize for s in held)
    return pl.pallas_call(
        kernel,
        out_shape=tuple(outs),
        in_specs=ins,
        out_specs=(VMEM,) * len(outs),
        scratch_shapes=[
            pltpu.VMEM(s.shape, s.dtype) if isinstance(s, jax.ShapeDtypeStruct) else s
            for s in scratch
        ],
        compiler_params=pltpu.CompilerParams(vmem_limit_bytes=total + (extra << 20)),
        cost_estimate=pl.CostEstimate(flops=1000, bytes_accessed=1000, transcendentals=0),
        name=name,
    )(*args)


def first_kernel(ndomain, ncolour, *refs):
    tables, margin = refs[:4], refs[4]
    near, far, sums, blocks, totals = refs[5:10]
    neighbours, pattern, colour, sends, table, sems, small = refs[10:]
    domain = lax.axis_index("dom")
    shade = lax.axis_index("col")
    rows, slots, orbits, _ = margin.shape
    own = neighbours.shape[0]
    width = sends.shape[1]
    loads = [
        pltpu.make_async_copy(source, target, small.at[i])
        for i, (source, target) in enumerate(zip(tables, (neighbours, pattern, colour, sends)))
    ]
    for load in loads:
        load.start()
    copies = []
    for row in range(rows):
        for i, k in enumerate(range(0, slots, CHUNK)):
            part = pl.ds(k, min(CHUNK, slots - k))
            copies.append(
                pltpu.make_async_copy(margin.at[row, part], blocks.at[row, part], sems.at[row, i])
            )
    for copy in copies:
        copy.start()
    sums[...] = jnp.zeros_like(sums)
    totals[...] = jnp.zeros_like(totals)
    base = shade - lax.rem(shade, 2)
    lower = lax.rem(domain + ndomain - 1, ndomain)
    upper = lax.rem(domain + 1, ndomain)
    for load in loads:
        load.wait()
    for i in range(own):
        table[i] = colour[domain * own + i] ^ base
    for i in range(width):
        table[own + i] = colour[lower * own + sends[1, i, lower]] ^ base
        table[own + width + i] = colour[upper * own + sends[0, i, upper]] ^ base
    eye = unit(orbits)
    half = ncolour // 4
    for row in range(rows):
        block = shade * rows + row
        totals[row, table[block]] = (-CENTRE) * eye
        for k0 in range(0, slots, CHUNK):
            copies.pop(0).wait()

            @pl.loop(k0, min(k0 + CHUNK, slots))
            def _(k):
                entry = jnp.where(pattern[block, k] == 1, neighbours[block, k], own + 2 * width)
                sums[row, entry] += blocks[row, k].astype(jnp.float32)

        @pl.loop(0, own + 2 * width)
        def _(entry):
            totals[row, table[entry]] += sums[row, entry]

        for c in range(ncolour):
            r = c // 2
            (near if r < half else far)[r % half, c % 2, row] = (
                totals[row, c] * (1.0 / HALF_WIDTH)
            ).astype(jnp.bfloat16)


def first_terms(ndomain, ncolour, neighbours, pattern, colour, sends, margin):
    rows, slots, orbits, _ = margin.shape
    ext = neighbours.shape[0] + 2 * sends.shape[1]
    half = like((ncolour // 4, 2, rows, orbits, orbits), jnp.bfloat16)
    sums = like((rows, ext + 1, orbits, orbits), jnp.float32)
    tables = [neighbours, pattern, colour, sends]
    return call(
        functools.partial(first_kernel, ndomain, ncolour),
        "first_terms",
        [HBM] * 5,
        [half, half, sums],
        [
            like(margin.shape, margin.dtype),
            like((rows, ncolour, orbits, orbits), jnp.float32),
            *[pltpu.SMEM(t.shape, jnp.int32) for t in tables],
            pltpu.SMEM((ext,), jnp.int32),
            pltpu.SemaphoreType.DMA((rows, pl.cdiv(slots, CHUNK))),
            pltpu.SemaphoreType.DMA((4,)),
        ],
        [pltpu.with_memory_space_constraint(t, pltpu.HBM) for t in tables + [margin]],
    )


def border_kernel(sends, near0, far0, near1, far1, up, down):
    domain = lax.axis_index("dom")
    shade = lax.axis_index("col")
    parity = lax.rem(shade, 2)
    half, _, rows, orbits, _ = near0.shape
    for side, out in ((1, up), (0, down)):
        for i in range(sends.shape[1]):
            entry = sends[side, i, domain]
            relative = lax.div(entry, rows) ^ shade
            row = lax.rem(entry, rows)

            @pl.when(relative == 0)
            def _():
                for s in range(2 * half):
                    out[s, i] = (near0 if s < half else far0)[s % half, parity, row]

            @pl.when(relative == 1)
            def _():
                for s in range(2 * half):
                    out[s, i] = (near1 if s < half else far1)[s % half, parity, row]

            @pl.when(relative > 1)
            def _():
                for s in range(2 * half):
                    out[s, i] = jnp.zeros(out.shape[2:], out.dtype)


def borders(sends, near0, far0, near1, far1):
    half, _, _, orbits, _ = near0.shape
    out = like((2 * half, sends.shape[1], orbits, orbits), jnp.bfloat16)
    return call(
        border_kernel,
        "borders",
        [SMEM] + [VMEM] * 4,
        [out, out],
        [],
        [sends, near0, far0, near1, far1],
    )


def split_kernel(own, sums, left):
    shade = lax.axis_index("col")
    rows, _, orbits, _ = sums.shape
    for spot in range(own):
        entry = ((spot // rows) ^ shade) * rows + spot % rows
        for row in range(rows):
            value = sums[row, entry]
            high = value.astype(jnp.bfloat16)
            low = (value - high.astype(jnp.float32)).astype(jnp.bfloat16)
            lanes = slice(spot * orbits, (spot + 1) * orbits)
            left[2 * row * orbits : (2 * row + 1) * orbits, lanes] = high
            left[(2 * row + 1) * orbits : (2 * row + 2) * orbits, lanes] = low


def split_sums(own, sums):
    rows, _, orbits, _ = sums.shape
    left = like((2 * rows * orbits, own * orbits), jnp.bfloat16)
    return call(functools.partial(split_kernel, own), "split_sums", [VMEM], [left], [], [sums])[0]


def image_kernel(coeffs, upper_half, own, colour, left, *refs):
    pieces, images = refs[:-1], refs[-1]
    domain = lax.axis_index("dom")
    shade = lax.axis_index("col")
    parity = lax.rem(shade, 2)
    base = shade - parity
    half, _, rows, orbits, _ = pieces[0].shape
    eye = unit(orbits)
    for r in range(half):
        right = []
        for relative, piece in enumerate(pieces):
            turn = ((relative // 2) % half) ^ r
            for row in range(rows):
                right.append(jnp.concatenate([piece[turn, 0, row], piece[turn, 1, row]], axis=1))
        total = jnp.dot(
            left[...], jnp.concatenate(right, axis=0), preferred_element_type=jnp.float32
        )
        for row in range(rows):
            mine = colour[domain * own + shade * rows + row] ^ base
            high = total[2 * row * orbits : (2 * row + 1) * orbits]
            low = total[(2 * row + 1) * orbits : (2 * row + 2) * orbits]
            product = high + low
            for q in range(2):
                first = pieces[0][r, q, row].astype(jnp.float32)
                relative = 2 * (r + (half if upper_half else 0)) + q
                probe = jnp.where(mine == relative, eye, 0.0)
                applied = product[:, q * orbits : (q + 1) * orbits] - CENTRE * first
                applied = applied * (1.0 / HALF_WIDTH)
                images[2 * r + (parity ^ q), row] = (
                    coeffs[0] * probe + coeffs[1] * first + coeffs[2] * (2.0 * applied - probe)
                )


def image_terms(coeffs, upper_half, own, colour, left, pieces):
    half, _, rows, orbits, _ = pieces[0].shape
    images = like((2 * half, rows, orbits, orbits), jnp.float32)
    return call(
        functools.partial(image_kernel, coeffs, upper_half, own),
        "image_terms",
        [SMEM] + [VMEM] * (1 + len(pieces)),
        [images],
        [],
        [colour, left, *pieces],
        4,
    )[0]


def final_kernel(scale, count, mine, *refs):
    images, refs = refs[: count - 1], refs[count - 1 :]
    blocks, refs = refs[:count], refs[count:]
    firsts, out = refs[:-1], refs[-1]
    shade = lax.axis_index("col")
    rows, wide, orbits, _ = blocks[0].shape
    width = wide // 2
    right = []
    for e in range(wide):
        side, i = divmod(e, width)
        value = firsts[side][0, i].astype(jnp.float32)
        for other in firsts[2:]:
            value += other[side, i].astype(jnp.float32)
        right.append(value.astype(jnp.bfloat16))
    right = jnp.concatenate(right + right, axis=0)
    for relative in range(count):
        for row in range(rows):
            left = jnp.concatenate([blocks[relative][row, e] for e in range(wide)], axis=1)
            high = left.astype(jnp.bfloat16)
            low = (left - high.astype(jnp.float32)).astype(jnp.bfloat16)
            extra = jnp.dot(
                jnp.concatenate([high, low], axis=1), right, preferred_element_type=jnp.float32
            )
            if relative == 0:
                value = mine[0, row]
            else:
                value = images[relative - 1][row] * (1.0 / WIRE_SCALE)
            at = (shade ^ relative) * rows + row
            out[pl.ds(pl.multiple_of(at * orbits, orbits), orbits), :] = value + scale * extra


def final_images(scale, mine, images, blocks, firsts):
    count = len(blocks)
    rows, _, orbits, _ = blocks[0].shape
    return call(
        functools.partial(final_kernel, scale, count),
        "final_images",
        [VMEM] * (1 + len(images) + len(blocks) + len(firsts)),
        [like((count * rows * orbits, orbits), jnp.float32)],
        [],
        [mine, *images, *blocks, *firsts],
        4,
    )[0]


def per_device(ndomain, ncolour, margin, neighbours, pattern, colour, send_list):
    coeffs = cheb_coefficients()
    pairs = ncolour // 2
    half = pairs // 2
    sends = jnp.transpose(send_list, (1, 2, 0))
    rows, width = margin.shape[0], send_list.shape[2]
    own = neighbours.shape[0]

    def across(value, step):
        return lax.ppermute(value, "col", [(i, i ^ step) for i in range(ncolour)])

    near, far, sums = first_terms(ndomain, ncolour, neighbours, pattern, colour, sends, margin)
    border = sums[:, own : own + 2 * width]
    left = split_sums(own, sums)
    wire = border.astype(WIRE)
    nears, fars, wires = {0: near}, {0: far}, [wire]
    for s in range(1, pairs):
        nears[2 * s] = across(near, 2 * s)
        fars[2 * s] = across(far, 2 * s)
    nears[1] = across(near, 1)
    fars[1] = across(far, 1)
    up, down = borders(sends, near, far, nears[1], fars[1])
    onward = [(i, (i + 1) % ndomain) for i in range(ndomain)]
    before = lax.ppermute(up, "dom", onward)
    after = lax.ppermute(down, "dom", [(j, i) for i, j in onward])
    for s in range(1, pairs):
        wires.append(across(wire, 2 * s))
    for s in range(1, pairs):
        nears[2 * s], _, _ = lax.optimization_barrier((nears[2 * s], up, down))
        nears[2 * s + 1] = across(nears[2 * s], 1)
    for s in range(1, pairs):
        fars[2 * s + 1] = across(fars[2 * s], 1)

    def pieces(upper):
        picked = []
        for relative in range(ncolour):
            top = relative // 2 >= half
            picked.append((nears if top == upper else fars)[relative])
        return picked

    outer = image_terms(coeffs, True, own, colour, left, pieces(True))
    before, after, outer = lax.optimization_barrier((before, after, outer))
    others = across(jnp.concatenate(wires), 1)
    blocks = []
    for s in range(pairs):
        for side in (wires[s], others[s * rows : (s + 1) * rows]):
            blocks.append(side.astype(jnp.float32))
    blocks[0] = border
    images = {}
    sent = (outer * WIRE_SCALE).astype(WIRE)
    for m in range(pairs, ncolour):
        images[m] = sent[m - pairs]
    inner = image_terms(coeffs, False, own, colour, left, pieces(False))
    sent = (inner * WIRE_SCALE).astype(WIRE)
    for m in range(1, pairs):
        images[m] = sent[m]
    firsts = [before, after]
    for m in images:
        if m % 2:
            images[m] = across(images[m], m)
        else:
            second = jnp.stack([before[m // 2], after[m // 2]]).astype(WIRE)
            sent = jnp.concatenate([images[m], second.reshape((-1,) + images[m].shape[1:])])
            sent = across(sent, m)
            images[m], second = sent[:rows], sent[rows:]
            firsts.append(second.reshape((2, width) + second.shape[1:]).astype(jnp.bfloat16))
    return final_images(
        2.0 * coeffs[2] / HALF_WIDTH,
        inner,
        [images[m].astype(jnp.float32) for m in range(1, ncolour)],
        blocks,
        firsts,
    )


def solution(mesh):
    placed = (P(("dom", "col"), None, None, None), P("dom", None), P("dom", None), P(), P())
    return jax.shard_map(
        functools.partial(per_device, mesh.shape["dom"], mesh.shape["col"]),
        mesh=mesh,
        in_specs=placed,
        out_specs=P("dom", "col"),
        check_vma=False,
    )
```

time: 27 us -> 23 us (0.85)
  starting transfers between devices: 14.7 us -> 13 us
  waiting for transfers between devices: 4.57 us -> 3.06 us
  Pallas kernels: 7.19 us -> 6.24 us
    ppermute x13 -> x11, starting transfers between devices: 9.93 us -> 7.85 us  [across(): return lax.ppermute(value, 'col', [(i, i ^ step) for i in range(ncolour)])]
    ppermute x13 -> x11, waiting for transfers between devices: 4.14 us -> 3.05 us  [across(): return lax.ppermute(value, 'col', [(i, i ^ step) for i in range(ncolour)])]
    pallas_call x5 -> x6, Pallas kernels: 7.19 us -> 6.24 us  [call(): pl.pallas_call(kernel, out_shape=tuple(outs), in_specs=ins, out_specs=(VM...]
    ppermute x1, starting transfers between devices: 1.57 us -> 2.07 us  [per_device(): before = lax.ppermute(up, 'dom', onward)]
    ppermute x1, waiting for transfers between devices: 0.43 us -> 0.01 us  [per_device(): before = lax.ppermute(up, 'dom', onward)]
  transfers between devices with their start and end apart: 15 -> 13, of which waited for: 4 -> 1; matrix products, arithmetic and copies ran while one was open for 1% -> 1% of each run, Pallas kernels for 13% -> 13%
where the time goes in v3:
time: 23 us; the launch traced here: 22.9 us
  starting transfers between devices  13 us (57%)
  Pallas kernels  6.24 us (27%)
  waiting for transfers between devices  3.06 us (13%)
  other arithmetic  0.32 us (1%)
    ppermute x11, starting transfers between devices, across(): return lax.ppermute(value, 'col', [(i, i ^ step) for i in range(ncolour)])  7.85 us
    pallas_call x6, Pallas kernels, call(): pl.pallas_call(kernel, out_shape=tuple(outs), in_specs=ins, out_specs=(VM...  6.24 us
    ppermute x1, starting transfers between devices, per_device(): after = lax.ppermute(down, 'dom', [(j, i) for i, j in onward])  3.1 us
    ppermute x11, waiting for transfers between devices, across(): return lax.ppermute(value, 'col', [(i, i ^ step) for i in range(ncolour)])  3.05 us
    ppermute x1, starting transfers between devices, per_device(): before = lax.ppermute(up, 'dom', onward)  2.07 us
  transfers between devices with their start and end apart: 13, of which 1 were waited for; matrix products, arithmetic and copies ran while one was open for 1% of the time, Pallas kernels for 13%

profile of v3, /device:TPU:0, one launch (start us, length us, event | category | flops | bytes accessed | tf_op | source)
XLA Modules:
  0.0 22.9 jit_solution(4348380184293181314)
XLA Ops:
  0.0 2.1 %first_terms.1 = (bf16[1,2,2,128,128]{4,3,2,1,0:T(8,128)(2,1)S(1)}, bf16[1,2,2,128,128]{4,3,2,1,0:T(8,128)(2,1)S(1)}, f32[2,11,128,128]{3,2,1,0:T(8,128)S(1)}) custom-call(s32[8,27]{1,0:T(8,128)} %refs_0_.1, s32[8,27]{1,0:T(8,128)} %refs_1_.1, s32[64]{0:T(128)} %colour.3, s32[2,1,8]{2,1,0:T(1,128)} %bitcast.13, bf16[2,27,128,128]{3,2,1,0:T(8,128)(2,1)} %refs_4_.1), custom_call_target="tpu_custom_call" | custom-call | flops 1000 | bytes 1000 | tf_op jit(solution)/shard_map/first_terms/pallas_call | solution.py:51
  2.1 0.5 %collective-permute-start = (bf16[1,2,2,128,128]{4,3,2,1,0:T(8,128)(2,1)S(1)}, bf16[1,2,2,128,128]{4,3,2,1,0:T(8,128)(2,1)S(1)}, u32[]{:S(2)}, u32[]{:S(2)}) collective-permute-start(bf16[1,2,2,128,128]{4,3,2,1,0:T(8,128)(2,1)S(1)} %get-tuple-element.15.refs_0_.near0), channel_id=1, source_target_pairs={{0,1},{1,0},{2,3},{3,2},{4,5},{5,4},{6,7},{7,6},{8,9},{9,8},{10,11... | collective-permute-start | bytes 393224 | tf_op jit(solution)/shard_map/ppermute | solution.py:310
  2.7 0.1 collective-permute-start.4
  2.7 2.9 %collective-permute-start.7 = (bf16[1,2,2,128,128]{4,3,2,1,0:T(8,128)(2,1)S(1)}, bf16[1,2,2,128,128]{4,3,2,1,0:T(8,128)(2,1)S(1)}, u32[]{:S(2)}, u32[]{:S(2)}) collective-permute-start(bf16[1,2,2,128,128]{4,3,2,1,0:T(8,128)(2,1)S(1)} %get-tuple-element.15.refs_0_.near0), channel_id=1, source_target_pairs={{0,2},{1,3},{2,0},{3,1},{4,6},{5,7},{6,4},{7,5},{8,10},{9,11},{10,... | collective-permute-start | bytes 393224 | tf_op jit(solution)/shard_map/ppermute | solution.py:310
  5.7 0.0 collective-permute-start.1
  5.7 0.6 %borders.1 = (bf16[2,1,128,128]{3,2,1,0:T(8,128)(2,1)S(1)}, bf16[2,1,128,128]{3,2,1,0:T(8,128)(2,1)S(1)}) custom-call(s32[2,1,8]{2,1,0:T(1,128)S(1)} %bitcast.14, bf16[1,2,2,128,128]{4,3,2,1,0:T(8,128)(2,1)S(1)} %get-tuple-element.15.refs_0_.near0, bf16[1,2,2,128,128]{4,3,2,1,0:T(8,128)(2,1)S(1)} %get-tuple-element.16.far0.refs_0_, ...), custom_call_target="tpu_custom_call" | custom-call | flops 1000 | bytes 1000 | tf_op jit(solution)/shard_map/borders/pallas_call | solution.py:51
  6.3 2.1 %collective-permute-start.5 = (bf16[2,1,128,128]{3,2,1,0:T(8,128)(2,1)S(1)}, bf16[2,1,128,128]{3,2,1,0:T(8,128)(2,1)S(1)}, u32[]{:S(2)}, u32[]{:S(2)}) collective-permute-start(bf16[2,1,128,128]{3,2,1,0:T(8,128)(2,1)S(1)} %get-tuple-element.17), channel_id=1, source_target_pairs={{0,4},{4,8},{8,12},{12,16},{16,20},{20,24},{24,28},{28,0},{1,5},{5... | collective-permute-start | bytes 196616 | tf_op jit(solution)/shard_map/ppermute | solution.py:324
  8.4 3.1 %collective-permute-start.6 = (bf16[2,1,128,128]{3,2,1,0:T(8,128)(2,1)S(1)}, bf16[2,1,128,128]{3,2,1,0:T(8,128)(2,1)S(1)}, u32[]{:S(2)}, u32[]{:S(2)}) collective-permute-start(bf16[2,1,128,128]{3,2,1,0:T(8,128)(2,1)S(1)} %get-tuple-element.18), channel_id=1, source_target_pairs={{4,0},{8,4},{12,8},{16,12},{20,16},{24,20},{28,24},{0,28},{5,1},{9... | collective-permute-start | bytes 196616 | tf_op jit(solution)/shard_map/ppermute | solution.py:325
  11.5 0.0 collective-permute-done.7.refs_2_
  11.5 0.0 collective-permute-start.8
  11.6 1.7 %collective-permute-start.11 = (f16[2,2,128,128]{3,2,1,0:T(8,128)(2,1)S(1)}, f16[2,2,128,128]{3,2,1,0:T(8,128)(2,1)S(1)}, u32[]{:S(2)}, u32[]{:S(2)}) collective-permute-start(f16[2,2,128,128]{3,2,1,0:T(8,128)(2,1)S(1)} %get-tuple-element.23), channel_id=1, source_target_pairs={{0,2},{1,3},{2,0},{3,1},{4,6},{5,7},{6,4},{7,5},{8,10},{9,11},{10,... | collective-permute-start | bytes 393224 | tf_op jit(solution)/shard_map/ppermute | solution.py:310
  13.2 0.3 %split_sums.1.left = bf16[512,1024]{1,0:T(8,128)(2,1)S(1)} custom-call(f32[2,11,128,128]{3,2,1,0:T(8,128)S(1)} %get-tuple-element.14.sums), custom_call_target="tpu_custom_call" | custom-call | flops 1000 | bytes 1000 | tf_op jit(solution)/shard_map/split_sums/pallas_call | solution.py:51
  13.5 0.3 %collective-permute-start.2 = (bf16[1,2,2,128,128]{4,3,2,1,0:T(8,128)(2,1)S(1)}, bf16[1,2,2,128,128]{4,3,2,1,0:T(8,128)(2,1)S(1)}, u32[]{:S(2)}, u32[]{:S(2)}) collective-permute-start(bf16[1,2,2,128,128]{4,3,2,1,0:T(8,128)(2,1)S(1)} %collective-permute-done.1.refs_2_), channel_id=1, source_target_pairs={{0,1},{1,0},{2,3},{3,2},{4,5},{5,4},{6,7},{7,6},{8,9},{9,8},{10,11... | collective-permute-start | bytes 393224 | tf_op jit(solution)/shard_map/ppermute | solution.py:310
  13.8 0.0 collective-permute-done.8.refs_3_
  13.8 1.0 %image_terms.3 = f32[2,2,128,128]{3,2,1,0:T(8,128)S(1)} custom-call(s32[64]{0:T(128)S(1)} %copy-done, bf16[512,1024]{1,0:T(8,128)(2,1)S(1)} %split_sums.1.left, bf16[1,2,2,128,128]{4,3,2,1,0:T(8,128)(2,1)S(1)} %get-tuple-element.16.far0.refs_0_, bf16[1,2,2,128,128]{4,3,2,1,0:T(8,128)(2,1)S(1)} %collective-permute-done.4.far1.refs_1_, ...), custom_call_target="tpu_custom_call" | custom-call | flops 1000 | bytes 1000 | tf_op jit(solution)/shard_map/image_terms/pallas_call | solution.py:51
  14.8 0.0 collective-permute-done.5.refs_7_
  15.0 0.7 %collective-permute-start.9 = (f16[4,128,128]{2,1,0:T(8,128)(2,1)S(1)}, f16[4,128,128]{2,1,0:T(8,128)(2,1)S(1)}, u32[]{:S(2)}, u32[]{:S(2)}) collective-permute-start(f16[4,128,128]{2,1,0:T(8,128)(2,1)S(1)} %pad_maximum_fusion.1), channel_id=1, source_target_pairs={{0,2},{1,3},{2,0},{3,1},{4,6},{5,7},{6,4},{7,5},{8,10},{9,11},{10,... | collective-permute-start | bytes 393224 | tf_op jit(solution)/shard_map/ppermute | solution.py:310
  15.7 1.0 %collective-permute-start.10 = (f16[2,128,128]{2,1,0:T(8,128)(2,1)S(1)}, f16[2,128,128]{2,1,0:T(8,128)(2,1)S(1)}, u32[]{:S(2)}, u32[]{:S(2)}) collective-permute-start(f16[2,128,128]{2,1,0:T(8,128)(2,1)S(1)} %get-tuple-element.29), channel_id=1, source_target_pairs={{0,3},{1,2},{2,1},{3,0},{4,7},{5,6},{6,5},{7,4},{8,11},{9,10},{10,... | collective-permute-start | bytes 196616 | tf_op jit(solution)/shard_map/ppermute | solution.py:310
  16.7 1.0 %image_terms.2.mine = f32[2,2,128,128]{3,2,1,0:T(8,128)S(1)} custom-call(s32[64]{0:T(128)S(1)} %copy-done, bf16[512,1024]{1,0:T(8,128)(2,1)S(1)} %split_sums.1.left, bf16[1,2,2,128,128]{4,3,2,1,0:T(8,128)(2,1)S(1)} %get-tuple-element.15.refs_0_.near0, bf16[1,2,2,128,128]{4,3,2,1,0:T(8,128)(2,1)S(1)} %collective-permute-done.refs_1_.near1, ...), custom_call_target="tpu_custom_call" | custom-call | flops 1000 | bytes 1000 | tf_op jit(solution)/shard_map/image_terms/pallas_call | solution.py:51
  17.7 0.6 %collective-permute-start.3 = (f16[2,128,128]{2,1,0:T(8,128)(2,1)S(1)}, f16[2,128,128]{2,1,0:T(8,128)(2,1)S(1)}, u32[]{:S(2)}, u32[]{:S(2)}) collective-permute-start(f16[2,128,128]{2,1,0:T(8,128)(2,1)S(1)} %fusion.1), channel_id=1, source_target_pairs={{0,1},{1,0},{2,3},{3,2},{4,5},{5,4},{6,7},{7,6},{8,9},{9,8},{10,11... | collective-permute-start | bytes 196616 | tf_op jit(solution)/shard_map/ppermute | solution.py:310
  18.3 0.1 pad_maximum_fusion
  18.4 0.1 collective-permute-start.12
  18.5 3.0 %collective-permute-done.10 = f16[2,128,128]{2,1,0:T(8,128)(2,1)S(1)} collective-permute-done((f16[2,128,128]{2,1,0:T(8,128)(2,1)S(1)}, f16[2,128,128]{2,1,0:T(8,128)(2,1)S(1)}, u32[]{:S(2)}, u32[]{:S(2)}) %collective-permute-start.10) | collective-permute-done | bytes 65568 | tf_op jit(solution)/shard_map/ppermute | solution.py:310
  21.7 1.2 %final_images.1 = f32[1024,128]{1,0:T(8,128)} custom-call(f32[2,2,128,128]{3,2,1,0:T(8,128)S(1)} %image_terms.2.mine, f32[2,128,128]{2,1,0:T(8,128)S(1)} %convert_element_type.39.refs_0_, f32[2,128,128]{2,1,0:T(8,128)S(1)} %get-tuple-element.28.refs_1_, f32[2,128,128]{2,1,0:T(8,128)S(1)} %convert_element_type.43.refs_2_, ...), custom_call_target="tpu_custom_call" | custom-call | flops 1000 | bytes 1000 | tf_op jit(solution)/shard_map/final_images/pallas_call | solution.py:51
  (25 shorter events, 0.3 us)
Async XLA Ops:
  0.0 5.7 %copy-start.1 = (s32[8,2,1]{0,2,1:T(1,128)S(1)}, s32[8,2,1]{0,2,1:T(1,128)}, u32[]{:S(2)}) copy-start(s32[8,2,1]{0,2,1:T(1,128)} %param.9) | copy-start | bytes 196
  2.1 3.6 %collective-permute-start = (bf16[1,2,2,128,128]{4,3,2,1,0:T(8,128)(2,1)S(1)}, bf16[1,2,2,128,128]{4,3,2,1,0:T(8,128)(2,1)S(1)}, u32[]{:S(2)}, u32[]{:S(2)}) collective-permute-start(bf16[1,2,2,128,128]{4,3,2,1,0:T(8,128)(2,1)S(1)} %get-tuple-element.15.refs_0_.near0), channel_id=1, source_target_pairs={{0,1},{1,0},{2,3},{3,2},{4,5},{5,4},{6,7},{7,6},{8,9},{9,8},{10,11... | collective-permute-start | bytes 393224 | tf_op jit(solution)/shard_map/ppermute | solution.py:310
  2.7 3.0 %collective-permute-start.4 = (bf16[1,2,2,128,128]{4,3,2,1,0:T(8,128)(2,1)S(1)}, bf16[1,2,2,128,128]{4,3,2,1,0:T(8,128)(2,1)S(1)}, u32[]{:S(2)}, u32[]{:S(2)}) collective-permute-start(bf16[1,2,2,128,128]{4,3,2,1,0:T(8,128)(2,1)S(1)} %get-tuple-element.16.far0.refs_0_), channel_id=1, source_target_pairs={{0,1},{1,0},{2,3},{3,2},{4,5},{5,4},{6,7},{7,6},{8,9},{9,8},{10,11... | collective-permute-start | bytes 393224 | tf_op jit(solution)/shard_map/ppermute | solution.py:310
  2.7 8.8 %collective-permute-start.7 = (bf16[1,2,2,128,128]{4,3,2,1,0:T(8,128)(2,1)S(1)}, bf16[1,2,2,128,128]{4,3,2,1,0:T(8,128)(2,1)S(1)}, u32[]{:S(2)}, u32[]{:S(2)}) collective-permute-start(bf16[1,2,2,128,128]{4,3,2,1,0:T(8,128)(2,1)S(1)} %get-tuple-element.15.refs_0_.near0), channel_id=1, source_target_pairs={{0,2},{1,3},{2,0},{3,1},{4,6},{5,7},{6,4},{7,5},{8,10},{9,11},{10,... | collective-permute-start | bytes 393224 | tf_op jit(solution)/shard_map/ppermute | solution.py:310
  5.7 7.8 %collective-permute-start.1 = (bf16[1,2,2,128,128]{4,3,2,1,0:T(8,128)(2,1)S(1)}, bf16[1,2,2,128,128]{4,3,2,1,0:T(8,128)(2,1)S(1)}, u32[]{:S(2)}, u32[]{:S(2)}) collective-permute-start(bf16[1,2,2,128,128]{4,3,2,1,0:T(8,128)(2,1)S(1)} %get-tuple-element.16.far0.refs_0_), channel_id=1, source_target_pairs={{0,2},{1,3},{2,0},{3,1},{4,6},{5,7},{6,4},{7,5},{8,10},{9,11},{10,... | collective-permute-start | bytes 393224 | tf_op jit(solution)/shard_map/ppermute | solution.py:310
  6.3 8.5 %collective-permute-start.5 = (bf16[2,1,128,128]{3,2,1,0:T(8,128)(2,1)S(1)}, bf16[2,1,128,128]{3,2,1,0:T(8,128)(2,1)S(1)}, u32[]{:S(2)}, u32[]{:S(2)}) collective-permute-start(bf16[2,1,128,128]{3,2,1,0:T(8,128)(2,1)S(1)} %get-tuple-element.17), channel_id=1, source_target_pairs={{0,4},{4,8},{8,12},{12,16},{16,20},{20,24},{24,28},{28,0},{1,5},{5... | collective-permute-start | bytes 196616 | tf_op jit(solution)/shard_map/ppermute | solution.py:324
  8.4 6.4 %collective-permute-start.6 = (bf16[2,1,128,128]{3,2,1,0:T(8,128)(2,1)S(1)}, bf16[2,1,128,128]{3,2,1,0:T(8,128)(2,1)S(1)}, u32[]{:S(2)}, u32[]{:S(2)}) collective-permute-start(bf16[2,1,128,128]{3,2,1,0:T(8,128)(2,1)S(1)} %get-tuple-element.18), channel_id=1, source_target_pairs={{4,0},{8,4},{12,8},{16,12},{20,16},{24,20},{28,24},{0,28},{5,1},{9... | collective-permute-start | bytes 196616 | tf_op jit(solution)/shard_map/ppermute | solution.py:325
  11.5 2.3 %collective-permute-start.8 = (bf16[1,2,2,128,128]{4,3,2,1,0:T(8,128)(2,1)S(1)}, bf16[1,2,2,128,128]{4,3,2,1,0:T(8,128)(2,1)S(1)}, u32[]{:S(2)}, u32[]{:S(2)}) collective-permute-start(bf16[1,2,2,128,128]{4,3,2,1,0:T(8,128)(2,1)S(1)} %collective-permute-done.7.refs_2_), channel_id=1, source_target_pairs={{0,1},{1,0},{2,3},{3,2},{4,5},{5,4},{6,7},{7,6},{8,9},{9,8},{10,11... | collective-permute-start | bytes 393224 | tf_op jit(solution)/shard_map/ppermute | solution.py:310
  11.5 2.3 %copy-start = (s32[64]{0:T(128)S(1)}, s32[64]{0:T(128)}, u32[]{:S(2)}) copy-start(s32[64]{0:T(128)} %colour.3) | copy-start | bytes 772
  11.6 6.7 %collective-permute-start.11 = (f16[2,2,128,128]{3,2,1,0:T(8,128)(2,1)S(1)}, f16[2,2,128,128]{3,2,1,0:T(8,128)(2,1)S(1)}, u32[]{:S(2)}, u32[]{:S(2)}) collective-permute-start(f16[2,2,128,128]{3,2,1,0:T(8,128)(2,1)S(1)} %get-tuple-element.23), channel_id=1, source_target_pairs={{0,2},{1,3},{2,0},{3,1},{4,6},{5,7},{6,4},{7,5},{8,10},{9,11},{10,... | collective-permute-start | bytes 393224 | tf_op jit(solution)/shard_map/ppermute | solution.py:310
  13.5 3.2 %collective-permute-start.2 = (bf16[1,2,2,128,128]{4,3,2,1,0:T(8,128)(2,1)S(1)}, bf16[1,2,2,128,128]{4,3,2,1,0:T(8,128)(2,1)S(1)}, u32[]{:S(2)}, u32[]{:S(2)}) collective-permute-start(bf16[1,2,2,128,128]{4,3,2,1,0:T(8,128)(2,1)S(1)} %collective-permute-done.1.refs_2_), channel_id=1, source_target_pairs={{0,1},{1,0},{2,3},{3,2},{4,5},{5,4},{6,7},{7,6},{8,9},{9,8},{10,11... | collective-permute-start | bytes 393224 | tf_op jit(solution)/shard_map/ppermute | solution.py:310
  15.0 6.6 %collective-permute-start.9 = (f16[4,128,128]{2,1,0:T(8,128)(2,1)S(1)}, f16[4,128,128]{2,1,0:T(8,128)(2,1)S(1)}, u32[]{:S(2)}, u32[]{:S(2)}) collective-permute-start(f16[4,128,128]{2,1,0:T(8,128)(2,1)S(1)} %pad_maximum_fusion.1), channel_id=1, source_target_pairs={{0,2},{1,3},{2,0},{3,1},{4,6},{5,7},{6,4},{7,5},{8,10},{9,11},{10,... | collective-permute-start | bytes 393224 | tf_op jit(solution)/shard_map/ppermute | solution.py:310
  15.7 5.8 %collective-permute-start.10 = (f16[2,128,128]{2,1,0:T(8,128)(2,1)S(1)}, f16[2,128,128]{2,1,0:T(8,128)(2,1)S(1)}, u32[]{:S(2)}, u32[]{:S(2)}) collective-permute-start(f16[2,128,128]{2,1,0:T(8,128)(2,1)S(1)} %get-tuple-element.29), channel_id=1, source_target_pairs={{0,3},{1,2},{2,1},{3,0},{4,7},{5,6},{6,5},{7,4},{8,11},{9,10},{10,... | collective-permute-start | bytes 196616 | tf_op jit(solution)/shard_map/ppermute | solution.py:310
  17.7 3.8 %collective-permute-start.3 = (f16[2,128,128]{2,1,0:T(8,128)(2,1)S(1)}, f16[2,128,128]{2,1,0:T(8,128)(2,1)S(1)}, u32[]{:S(2)}, u32[]{:S(2)}) collective-permute-start(f16[2,128,128]{2,1,0:T(8,128)(2,1)S(1)} %fusion.1), channel_id=1, source_target_pairs={{0,1},{1,0},{2,3},{3,2},{4,5},{5,4},{6,7},{7,6},{8,9},{9,8},{10,11... | collective-permute-start | bytes 196616 | tf_op jit(solution)/shard_map/ppermute | solution.py:310
  18.4 3.2 %collective-permute-start.12 = (f16[4,2,128,128]{3,2,1,0:T(8,128)(2,1)S(1)}, f16[4,2,128,128]{3,2,1,0:T(8,128)(2,1)S(1)}, u32[]{:S(2)}, u32[]{:S(2)}) collective-permute-start(f16[4,2,128,128]{3,2,1,0:T(8,128)(2,1)S(1)} %pad_maximum_fusion), channel_id=1, source_target_pairs={{0,1},{1,0},{2,3},{3,2},{4,5},{5,4},{6,7},{7,6},{8,9},{9,8},{10,11... | collective-permute-start | bytes 786440 | tf_op jit(solution)/shard_map/ppermute | solution.py:310

commit v4 on v3

--- a/solution.py
+++ b/solution.py
@@ -44,7 +44,7 @@
     return jax.ShapeDtypeStruct(shape, dtype)
 
 
-def call(kernel, name, ins, outs, scratch, args, extra=2):
+def call(kernel, name, ins, outs, scratch, args, extra=2, cost=1000, out_space=VMEM):
     held = [*outs, *(s for s in scratch if isinstance(s, jax.ShapeDtypeStruct))]
     held += [a for spec, a in zip(ins, args) if spec is VMEM]
     total = sum(math.prod(s.shape) * jnp.dtype(s.dtype).itemsize for s in held)
@@ -52,13 +52,13 @@
         kernel,
         out_shape=tuple(outs),
         in_specs=ins,
-        out_specs=(VMEM,) * len(outs),
+        out_specs=(out_space,) * len(outs),
         scratch_shapes=[
             pltpu.VMEM(s.shape, s.dtype) if isinstance(s, jax.ShapeDtypeStruct) else s
             for s in scratch
         ],
         compiler_params=pltpu.CompilerParams(vmem_limit_bytes=total + (extra << 20)),
-        cost_estimate=pl.CostEstimate(flops=1000, bytes_accessed=1000, transcendentals=0),
+        cost_estimate=pl.CostEstimate(flops=cost, bytes_accessed=1000, transcendentals=0),
         name=name,
     )(*args)
 
@@ -107,7 +107,7 @@
         for k0 in range(0, slots, CHUNK):
             copies.pop(0).wait()
 
-            @pl.loop(k0, min(k0 + CHUNK, slots))
+            @pl.loop(k0, min(k0 + CHUNK, slots), unroll=9)
             def _(k):
                 entry = jnp.where(pattern[block, k] == 1, neighbours[block, k], own + 2 * width)
                 sums[row, entry] += blocks[row, k].astype(jnp.float32)
@@ -183,6 +183,7 @@
         [out, out],
         [],
         [sends, near0, far0, near1, far1],
+        cost=1000,
     )
 
 
@@ -203,7 +204,9 @@
 def split_sums(own, sums):
     rows, _, orbits, _ = sums.shape
     left = like((2 * rows * orbits, own * orbits), jnp.bfloat16)
-    return call(functools.partial(split_kernel, own), "split_sums", [VMEM], [left], [], [sums])[0]
+    return call(
+        functools.partial(split_kernel, own), "split_sums", [VMEM], [left], [], [sums], cost=1000
+    )[0]
 
 
 def image_kernel(coeffs, upper_half, own, colour, left, *refs):
@@ -250,51 +253,65 @@
         [],
         [colour, left, *pieces],
         4,
+        1000,
     )[0]
 
 
 def final_kernel(scale, count, mine, *refs):
     images, refs = refs[: count - 1], refs[count - 1 :]
     blocks, refs = refs[:count], refs[count:]
-    firsts, out = refs[:-1], refs[-1]
+    firsts, (out, value, sems) = refs[:-3], refs[-3:]
     shade = lax.axis_index("col")
     rows, wide, orbits, _ = blocks[0].shape
     width = wide // 2
     right = []
     for e in range(wide):
         side, i = divmod(e, width)
-        value = firsts[side][0, i].astype(jnp.float32)
+        first = firsts[side][0, i].astype(jnp.float32)
         for other in firsts[2:]:
-            value += other[side, i].astype(jnp.float32)
-        right.append(value.astype(jnp.bfloat16))
+            first += other[1 - side, i].astype(jnp.float32)
+        right.append(first.astype(jnp.bfloat16))
     right = jnp.concatenate(right + right, axis=0)
+    copies = []
     for relative in range(count):
-        for row in range(rows):
-            left = jnp.concatenate([blocks[relative][row, e] for e in range(wide)], axis=1)
-            high = left.astype(jnp.bfloat16)
-            low = (left - high.astype(jnp.float32)).astype(jnp.bfloat16)
-            extra = jnp.dot(
-                jnp.concatenate([high, low], axis=1), right, preferred_element_type=jnp.float32
-            )
-            if relative == 0:
-                value = mine[0, row]
-            else:
-                value = images[relative - 1][row] * (1.0 / WIRE_SCALE)
-            at = (shade ^ relative) * rows + row
-            out[pl.ds(pl.multiple_of(at * orbits, orbits), orbits), :] = value + scale * extra
+        left = [
+            jnp.concatenate([blocks[relative][row, e] for row in range(rows)], axis=0)
+            for e in range(wide)
+        ]
+        left = jnp.concatenate(left, axis=1)
+        high = left.astype(jnp.bfloat16)
+        low = (left - high.astype(jnp.float32)).astype(jnp.bfloat16)
+        extra = jnp.dot(
+            jnp.concatenate([high, low], axis=1), right, preferred_element_type=jnp.float32
+        )
+        if relative == 0:
+            image = mine[0]
+        else:
+            image = images[relative - 1][...] * (1.0 / WIRE_SCALE)
+        value[relative] = image.reshape(rows * orbits, orbits) + scale * extra
+        at = pl.multiple_of((shade ^ relative) * (rows * orbits), rows * orbits)
+        copy = pltpu.make_async_copy(
+            value.at[relative], out.at[pl.ds(at, rows * orbits)], sems.at[relative]
+        )
+        copy.start()
+        copies.append(copy)
+    for copy in copies:
+        copy.wait()
 
 
 def final_images(scale, mine, images, blocks, firsts):
     count = len(blocks)
     rows, _, orbits, _ = blocks[0].shape
+    size = rows * orbits
     return call(
         functools.partial(final_kernel, scale, count),
         "final_images",
         [VMEM] * (1 + len(images) + len(blocks) + len(firsts)),
-        [like((count * rows * orbits, orbits), jnp.float32)],
-        [],
+        [like((count * size, orbits), jnp.float32)],
+        [like((count, size, orbits), jnp.float32), pltpu.SemaphoreType.DMA((count,))],
         [mine, *images, *blocks, *firsts],
         4,
+        out_space=HBM,
     )[0]
 
 
@@ -311,20 +328,21 @@
 
     near, far, sums = first_terms(ndomain, ncolour, neighbours, pattern, colour, sends, margin)
     border = sums[:, own : own + 2 * width]
-    left = split_sums(own, sums)
     wire = border.astype(WIRE)
-    nears, fars, wires = {0: near}, {0: far}, [wire]
-    for s in range(1, pairs):
-        nears[2 * s] = across(near, 2 * s)
-        fars[2 * s] = across(far, 2 * s)
+    nears, fars, wires = {0: near}, {0: far}, {0: wire}
     nears[1] = across(near, 1)
     fars[1] = across(far, 1)
+    near_out, far_out = near, far
+    for s in range(1, pairs):
+        nears[2 * s] = across(near_out, 2 * s)
+        fars[2 * s] = across(far_out, 2 * s)
     up, down = borders(sends, near, far, nears[1], fars[1])
     onward = [(i, (i + 1) % ndomain) for i in range(ndomain)]
     before = lax.ppermute(up, "dom", onward)
     after = lax.ppermute(down, "dom", [(j, i) for i, j in onward])
     for s in range(1, pairs):
-        wires.append(across(wire, 2 * s))
+        wires[2 * s] = across(wire, 2 * s)
+    left = split_sums(own, sums)
     for s in range(1, pairs):
         nears[2 * s], _, _ = lax.optimization_barrier((nears[2 * s], up, down))
         nears[2 * s + 1] = across(nears[2 * s], 1)
@@ -340,12 +358,10 @@
 
     outer = image_terms(coeffs, True, own, colour, left, pieces(True))
     before, after, outer = lax.optimization_barrier((before, after, outer))
-    others = across(jnp.concatenate(wires), 1)
-    blocks = []
+    others = across(jnp.concatenate([wires[2 * s] for s in range(pairs)]), 1)
     for s in range(pairs):
-        for side in (wires[s], others[s * rows : (s + 1) * rows]):
-            blocks.append(side.astype(jnp.float32))
-    blocks[0] = border
+        wires[2 * s + 1] = others[s * rows : (s + 1) * rows]
+    blocks = [border] + [wires[m].astype(jnp.float32) for m in range(1, ncolour)]
     images = {}
     sent = (outer * WIRE_SCALE).astype(WIRE)
     for m in range(pairs, ncolour):
@@ -359,7 +375,7 @@
         if m % 2:
             images[m] = across(images[m], m)
         else:
-            second = jnp.stack([before[m // 2], after[m // 2]]).astype(WIRE)
+            second = jnp.stack([after[m // 2], before[m // 2]]).astype(WIRE)
             sent = jnp.concatenate([images[m], second.reshape((-1,) + images[m].shape[1:])])
             sent = across(sent, m)
             images[m], second = sent[:rows], sent[rows:]

time: 23 us -> 22.6 us (0.983)
  Pallas kernels: 6.24 us -> 5.79 us
    pallas_call x6, Pallas kernels: 6.24 us -> 5.79 us  [call(): pl.pallas_call(kernel, out_shape=tuple(outs), in_specs=ins, out_specs=(ou...]
where the time goes in v4:
time: 22.6 us; the launch traced here: 22.4 us
  starting transfers between devices  13 us (58%)
  Pallas kernels  5.79 us (26%)
  waiting for transfers between devices  3.07 us (14%)
  other arithmetic  0.32 us (1%)
    ppermute x11, starting transfers between devices, across(): return lax.ppermute(value, 'col', [(i, i ^ step) for i in range(ncolour)])  7.85 us
    pallas_call x6, Pallas kernels, call(): pl.pallas_call(kernel, out_shape=tuple(outs), in_specs=ins, out_specs=(ou...  5.79 us
    ppermute x1, starting transfers between devices, per_device(): after = lax.ppermute(down, 'dom', [(j, i) for i, j in onward])  3.11 us
    ppermute x11, waiting for transfers between devices, across(): return lax.ppermute(value, 'col', [(i, i ^ step) for i in range(ncolour)])  3.06 us
    ppermute x1, starting transfers between devices, per_device(): before = lax.ppermute(up, 'dom', onward)  2.07 us
  transfers between devices with their start and end apart: 13, of which 1 were waited for; matrix products, arithmetic and copies ran while one was open for 1% of the time, Pallas kernels for 13%

profile of v4, /device:TPU:0, one launch (start us, length us, event | category | flops | bytes accessed | tf_op | source)
XLA Modules:
  0.0 22.4 jit_solution(10031328149959167270)
XLA Ops:
  0.0 1.8 %first_terms.1 = (bf16[1,2,2,128,128]{4,3,2,1,0:T(8,128)(2,1)S(1)}, bf16[1,2,2,128,128]{4,3,2,1,0:T(8,128)(2,1)S(1)}, f32[2,11,128,128]{3,2,1,0:T(8,128)S(1)}) custom-call(s32[8,27]{1,0:T(8,128)} %refs_0_.1, s32[8,27]{1,0:T(8,128)} %refs_1_.1, s32[64]{0:T(128)} %colour.3, s32[2,1,8]{2,1,0:T(1,128)} %bitcast.13, bf16[2,27,128,128]{3,2,1,0:T(8,128)(2,1)} %refs_4_.1), custom_call_target="tpu_custom_call" | custom-call | flops 1000 | bytes 1000 | tf_op jit(solution)/shard_map/first_terms/pallas_call | solution.py:51
  1.8 0.5 %collective-permute-start = (bf16[1,2,2,128,128]{4,3,2,1,0:T(8,128)(2,1)S(1)}, bf16[1,2,2,128,128]{4,3,2,1,0:T(8,128)(2,1)S(1)}, u32[]{:S(2)}, u32[]{:S(2)}) collective-permute-start(bf16[1,2,2,128,128]{4,3,2,1,0:T(8,128)(2,1)S(1)} %get-tuple-element.15.refs_0_.near0), channel_id=1, source_target_pairs={{0,1},{1,0},{2,3},{3,2},{4,5},{5,4},{6,7},{7,6},{8,9},{9,8},{10,11... | collective-permute-start | bytes 393224 | tf_op jit(solution)/shard_map/ppermute | solution.py:327
  2.3 0.1 collective-permute-start.4
  2.4 2.9 %collective-permute-start.7 = (bf16[1,2,2,128,128]{4,3,2,1,0:T(8,128)(2,1)S(1)}, bf16[1,2,2,128,128]{4,3,2,1,0:T(8,128)(2,1)S(1)}, u32[]{:S(2)}, u32[]{:S(2)}) collective-permute-start(bf16[1,2,2,128,128]{4,3,2,1,0:T(8,128)(2,1)S(1)} %get-tuple-element.15.refs_0_.near0), channel_id=1, source_target_pairs={{0,2},{1,3},{2,0},{3,1},{4,6},{5,7},{6,4},{7,5},{8,10},{9,11},{10,... | collective-permute-start | bytes 393224 | tf_op jit(solution)/shard_map/ppermute | solution.py:327
  5.3 0.0 collective-permute-start.1
  5.3 0.0 collective-permute-done.refs_1_.near1
  5.3 0.0 collective-permute-done.4.far1.refs_1_
  5.3 0.6 %borders.1 = (bf16[2,1,128,128]{3,2,1,0:T(8,128)(2,1)S(1)}, bf16[2,1,128,128]{3,2,1,0:T(8,128)(2,1)S(1)}) custom-call(s32[2,1,8]{2,1,0:T(1,128)S(1)} %bitcast.14, bf16[1,2,2,128,128]{4,3,2,1,0:T(8,128)(2,1)S(1)} %get-tuple-element.15.refs_0_.near0, bf16[1,2,2,128,128]{4,3,2,1,0:T(8,128)(2,1)S(1)} %get-tuple-element.16.far0.refs_0_, ...), custom_call_target="tpu_custom_call" | custom-call | flops 1000 | bytes 1000 | tf_op jit(solution)/shard_map/borders/pallas_call | solution.py:51
  6.0 2.1 %collective-permute-start.5 = (bf16[2,1,128,128]{3,2,1,0:T(8,128)(2,1)S(1)}, bf16[2,1,128,128]{3,2,1,0:T(8,128)(2,1)S(1)}, u32[]{:S(2)}, u32[]{:S(2)}) collective-permute-start(bf16[2,1,128,128]{3,2,1,0:T(8,128)(2,1)S(1)} %get-tuple-element.17), channel_id=1, source_target_pairs={{0,4},{4,8},{8,12},{12,16},{16,20},{20,24},{24,28},{28,0},{1,5},{5... | collective-permute-start | bytes 196616 | tf_op jit(solution)/shard_map/ppermute | solution.py:341
  8.0 3.1 %collective-permute-start.6 = (bf16[2,1,128,128]{3,2,1,0:T(8,128)(2,1)S(1)}, bf16[2,1,128,128]{3,2,1,0:T(8,128)(2,1)S(1)}, u32[]{:S(2)}, u32[]{:S(2)}) collective-permute-start(bf16[2,1,128,128]{3,2,1,0:T(8,128)(2,1)S(1)} %get-tuple-element.18), channel_id=1, source_target_pairs={{4,0},{8,4},{12,8},{16,12},{20,16},{24,20},{28,24},{0,28},{5,1},{9... | collective-permute-start | bytes 196616 | tf_op jit(solution)/shard_map/ppermute | solution.py:342
  11.2 1.7 %collective-permute-start.11 = (f16[2,2,128,128]{3,2,1,0:T(8,128)(2,1)S(1)}, f16[2,2,128,128]{3,2,1,0:T(8,128)(2,1)S(1)}, u32[]{:S(2)}, u32[]{:S(2)}) collective-permute-start(f16[2,2,128,128]{3,2,1,0:T(8,128)(2,1)S(1)} %get-tuple-element.23), channel_id=1, source_target_pairs={{0,2},{1,3},{2,0},{3,1},{4,6},{5,7},{6,4},{7,5},{8,10},{9,11},{10,... | collective-permute-start | bytes 393224 | tf_op jit(solution)/shard_map/ppermute | solution.py:327
  12.9 0.3 %split_sums.1.left = bf16[512,1024]{1,0:T(8,128)(2,1)S(1)} custom-call(f32[2,11,128,128]{3,2,1,0:T(8,128)S(1)} %get-tuple-element.14.sums), custom_call_target="tpu_custom_call" | custom-call | flops 1000 | bytes 1000 | tf_op jit(solution)/shard_map/split_sums/pallas_call | solution.py:51
  13.2 0.3 %collective-permute-start.2 = (bf16[1,2,2,128,128]{4,3,2,1,0:T(8,128)(2,1)S(1)}, bf16[1,2,2,128,128]{4,3,2,1,0:T(8,128)(2,1)S(1)}, u32[]{:S(2)}, u32[]{:S(2)}) collective-permute-start(bf16[1,2,2,128,128]{4,3,2,1,0:T(8,128)(2,1)S(1)} %collective-permute-done.1.refs_2_), channel_id=1, source_target_pairs={{0,1},{1,0},{2,3},{3,2},{4,5},{5,4},{6,7},{7,6},{8,9},{9,8},{10,11... | collective-permute-start | bytes 393224 | tf_op jit(solution)/shard_map/ppermute | solution.py:327
  13.4 0.0 collective-permute-done.8.refs_3_
  13.4 1.0 %image_terms.3 = f32[2,2,128,128]{3,2,1,0:T(8,128)S(1)} custom-call(s32[64]{0:T(128)S(1)} %copy-done, bf16[512,1024]{1,0:T(8,128)(2,1)S(1)} %split_sums.1.left, bf16[1,2,2,128,128]{4,3,2,1,0:T(8,128)(2,1)S(1)} %get-tuple-element.16.far0.refs_0_, bf16[1,2,2,128,128]{4,3,2,1,0:T(8,128)(2,1)S(1)} %collective-permute-done.4.far1.refs_1_, ...), custom_call_target="tpu_custom_call" | custom-call | flops 1000 | bytes 1000 | tf_op jit(solution)/shard_map/image_terms/pallas_call | solution.py:51
  14.5 0.0 collective-permute-done.6.refs_8_
  14.6 0.7 %collective-permute-start.9 = (f16[4,128,128]{2,1,0:T(8,128)(2,1)S(1)}, f16[4,128,128]{2,1,0:T(8,128)(2,1)S(1)}, u32[]{:S(2)}, u32[]{:S(2)}) collective-permute-start(f16[4,128,128]{2,1,0:T(8,128)(2,1)S(1)} %pad_maximum_fusion.1), channel_id=1, source_target_pairs={{0,2},{1,3},{2,0},{3,1},{4,6},{5,7},{6,4},{7,5},{8,10},{9,11},{10,... | collective-permute-start | bytes 393224 | tf_op jit(solution)/shard_map/ppermute | solution.py:327
  15.3 1.0 %collective-permute-start.10 = (f16[2,128,128]{2,1,0:T(8,128)(2,1)S(1)}, f16[2,128,128]{2,1,0:T(8,128)(2,1)S(1)}, u32[]{:S(2)}, u32[]{:S(2)}) collective-permute-start(f16[2,128,128]{2,1,0:T(8,128)(2,1)S(1)} %get-tuple-element.29), channel_id=1, source_target_pairs={{0,3},{1,2},{2,1},{3,0},{4,7},{5,6},{6,5},{7,4},{8,11},{9,10},{10,... | collective-permute-start | bytes 196616 | tf_op jit(solution)/shard_map/ppermute | solution.py:327
  16.3 1.0 %image_terms.2.mine = f32[2,2,128,128]{3,2,1,0:T(8,128)S(1)} custom-call(s32[64]{0:T(128)S(1)} %copy-done, bf16[512,1024]{1,0:T(8,128)(2,1)S(1)} %split_sums.1.left, bf16[1,2,2,128,128]{4,3,2,1,0:T(8,128)(2,1)S(1)} %get-tuple-element.15.refs_0_.near0, bf16[1,2,2,128,128]{4,3,2,1,0:T(8,128)(2,1)S(1)} %collective-permute-done.refs_1_.near1, ...), custom_call_target="tpu_custom_call" | custom-call | flops 1000 | bytes 1000 | tf_op jit(solution)/shard_map/image_terms/pallas_call | solution.py:51
  17.4 0.6 %collective-permute-start.3 = (f16[2,128,128]{2,1,0:T(8,128)(2,1)S(1)}, f16[2,128,128]{2,1,0:T(8,128)(2,1)S(1)}, u32[]{:S(2)}, u32[]{:S(2)}) collective-permute-start(f16[2,128,128]{2,1,0:T(8,128)(2,1)S(1)} %fusion.1), channel_id=1, source_target_pairs={{0,1},{1,0},{2,3},{3,2},{4,5},{5,4},{6,7},{7,6},{8,9},{9,8},{10,11... | collective-permute-start | bytes 196616 | tf_op jit(solution)/shard_map/ppermute | solution.py:327
  17.9 0.1 pad_maximum_fusion
  18.0 0.1 collective-permute-start.12
  18.1 3.0 %collective-permute-done.10 = f16[2,128,128]{2,1,0:T(8,128)(2,1)S(1)} collective-permute-done((f16[2,128,128]{2,1,0:T(8,128)(2,1)S(1)}, f16[2,128,128]{2,1,0:T(8,128)(2,1)S(1)}, u32[]{:S(2)}, u32[]{:S(2)}) %collective-permute-start.10) | collective-permute-done | bytes 65568 | tf_op jit(solution)/shard_map/ppermute | solution.py:327
  21.3 1.1 %final_images.1 = f32[1024,128]{1,0:T(8,128)} custom-call(f32[2,2,128,128]{3,2,1,0:T(8,128)S(1)} %image_terms.2.mine, f32[2,128,128]{2,1,0:T(8,128)S(1)} %convert_element_type.39.refs_0_, f32[2,128,128]{2,1,0:T(8,128)S(1)} %get-tuple-element.28.refs_1_, f32[2,128,128]{2,1,0:T(8,128)S(1)} %convert_element_type.43.refs_2_, ...), custom_call_target="tpu_custom_call" | custom-call | flops 1000 | bytes 1000 | tf_op jit(solution)/shard_map/final_images/pallas_call | solution.py:51
  (25 shorter events, 0.3 us)
Async XLA Ops:
  0.0 5.3 %copy-start.1 = (s32[8,2,1]{0,2,1:T(1,128)S(1)}, s32[8,2,1]{0,2,1:T(1,128)}, u32[]{:S(2)}) copy-start(s32[8,2,1]{0,2,1:T(1,128)} %param.9) | copy-start | bytes 196
  1.8 3.5 %collective-permute-start = (bf16[1,2,2,128,128]{4,3,2,1,0:T(8,128)(2,1)S(1)}, bf16[1,2,2,128,128]{4,3,2,1,0:T(8,128)(2,1)S(1)}, u32[]{:S(2)}, u32[]{:S(2)}) collective-permute-start(bf16[1,2,2,128,128]{4,3,2,1,0:T(8,128)(2,1)S(1)} %get-tuple-element.15.refs_0_.near0), channel_id=1, source_target_pairs={{0,1},{1,0},{2,3},{3,2},{4,5},{5,4},{6,7},{7,6},{8,9},{9,8},{10,11... | collective-permute-start | bytes 393224 | tf_op jit(solution)/shard_map/ppermute | solution.py:327
  2.3 3.0 %collective-permute-start.4 = (bf16[1,2,2,128,128]{4,3,2,1,0:T(8,128)(2,1)S(1)}, bf16[1,2,2,128,128]{4,3,2,1,0:T(8,128)(2,1)S(1)}, u32[]{:S(2)}, u32[]{:S(2)}) collective-permute-start(bf16[1,2,2,128,128]{4,3,2,1,0:T(8,128)(2,1)S(1)} %get-tuple-element.16.far0.refs_0_), channel_id=1, source_target_pairs={{0,1},{1,0},{2,3},{3,2},{4,5},{5,4},{6,7},{7,6},{8,9},{9,8},{10,11... | collective-permute-start | bytes 393224 | tf_op jit(solution)/shard_map/ppermute | solution.py:327
  2.4 8.8 %collective-permute-start.7 = (bf16[1,2,2,128,128]{4,3,2,1,0:T(8,128)(2,1)S(1)}, bf16[1,2,2,128,128]{4,3,2,1,0:T(8,128)(2,1)S(1)}, u32[]{:S(2)}, u32[]{:S(2)}) collective-permute-start(bf16[1,2,2,128,128]{4,3,2,1,0:T(8,128)(2,1)S(1)} %get-tuple-element.15.refs_0_.near0), channel_id=1, source_target_pairs={{0,2},{1,3},{2,0},{3,1},{4,6},{5,7},{6,4},{7,5},{8,10},{9,11},{10,... | collective-permute-start | bytes 393224 | tf_op jit(solution)/shard_map/ppermute | solution.py:327
  5.3 7.8 %collective-permute-start.1 = (bf16[1,2,2,128,128]{4,3,2,1,0:T(8,128)(2,1)S(1)}, bf16[1,2,2,128,128]{4,3,2,1,0:T(8,128)(2,1)S(1)}, u32[]{:S(2)}, u32[]{:S(2)}) collective-permute-start(bf16[1,2,2,128,128]{4,3,2,1,0:T(8,128)(2,1)S(1)} %get-tuple-element.16.far0.refs_0_), channel_id=1, source_target_pairs={{0,2},{1,3},{2,0},{3,1},{4,6},{5,7},{6,4},{7,5},{8,10},{9,11},{10,... | collective-permute-start | bytes 393224 | tf_op jit(solution)/shard_map/ppermute | solution.py:327
  6.0 8.5 %collective-permute-start.5 = (bf16[2,1,128,128]{3,2,1,0:T(8,128)(2,1)S(1)}, bf16[2,1,128,128]{3,2,1,0:T(8,128)(2,1)S(1)}, u32[]{:S(2)}, u32[]{:S(2)}) collective-permute-start(bf16[2,1,128,128]{3,2,1,0:T(8,128)(2,1)S(1)} %get-tuple-element.17), channel_id=1, source_target_pairs={{0,4},{4,8},{8,12},{12,16},{16,20},{20,24},{24,28},{28,0},{1,5},{5... | collective-permute-start | bytes 196616 | tf_op jit(solution)/shard_map/ppermute | solution.py:341
  8.0 6.4 %collective-permute-start.6 = (bf16[2,1,128,128]{3,2,1,0:T(8,128)(2,1)S(1)}, bf16[2,1,128,128]{3,2,1,0:T(8,128)(2,1)S(1)}, u32[]{:S(2)}, u32[]{:S(2)}) collective-permute-start(bf16[2,1,128,128]{3,2,1,0:T(8,128)(2,1)S(1)} %get-tuple-element.18), channel_id=1, source_target_pairs={{4,0},{8,4},{12,8},{16,12},{20,16},{24,20},{28,24},{0,28},{5,1},{9... | collective-permute-start | bytes 196616 | tf_op jit(solution)/shard_map/ppermute | solution.py:342
  11.2 2.3 %collective-permute-start.8 = (bf16[1,2,2,128,128]{4,3,2,1,0:T(8,128)(2,1)S(1)}, bf16[1,2,2,128,128]{4,3,2,1,0:T(8,128)(2,1)S(1)}, u32[]{:S(2)}, u32[]{:S(2)}) collective-permute-start(bf16[1,2,2,128,128]{4,3,2,1,0:T(8,128)(2,1)S(1)} %collective-permute-done.7.refs_2_), channel_id=1, source_target_pairs={{0,1},{1,0},{2,3},{3,2},{4,5},{5,4},{6,7},{7,6},{8,9},{9,8},{10,11... | collective-permute-start | bytes 393224 | tf_op jit(solution)/shard_map/ppermute | solution.py:327
  11.2 2.3 %copy-start = (s32[64]{0:T(128)S(1)}, s32[64]{0:T(128)}, u32[]{:S(2)}) copy-start(s32[64]{0:T(128)} %colour.3) | copy-start | bytes 772
  11.2 6.7 %collective-permute-start.11 = (f16[2,2,128,128]{3,2,1,0:T(8,128)(2,1)S(1)}, f16[2,2,128,128]{3,2,1,0:T(8,128)(2,1)S(1)}, u32[]{:S(2)}, u32[]{:S(2)}) collective-permute-start(f16[2,2,128,128]{3,2,1,0:T(8,128)(2,1)S(1)} %get-tuple-element.23), channel_id=1, source_target_pairs={{0,2},{1,3},{2,0},{3,1},{4,6},{5,7},{6,4},{7,5},{8,10},{9,11},{10,... | collective-permute-start | bytes 393224 | tf_op jit(solution)/shard_map/ppermute | solution.py:327
  13.2 3.2 %collective-permute-start.2 = (bf16[1,2,2,128,128]{4,3,2,1,0:T(8,128)(2,1)S(1)}, bf16[1,2,2,128,128]{4,3,2,1,0:T(8,128)(2,1)S(1)}, u32[]{:S(2)}, u32[]{:S(2)}) collective-permute-start(bf16[1,2,2,128,128]{4,3,2,1,0:T(8,128)(2,1)S(1)} %collective-permute-done.1.refs_2_), channel_id=1, source_target_pairs={{0,1},{1,0},{2,3},{3,2},{4,5},{5,4},{6,7},{7,6},{8,9},{9,8},{10,11... | collective-permute-start | bytes 393224 | tf_op jit(solution)/shard_map/ppermute | solution.py:327
  14.6 6.6 %collective-permute-start.9 = (f16[4,128,128]{2,1,0:T(8,128)(2,1)S(1)}, f16[4,128,128]{2,1,0:T(8,128)(2,1)S(1)}, u32[]{:S(2)}, u32[]{:S(2)}) collective-permute-start(f16[4,128,128]{2,1,0:T(8,128)(2,1)S(1)} %pad_maximum_fusion.1), channel_id=1, source_target_pairs={{0,2},{1,3},{2,0},{3,1},{4,6},{5,7},{6,4},{7,5},{8,10},{9,11},{10,... | collective-permute-start | bytes 393224 | tf_op jit(solution)/shard_map/ppermute | solution.py:327
  15.3 5.8 %collective-permute-start.10 = (f16[2,128,128]{2,1,0:T(8,128)(2,1)S(1)}, f16[2,128,128]{2,1,0:T(8,128)(2,1)S(1)}, u32[]{:S(2)}, u32[]{:S(2)}) collective-permute-start(f16[2,128,128]{2,1,0:T(8,128)(2,1)S(1)} %get-tuple-element.29), channel_id=1, source_target_pairs={{0,3},{1,2},{2,1},{3,0},{4,7},{5,6},{6,5},{7,4},{8,11},{9,10},{10,... | collective-permute-start | bytes 196616 | tf_op jit(solution)/shard_map/ppermute | solution.py:327
  17.4 3.8 %collective-permute-start.3 = (f16[2,128,128]{2,1,0:T(8,128)(2,1)S(1)}, f16[2,128,128]{2,1,0:T(8,128)(2,1)S(1)}, u32[]{:S(2)}, u32[]{:S(2)}) collective-permute-start(f16[2,128,128]{2,1,0:T(8,128)(2,1)S(1)} %fusion.1), channel_id=1, source_target_pairs={{0,1},{1,0},{2,3},{3,2},{4,5},{5,4},{6,7},{7,6},{8,9},{9,8},{10,11... | collective-permute-start | bytes 196616 | tf_op jit(solution)/shard_map/ppermute | solution.py:327
  18.0 3.2 %collective-permute-start.12 = (f16[4,2,128,128]{3,2,1,0:T(8,128)(2,1)S(1)}, f16[4,2,128,128]{3,2,1,0:T(8,128)(2,1)S(1)}, u32[]{:S(2)}, u32[]{:S(2)}) collective-permute-start(f16[4,2,128,128]{3,2,1,0:T(8,128)(2,1)S(1)} %pad_maximum_fusion), channel_id=1, source_target_pairs={{0,1},{1,0},{2,3},{3,2},{4,5},{5,4},{6,7},{7,6},{8,9},{9,8},{10,11... | collective-permute-start | bytes 786440 | tf_op jit(solution)/shard_map/ppermute | solution.py:327

commit v5 on v4

--- a/solution.py
+++ b/solution.py
@@ -112,7 +112,7 @@
                 entry = jnp.where(pattern[block, k] == 1, neighbours[block, k], own + 2 * width)
                 sums[row, entry] += blocks[row, k].astype(jnp.float32)
 
-        @pl.loop(0, own + 2 * width)
+        @pl.loop(0, own + 2 * width, unroll=5)
         def _(entry):
             totals[row, table[entry]] += sums[row, entry]
 

time: 22.6 us -> 22.5 us (level)
  no operation moved by 1% of the time
where the time goes in v5:
time: 22.5 us; the launch traced here: 22.4 us
  starting transfers between devices  13 us (58%)
  Pallas kernels  5.72 us (25%)
  waiting for transfers between devices  3.07 us (14%)
  other arithmetic  0.32 us (1%)
    ppermute x11, starting transfers between devices, across(): return lax.ppermute(value, 'col', [(i, i ^ step) for i in range(ncolour)])  7.85 us
    pallas_call x6, Pallas kernels, call(): pl.pallas_call(kernel, out_shape=tuple(outs), in_specs=ins, out_specs=(ou...  5.72 us
    ppermute x1, starting transfers between devices, per_device(): after = lax.ppermute(down, 'dom', [(j, i) for i, j in onward])  3.11 us
    ppermute x11, waiting for transfers between devices, across(): return lax.ppermute(value, 'col', [(i, i ^ step) for i in range(ncolour)])  3.06 us
    ppermute x1, starting transfers between devices, per_device(): before = lax.ppermute(up, 'dom', onward)  2.07 us
  transfers between devices with their start and end apart: 13, of which 1 were waited for; matrix products, arithmetic and copies ran while one was open for 1% of the time, Pallas kernels for 13%

profile of v5, /device:TPU:0, one launch (start us, length us, event | category | flops | bytes accessed | tf_op | source)
XLA Modules:
  0.0 22.4 jit_solution(16731545722540781767)
XLA Ops:
  0.0 1.7 %first_terms.1 = (bf16[1,2,2,128,128]{4,3,2,1,0:T(8,128)(2,1)S(1)}, bf16[1,2,2,128,128]{4,3,2,1,0:T(8,128)(2,1)S(1)}, f32[2,11,128,128]{3,2,1,0:T(8,128)S(1)}) custom-call(s32[8,27]{1,0:T(8,128)} %refs_0_.1, s32[8,27]{1,0:T(8,128)} %refs_1_.1, s32[64]{0:T(128)} %colour.3, s32[2,1,8]{2,1,0:T(1,128)} %bitcast.13, bf16[2,27,128,128]{3,2,1,0:T(8,128)(2,1)} %refs_4_.1), custom_call_target="tpu_custom_call" | custom-call | flops 1000 | bytes 1000 | tf_op jit(solution)/shard_map/first_terms/pallas_call | solution.py:51
  1.7 0.5 %collective-permute-start = (bf16[1,2,2,128,128]{4,3,2,1,0:T(8,128)(2,1)S(1)}, bf16[1,2,2,128,128]{4,3,2,1,0:T(8,128)(2,1)S(1)}, u32[]{:S(2)}, u32[]{:S(2)}) collective-permute-start(bf16[1,2,2,128,128]{4,3,2,1,0:T(8,128)(2,1)S(1)} %get-tuple-element.15.refs_0_.near0), channel_id=1, source_target_pairs={{0,1},{1,0},{2,3},{3,2},{4,5},{5,4},{6,7},{7,6},{8,9},{9,8},{10,11... | collective-permute-start | bytes 393224 | tf_op jit(solution)/shard_map/ppermute | solution.py:327
  2.2 0.1 collective-permute-start.4
  2.3 2.9 %collective-permute-start.7 = (bf16[1,2,2,128,128]{4,3,2,1,0:T(8,128)(2,1)S(1)}, bf16[1,2,2,128,128]{4,3,2,1,0:T(8,128)(2,1)S(1)}, u32[]{:S(2)}, u32[]{:S(2)}) collective-permute-start(bf16[1,2,2,128,128]{4,3,2,1,0:T(8,128)(2,1)S(1)} %get-tuple-element.15.refs_0_.near0), channel_id=1, source_target_pairs={{0,2},{1,3},{2,0},{3,1},{4,6},{5,7},{6,4},{7,5},{8,10},{9,11},{10,... | collective-permute-start | bytes 393224 | tf_op jit(solution)/shard_map/ppermute | solution.py:327
  5.2 0.0 collective-permute-start.1
  5.3 0.0 collective-permute-done.refs_1_.near1
  5.3 0.6 %borders.1 = (bf16[2,1,128,128]{3,2,1,0:T(8,128)(2,1)S(1)}, bf16[2,1,128,128]{3,2,1,0:T(8,128)(2,1)S(1)}) custom-call(s32[2,1,8]{2,1,0:T(1,128)S(1)} %bitcast.14, bf16[1,2,2,128,128]{4,3,2,1,0:T(8,128)(2,1)S(1)} %get-tuple-element.15.refs_0_.near0, bf16[1,2,2,128,128]{4,3,2,1,0:T(8,128)(2,1)S(1)} %get-tuple-element.16.far0.refs_0_, ...), custom_call_target="tpu_custom_call" | custom-call | flops 1000 | bytes 1000 | tf_op jit(solution)/shard_map/borders/pallas_call | solution.py:51
  5.9 2.1 %collective-permute-start.5 = (bf16[2,1,128,128]{3,2,1,0:T(8,128)(2,1)S(1)}, bf16[2,1,128,128]{3,2,1,0:T(8,128)(2,1)S(1)}, u32[]{:S(2)}, u32[]{:S(2)}) collective-permute-start(bf16[2,1,128,128]{3,2,1,0:T(8,128)(2,1)S(1)} %get-tuple-element.17), channel_id=1, source_target_pairs={{0,4},{4,8},{8,12},{12,16},{16,20},{20,24},{24,28},{28,0},{1,5},{5... | collective-permute-start | bytes 196616 | tf_op jit(solution)/shard_map/ppermute | solution.py:341
  8.0 3.1 %collective-permute-start.6 = (bf16[2,1,128,128]{3,2,1,0:T(8,128)(2,1)S(1)}, bf16[2,1,128,128]{3,2,1,0:T(8,128)(2,1)S(1)}, u32[]{:S(2)}, u32[]{:S(2)}) collective-permute-start(bf16[2,1,128,128]{3,2,1,0:T(8,128)(2,1)S(1)} %get-tuple-element.18), channel_id=1, source_target_pairs={{4,0},{8,4},{12,8},{16,12},{20,16},{24,20},{28,24},{0,28},{5,1},{9... | collective-permute-start | bytes 196616 | tf_op jit(solution)/shard_map/ppermute | solution.py:342
  11.1 0.0 collective-permute-done.7.refs_2_
  11.1 0.0 collective-permute-start.8
  11.1 1.7 %collective-permute-start.11 = (f16[2,2,128,128]{3,2,1,0:T(8,128)(2,1)S(1)}, f16[2,2,128,128]{3,2,1,0:T(8,128)(2,1)S(1)}, u32[]{:S(2)}, u32[]{:S(2)}) collective-permute-start(f16[2,2,128,128]{3,2,1,0:T(8,128)(2,1)S(1)} %get-tuple-element.23), channel_id=1, source_target_pairs={{0,2},{1,3},{2,0},{3,1},{4,6},{5,7},{6,4},{7,5},{8,10},{9,11},{10,... | collective-permute-start | bytes 393224 | tf_op jit(solution)/shard_map/ppermute | solution.py:327
  12.8 0.3 %split_sums.1.left = bf16[512,1024]{1,0:T(8,128)(2,1)S(1)} custom-call(f32[2,11,128,128]{3,2,1,0:T(8,128)S(1)} %get-tuple-element.14.sums), custom_call_target="tpu_custom_call" | custom-call | flops 1000 | bytes 1000 | tf_op jit(solution)/shard_map/split_sums/pallas_call | solution.py:51
  13.1 0.0 collective-permute-done.1.refs_2_
  13.1 0.3 %collective-permute-start.2 = (bf16[1,2,2,128,128]{4,3,2,1,0:T(8,128)(2,1)S(1)}, bf16[1,2,2,128,128]{4,3,2,1,0:T(8,128)(2,1)S(1)}, u32[]{:S(2)}, u32[]{:S(2)}) collective-permute-start(bf16[1,2,2,128,128]{4,3,2,1,0:T(8,128)(2,1)S(1)} %collective-permute-done.1.refs_2_), channel_id=1, source_target_pairs={{0,1},{1,0},{2,3},{3,2},{4,5},{5,4},{6,7},{7,6},{8,9},{9,8},{10,11... | collective-permute-start | bytes 393224 | tf_op jit(solution)/shard_map/ppermute | solution.py:327
  13.4 1.0 %image_terms.3 = f32[2,2,128,128]{3,2,1,0:T(8,128)S(1)} custom-call(s32[64]{0:T(128)S(1)} %copy-done, bf16[512,1024]{1,0:T(8,128)(2,1)S(1)} %split_sums.1.left, bf16[1,2,2,128,128]{4,3,2,1,0:T(8,128)(2,1)S(1)} %get-tuple-element.16.far0.refs_0_, bf16[1,2,2,128,128]{4,3,2,1,0:T(8,128)(2,1)S(1)} %collective-permute-done.4.far1.refs_1_, ...), custom_call_target="tpu_custom_call" | custom-call | flops 1000 | bytes 1000 | tf_op jit(solution)/shard_map/image_terms/pallas_call | solution.py:51
  14.6 0.7 %collective-permute-start.9 = (f16[4,128,128]{2,1,0:T(8,128)(2,1)S(1)}, f16[4,128,128]{2,1,0:T(8,128)(2,1)S(1)}, u32[]{:S(2)}, u32[]{:S(2)}) collective-permute-start(f16[4,128,128]{2,1,0:T(8,128)(2,1)S(1)} %pad_maximum_fusion.1), channel_id=1, source_target_pairs={{0,2},{1,3},{2,0},{3,1},{4,6},{5,7},{6,4},{7,5},{8,10},{9,11},{10,... | collective-permute-start | bytes 393224 | tf_op jit(solution)/shard_map/ppermute | solution.py:327
  15.3 1.0 %collective-permute-start.10 = (f16[2,128,128]{2,1,0:T(8,128)(2,1)S(1)}, f16[2,128,128]{2,1,0:T(8,128)(2,1)S(1)}, u32[]{:S(2)}, u32[]{:S(2)}) collective-permute-start(f16[2,128,128]{2,1,0:T(8,128)(2,1)S(1)} %get-tuple-element.29), channel_id=1, source_target_pairs={{0,3},{1,2},{2,1},{3,0},{4,7},{5,6},{6,5},{7,4},{8,11},{9,10},{10,... | collective-permute-start | bytes 196616 | tf_op jit(solution)/shard_map/ppermute | solution.py:327
  16.3 1.0 %image_terms.2.mine = f32[2,2,128,128]{3,2,1,0:T(8,128)S(1)} custom-call(s32[64]{0:T(128)S(1)} %copy-done, bf16[512,1024]{1,0:T(8,128)(2,1)S(1)} %split_sums.1.left, bf16[1,2,2,128,128]{4,3,2,1,0:T(8,128)(2,1)S(1)} %get-tuple-element.15.refs_0_.near0, bf16[1,2,2,128,128]{4,3,2,1,0:T(8,128)(2,1)S(1)} %collective-permute-done.refs_1_.near1, ...), custom_call_target="tpu_custom_call" | custom-call | flops 1000 | bytes 1000 | tf_op jit(solution)/shard_map/image_terms/pallas_call | solution.py:51
  17.3 0.6 %collective-permute-start.3 = (f16[2,128,128]{2,1,0:T(8,128)(2,1)S(1)}, f16[2,128,128]{2,1,0:T(8,128)(2,1)S(1)}, u32[]{:S(2)}, u32[]{:S(2)}) collective-permute-start(f16[2,128,128]{2,1,0:T(8,128)(2,1)S(1)} %fusion.1), channel_id=1, source_target_pairs={{0,1},{1,0},{2,3},{3,2},{4,5},{5,4},{6,7},{7,6},{8,9},{9,8},{10,11... | collective-permute-start | bytes 196616 | tf_op jit(solution)/shard_map/ppermute | solution.py:327
  17.9 0.1 pad_maximum_fusion
  18.0 0.1 collective-permute-start.12
  18.1 3.0 %collective-permute-done.10 = f16[2,128,128]{2,1,0:T(8,128)(2,1)S(1)} collective-permute-done((f16[2,128,128]{2,1,0:T(8,128)(2,1)S(1)}, f16[2,128,128]{2,1,0:T(8,128)(2,1)S(1)}, u32[]{:S(2)}, u32[]{:S(2)}) %collective-permute-start.10) | collective-permute-done | bytes 65568 | tf_op jit(solution)/shard_map/ppermute | solution.py:327
  21.2 1.1 %final_images.1 = f32[1024,128]{1,0:T(8,128)} custom-call(f32[2,2,128,128]{3,2,1,0:T(8,128)S(1)} %image_terms.2.mine, f32[2,128,128]{2,1,0:T(8,128)S(1)} %convert_element_type.39.refs_0_, f32[2,128,128]{2,1,0:T(8,128)S(1)} %get-tuple-element.28.refs_1_, f32[2,128,128]{2,1,0:T(8,128)S(1)} %convert_element_type.43.refs_2_, ...), custom_call_target="tpu_custom_call" | custom-call | flops 1000 | bytes 1000 | tf_op jit(solution)/shard_map/final_images/pallas_call | solution.py:51
  (25 shorter events, 0.3 us)
Async XLA Ops:
  0.0 5.3 %copy-start.1 = (s32[8,2,1]{0,2,1:T(1,128)S(1)}, s32[8,2,1]{0,2,1:T(1,128)}, u32[]{:S(2)}) copy-start(s32[8,2,1]{0,2,1:T(1,128)} %param.9) | copy-start | bytes 196
  1.7 3.6 %collective-permute-start = (bf16[1,2,2,128,128]{4,3,2,1,0:T(8,128)(2,1)S(1)}, bf16[1,2,2,128,128]{4,3,2,1,0:T(8,128)(2,1)S(1)}, u32[]{:S(2)}, u32[]{:S(2)}) collective-permute-start(bf16[1,2,2,128,128]{4,3,2,1,0:T(8,128)(2,1)S(1)} %get-tuple-element.15.refs_0_.near0), channel_id=1, source_target_pairs={{0,1},{1,0},{2,3},{3,2},{4,5},{5,4},{6,7},{7,6},{8,9},{9,8},{10,11... | collective-permute-start | bytes 393224 | tf_op jit(solution)/shard_map/ppermute | solution.py:327
  2.2 3.0 %collective-permute-start.4 = (bf16[1,2,2,128,128]{4,3,2,1,0:T(8,128)(2,1)S(1)}, bf16[1,2,2,128,128]{4,3,2,1,0:T(8,128)(2,1)S(1)}, u32[]{:S(2)}, u32[]{:S(2)}) collective-permute-start(bf16[1,2,2,128,128]{4,3,2,1,0:T(8,128)(2,1)S(1)} %get-tuple-element.16.far0.refs_0_), channel_id=1, source_target_pairs={{0,1},{1,0},{2,3},{3,2},{4,5},{5,4},{6,7},{7,6},{8,9},{9,8},{10,11... | collective-permute-start | bytes 393224 | tf_op jit(solution)/shard_map/ppermute | solution.py:327
  2.3 8.8 %collective-permute-start.7 = (bf16[1,2,2,128,128]{4,3,2,1,0:T(8,128)(2,1)S(1)}, bf16[1,2,2,128,128]{4,3,2,1,0:T(8,128)(2,1)S(1)}, u32[]{:S(2)}, u32[]{:S(2)}) collective-permute-start(bf16[1,2,2,128,128]{4,3,2,1,0:T(8,128)(2,1)S(1)} %get-tuple-element.15.refs_0_.near0), channel_id=1, source_target_pairs={{0,2},{1,3},{2,0},{3,1},{4,6},{5,7},{6,4},{7,5},{8,10},{9,11},{10,... | collective-permute-start | bytes 393224 | tf_op jit(solution)/shard_map/ppermute | solution.py:327
  5.2 7.8 %collective-permute-start.1 = (bf16[1,2,2,128,128]{4,3,2,1,0:T(8,128)(2,1)S(1)}, bf16[1,2,2,128,128]{4,3,2,1,0:T(8,128)(2,1)S(1)}, u32[]{:S(2)}, u32[]{:S(2)}) collective-permute-start(bf16[1,2,2,128,128]{4,3,2,1,0:T(8,128)(2,1)S(1)} %get-tuple-element.16.far0.refs_0_), channel_id=1, source_target_pairs={{0,2},{1,3},{2,0},{3,1},{4,6},{5,7},{6,4},{7,5},{8,10},{9,11},{10,... | collective-permute-start | bytes 393224 | tf_op jit(solution)/shard_map/ppermute | solution.py:327
  5.9 8.5 %collective-permute-start.5 = (bf16[2,1,128,128]{3,2,1,0:T(8,128)(2,1)S(1)}, bf16[2,1,128,128]{3,2,1,0:T(8,128)(2,1)S(1)}, u32[]{:S(2)}, u32[]{:S(2)}) collective-permute-start(bf16[2,1,128,128]{3,2,1,0:T(8,128)(2,1)S(1)} %get-tuple-element.17), channel_id=1, source_target_pairs={{0,4},{4,8},{8,12},{12,16},{16,20},{20,24},{24,28},{28,0},{1,5},{5... | collective-permute-start | bytes 196616 | tf_op jit(solution)/shard_map/ppermute | solution.py:341
  8.0 6.4 %collective-permute-start.6 = (bf16[2,1,128,128]{3,2,1,0:T(8,128)(2,1)S(1)}, bf16[2,1,128,128]{3,2,1,0:T(8,128)(2,1)S(1)}, u32[]{:S(2)}, u32[]{:S(2)}) collective-permute-start(bf16[2,1,128,128]{3,2,1,0:T(8,128)(2,1)S(1)} %get-tuple-element.18), channel_id=1, source_target_pairs={{4,0},{8,4},{12,8},{16,12},{20,16},{24,20},{28,24},{0,28},{5,1},{9... | collective-permute-start | bytes 196616 | tf_op jit(solution)/shard_map/ppermute | solution.py:342
  11.1 2.3 %collective-permute-start.8 = (bf16[1,2,2,128,128]{4,3,2,1,0:T(8,128)(2,1)S(1)}, bf16[1,2,2,128,128]{4,3,2,1,0:T(8,128)(2,1)S(1)}, u32[]{:S(2)}, u32[]{:S(2)}) collective-permute-start(bf16[1,2,2,128,128]{4,3,2,1,0:T(8,128)(2,1)S(1)} %collective-permute-done.7.refs_2_), channel_id=1, source_target_pairs={{0,1},{1,0},{2,3},{3,2},{4,5},{5,4},{6,7},{7,6},{8,9},{9,8},{10,11... | collective-permute-start | bytes 393224 | tf_op jit(solution)/shard_map/ppermute | solution.py:327
  11.1 2.3 %copy-start = (s32[64]{0:T(128)S(1)}, s32[64]{0:T(128)}, u32[]{:S(2)}) copy-start(s32[64]{0:T(128)} %colour.3) | copy-start | bytes 772
  11.1 6.7 %collective-permute-start.11 = (f16[2,2,128,128]{3,2,1,0:T(8,128)(2,1)S(1)}, f16[2,2,128,128]{3,2,1,0:T(8,128)(2,1)S(1)}, u32[]{:S(2)}, u32[]{:S(2)}) collective-permute-start(f16[2,2,128,128]{3,2,1,0:T(8,128)(2,1)S(1)} %get-tuple-element.23), channel_id=1, source_target_pairs={{0,2},{1,3},{2,0},{3,1},{4,6},{5,7},{6,4},{7,5},{8,10},{9,11},{10,... | collective-permute-start | bytes 393224 | tf_op jit(solution)/shard_map/ppermute | solution.py:327
  13.1 3.2 %collective-permute-start.2 = (bf16[1,2,2,128,128]{4,3,2,1,0:T(8,128)(2,1)S(1)}, bf16[1,2,2,128,128]{4,3,2,1,0:T(8,128)(2,1)S(1)}, u32[]{:S(2)}, u32[]{:S(2)}) collective-permute-start(bf16[1,2,2,128,128]{4,3,2,1,0:T(8,128)(2,1)S(1)} %collective-permute-done.1.refs_2_), channel_id=1, source_target_pairs={{0,1},{1,0},{2,3},{3,2},{4,5},{5,4},{6,7},{7,6},{8,9},{9,8},{10,11... | collective-permute-start | bytes 393224 | tf_op jit(solution)/shard_map/ppermute | solution.py:327
  14.6 6.6 %collective-permute-start.9 = (f16[4,128,128]{2,1,0:T(8,128)(2,1)S(1)}, f16[4,128,128]{2,1,0:T(8,128)(2,1)S(1)}, u32[]{:S(2)}, u32[]{:S(2)}) collective-permute-start(f16[4,128,128]{2,1,0:T(8,128)(2,1)S(1)} %pad_maximum_fusion.1), channel_id=1, source_target_pairs={{0,2},{1,3},{2,0},{3,1},{4,6},{5,7},{6,4},{7,5},{8,10},{9,11},{10,... | collective-permute-start | bytes 393224 | tf_op jit(solution)/shard_map/ppermute | solution.py:327
  15.3 5.8 %collective-permute-start.10 = (f16[2,128,128]{2,1,0:T(8,128)(2,1)S(1)}, f16[2,128,128]{2,1,0:T(8,128)(2,1)S(1)}, u32[]{:S(2)}, u32[]{:S(2)}) collective-permute-start(f16[2,128,128]{2,1,0:T(8,128)(2,1)S(1)} %get-tuple-element.29), channel_id=1, source_target_pairs={{0,3},{1,2},{2,1},{3,0},{4,7},{5,6},{6,5},{7,4},{8,11},{9,10},{10,... | collective-permute-start | bytes 196616 | tf_op jit(solution)/shard_map/ppermute | solution.py:327
  17.3 3.8 %collective-permute-start.3 = (f16[2,128,128]{2,1,0:T(8,128)(2,1)S(1)}, f16[2,128,128]{2,1,0:T(8,128)(2,1)S(1)}, u32[]{:S(2)}, u32[]{:S(2)}) collective-permute-start(f16[2,128,128]{2,1,0:T(8,128)(2,1)S(1)} %fusion.1), channel_id=1, source_target_pairs={{0,1},{1,0},{2,3},{3,2},{4,5},{5,4},{6,7},{7,6},{8,9},{9,8},{10,11... | collective-permute-start | bytes 196616 | tf_op jit(solution)/shard_map/ppermute | solution.py:327
  18.0 3.2 %collective-permute-start.12 = (f16[4,2,128,128]{3,2,1,0:T(8,128)(2,1)S(1)}, f16[4,2,128,128]{3,2,1,0:T(8,128)(2,1)S(1)}, u32[]{:S(2)}, u32[]{:S(2)}) collective-permute-start(f16[4,2,128,128]{3,2,1,0:T(8,128)(2,1)S(1)} %pad_maximum_fusion), channel_id=1, source_target_pairs={{0,1},{1,0},{2,3},{3,2},{4,5},{5,4},{6,7},{7,6},{8,9},{9,8},{10,11... | collective-permute-start | bytes 786440 | tf_op jit(solution)/shard_map/ppermute | solution.py:327

commit v6 on v5

--- a/solution.py
+++ b/solution.py
@@ -223,14 +223,12 @@
             turn = ((relative // 2) % half) ^ r
             for row in range(rows):
                 right.append(jnp.concatenate([piece[turn, 0, row], piece[turn, 1, row]], axis=1))
-        total = jnp.dot(
-            left[...], jnp.concatenate(right, axis=0), preferred_element_type=jnp.float32
-        )
+        right = jnp.concatenate(right, axis=0)
         for row in range(rows):
             mine = colour[domain * own + shade * rows + row] ^ base
-            high = total[2 * row * orbits : (2 * row + 1) * orbits]
-            low = total[(2 * row + 1) * orbits : (2 * row + 2) * orbits]
-            product = high + low
+            both = left[2 * row * orbits : (2 * row + 2) * orbits, :]
+            total = jnp.dot(both, right, preferred_element_type=jnp.float32)
+            product = total[:orbits] + total[orbits:]
             for q in range(2):
                 first = pieces[0][r, q, row].astype(jnp.float32)
                 relative = 2 * (r + (half if upper_half else 0)) + q

time: 22.5 us -> 22.5 us (level)
  no operation moved by 1% of the time
where the time goes in v6:
time: 22.5 us; the launch traced here: 22.4 us
  starting transfers between devices  13 us (58%)
  Pallas kernels  5.77 us (26%)
  waiting for transfers between devices  3.04 us (14%)
  other arithmetic  0.32 us (1%)
    ppermute x11, starting transfers between devices, across(): return lax.ppermute(value, 'col', [(i, i ^ step) for i in range(ncolour)])  7.85 us
    pallas_call x6, Pallas kernels, call(): pl.pallas_call(kernel, out_shape=tuple(outs), in_specs=ins, out_specs=(ou...  5.77 us
    ppermute x1, starting transfers between devices, per_device(): after = lax.ppermute(down, 'dom', [(j, i) for i, j in onward])  3.09 us
    ppermute x11, waiting for transfers between devices, across(): return lax.ppermute(value, 'col', [(i, i ^ step) for i in range(ncolour)])  3.04 us
    ppermute x1, starting transfers between devices, per_device(): before = lax.ppermute(up, 'dom', onward)  2.08 us
  transfers between devices with their start and end apart: 13, of which 1 were waited for; matrix products, arithmetic and copies ran while one was open for 1% of the time, Pallas kernels for 13%

profile of v6, /device:TPU:0, one launch (start us, length us, event | category | flops | bytes accessed | tf_op | source)
XLA Modules:
  0.0 22.4 jit_solution(11064059265449247781)
XLA Ops:
  0.0 1.7 %first_terms.1 = (bf16[1,2,2,128,128]{4,3,2,1,0:T(8,128)(2,1)S(1)}, bf16[1,2,2,128,128]{4,3,2,1,0:T(8,128)(2,1)S(1)}, f32[2,11,128,128]{3,2,1,0:T(8,128)S(1)}) custom-call(s32[8,27]{1,0:T(8,128)} %refs_0_.1, s32[8,27]{1,0:T(8,128)} %refs_1_.1, s32[64]{0:T(128)} %colour.3, s32[2,1,8]{2,1,0:T(1,128)} %bitcast.13, bf16[2,27,128,128]{3,2,1,0:T(8,128)(2,1)} %refs_4_.1), custom_call_target="tpu_custom_call" | custom-call | flops 1000 | bytes 1000 | tf_op jit(solution)/shard_map/first_terms/pallas_call | solution.py:51
  1.7 0.5 %collective-permute-start = (bf16[1,2,2,128,128]{4,3,2,1,0:T(8,128)(2,1)S(1)}, bf16[1,2,2,128,128]{4,3,2,1,0:T(8,128)(2,1)S(1)}, u32[]{:S(2)}, u32[]{:S(2)}) collective-permute-start(bf16[1,2,2,128,128]{4,3,2,1,0:T(8,128)(2,1)S(1)} %get-tuple-element.15.refs_0_.near0), channel_id=1, source_target_pairs={{0,1},{1,0},{2,3},{3,2},{4,5},{5,4},{6,7},{7,6},{8,9},{9,8},{10,11... | collective-permute-start | bytes 393224 | tf_op jit(solution)/shard_map/ppermute | solution.py:325
  2.2 0.1 collective-permute-start.4
  2.3 2.9 %collective-permute-start.7 = (bf16[1,2,2,128,128]{4,3,2,1,0:T(8,128)(2,1)S(1)}, bf16[1,2,2,128,128]{4,3,2,1,0:T(8,128)(2,1)S(1)}, u32[]{:S(2)}, u32[]{:S(2)}) collective-permute-start(bf16[1,2,2,128,128]{4,3,2,1,0:T(8,128)(2,1)S(1)} %get-tuple-element.15.refs_0_.near0), channel_id=1, source_target_pairs={{0,2},{1,3},{2,0},{3,1},{4,6},{5,7},{6,4},{7,5},{8,10},{9,11},{10,... | collective-permute-start | bytes 393224 | tf_op jit(solution)/shard_map/ppermute | solution.py:325
  5.2 0.0 collective-permute-start.1
  5.3 0.0 collective-permute-done.refs_1_.near1
  5.3 0.0 collective-permute-done.4.far1.refs_1_
  5.3 0.6 %borders.1 = (bf16[2,1,128,128]{3,2,1,0:T(8,128)(2,1)S(1)}, bf16[2,1,128,128]{3,2,1,0:T(8,128)(2,1)S(1)}) custom-call(s32[2,1,8]{2,1,0:T(1,128)S(1)} %bitcast.14, bf16[1,2,2,128,128]{4,3,2,1,0:T(8,128)(2,1)S(1)} %get-tuple-element.15.refs_0_.near0, bf16[1,2,2,128,128]{4,3,2,1,0:T(8,128)(2,1)S(1)} %get-tuple-element.16.far0.refs_0_, ...), custom_call_target="tpu_custom_call" | custom-call | flops 1000 | bytes 1000 | tf_op jit(solution)/shard_map/borders/pallas_call | solution.py:51
  5.9 2.1 %collective-permute-start.5 = (bf16[2,1,128,128]{3,2,1,0:T(8,128)(2,1)S(1)}, bf16[2,1,128,128]{3,2,1,0:T(8,128)(2,1)S(1)}, u32[]{:S(2)}, u32[]{:S(2)}) collective-permute-start(bf16[2,1,128,128]{3,2,1,0:T(8,128)(2,1)S(1)} %get-tuple-element.17), channel_id=1, source_target_pairs={{0,4},{4,8},{8,12},{12,16},{16,20},{20,24},{24,28},{28,0},{1,5},{5... | collective-permute-start | bytes 196616 | tf_op jit(solution)/shard_map/ppermute | solution.py:339
  8.0 3.1 %collective-permute-start.6 = (bf16[2,1,128,128]{3,2,1,0:T(8,128)(2,1)S(1)}, bf16[2,1,128,128]{3,2,1,0:T(8,128)(2,1)S(1)}, u32[]{:S(2)}, u32[]{:S(2)}) collective-permute-start(bf16[2,1,128,128]{3,2,1,0:T(8,128)(2,1)S(1)} %get-tuple-element.18), channel_id=1, source_target_pairs={{4,0},{8,4},{12,8},{16,12},{20,16},{24,20},{28,24},{0,28},{5,1},{9... | collective-permute-start | bytes 196616 | tf_op jit(solution)/shard_map/ppermute | solution.py:340
  11.1 0.0 collective-permute-done.7.refs_2_
  11.1 0.0 collective-permute-start.8
  11.1 1.7 %collective-permute-start.11 = (f16[2,2,128,128]{3,2,1,0:T(8,128)(2,1)S(1)}, f16[2,2,128,128]{3,2,1,0:T(8,128)(2,1)S(1)}, u32[]{:S(2)}, u32[]{:S(2)}) collective-permute-start(f16[2,2,128,128]{3,2,1,0:T(8,128)(2,1)S(1)} %get-tuple-element.23), channel_id=1, source_target_pairs={{0,2},{1,3},{2,0},{3,1},{4,6},{5,7},{6,4},{7,5},{8,10},{9,11},{10,... | collective-permute-start | bytes 393224 | tf_op jit(solution)/shard_map/ppermute | solution.py:325
  12.8 0.3 %split_sums.1.left = bf16[512,1024]{1,0:T(8,128)(2,1)S(1)} custom-call(f32[2,11,128,128]{3,2,1,0:T(8,128)S(1)} %get-tuple-element.14.sums), custom_call_target="tpu_custom_call" | custom-call | flops 1000 | bytes 1000 | tf_op jit(solution)/shard_map/split_sums/pallas_call | solution.py:51
  13.1 0.3 %collective-permute-start.2 = (bf16[1,2,2,128,128]{4,3,2,1,0:T(8,128)(2,1)S(1)}, bf16[1,2,2,128,128]{4,3,2,1,0:T(8,128)(2,1)S(1)}, u32[]{:S(2)}, u32[]{:S(2)}) collective-permute-start(bf16[1,2,2,128,128]{4,3,2,1,0:T(8,128)(2,1)S(1)} %collective-permute-done.1.refs_2_), channel_id=1, source_target_pairs={{0,1},{1,0},{2,3},{3,2},{4,5},{5,4},{6,7},{7,6},{8,9},{9,8},{10,11... | collective-permute-start | bytes 393224 | tf_op jit(solution)/shard_map/ppermute | solution.py:325
  13.4 1.0 %image_terms.3 = f32[2,2,128,128]{3,2,1,0:T(8,128)S(1)} custom-call(s32[64]{0:T(128)S(1)} %copy-done, bf16[512,1024]{1,0:T(8,128)(2,1)S(1)} %split_sums.1.left, bf16[1,2,2,128,128]{4,3,2,1,0:T(8,128)(2,1)S(1)} %get-tuple-element.16.far0.refs_0_, bf16[1,2,2,128,128]{4,3,2,1,0:T(8,128)(2,1)S(1)} %collective-permute-done.4.far1.refs_1_, ...), custom_call_target="tpu_custom_call" | custom-call | flops 1000 | bytes 1000 | tf_op jit(solution)/shard_map/image_terms/pallas_call | solution.py:51
  14.6 0.7 %collective-permute-start.9 = (f16[4,128,128]{2,1,0:T(8,128)(2,1)S(1)}, f16[4,128,128]{2,1,0:T(8,128)(2,1)S(1)}, u32[]{:S(2)}, u32[]{:S(2)}) collective-permute-start(f16[4,128,128]{2,1,0:T(8,128)(2,1)S(1)} %pad_maximum_fusion.1), channel_id=1, source_target_pairs={{0,2},{1,3},{2,0},{3,1},{4,6},{5,7},{6,4},{7,5},{8,10},{9,11},{10,... | collective-permute-start | bytes 393224 | tf_op jit(solution)/shard_map/ppermute | solution.py:325
  15.3 1.0 %collective-permute-start.10 = (f16[2,128,128]{2,1,0:T(8,128)(2,1)S(1)}, f16[2,128,128]{2,1,0:T(8,128)(2,1)S(1)}, u32[]{:S(2)}, u32[]{:S(2)}) collective-permute-start(f16[2,128,128]{2,1,0:T(8,128)(2,1)S(1)} %get-tuple-element.29), channel_id=1, source_target_pairs={{0,3},{1,2},{2,1},{3,0},{4,7},{5,6},{6,5},{7,4},{8,11},{9,10},{10,... | collective-permute-start | bytes 196616 | tf_op jit(solution)/shard_map/ppermute | solution.py:325
  16.3 1.0 %image_terms.2.mine = f32[2,2,128,128]{3,2,1,0:T(8,128)S(1)} custom-call(s32[64]{0:T(128)S(1)} %copy-done, bf16[512,1024]{1,0:T(8,128)(2,1)S(1)} %split_sums.1.left, bf16[1,2,2,128,128]{4,3,2,1,0:T(8,128)(2,1)S(1)} %get-tuple-element.15.refs_0_.near0, bf16[1,2,2,128,128]{4,3,2,1,0:T(8,128)(2,1)S(1)} %collective-permute-done.refs_1_.near1, ...), custom_call_target="tpu_custom_call" | custom-call | flops 1000 | bytes 1000 | tf_op jit(solution)/shard_map/image_terms/pallas_call | solution.py:51
  17.3 0.6 %collective-permute-start.3 = (f16[2,128,128]{2,1,0:T(8,128)(2,1)S(1)}, f16[2,128,128]{2,1,0:T(8,128)(2,1)S(1)}, u32[]{:S(2)}, u32[]{:S(2)}) collective-permute-start(f16[2,128,128]{2,1,0:T(8,128)(2,1)S(1)} %fusion.1), channel_id=1, source_target_pairs={{0,1},{1,0},{2,3},{3,2},{4,5},{5,4},{6,7},{7,6},{8,9},{9,8},{10,11... | collective-permute-start | bytes 196616 | tf_op jit(solution)/shard_map/ppermute | solution.py:325
  17.9 0.1 pad_maximum_fusion
  18.0 0.1 collective-permute-start.12
  18.1 3.0 %collective-permute-done.10 = f16[2,128,128]{2,1,0:T(8,128)(2,1)S(1)} collective-permute-done((f16[2,128,128]{2,1,0:T(8,128)(2,1)S(1)}, f16[2,128,128]{2,1,0:T(8,128)(2,1)S(1)}, u32[]{:S(2)}, u32[]{:S(2)}) %collective-permute-start.10) | collective-permute-done | bytes 65568 | tf_op jit(solution)/shard_map/ppermute | solution.py:325
  21.3 1.1 %final_images.1 = f32[1024,128]{1,0:T(8,128)} custom-call(f32[2,2,128,128]{3,2,1,0:T(8,128)S(1)} %image_terms.2.mine, f32[2,128,128]{2,1,0:T(8,128)S(1)} %convert_element_type.39.refs_0_, f32[2,128,128]{2,1,0:T(8,128)S(1)} %get-tuple-element.28.refs_1_, f32[2,128,128]{2,1,0:T(8,128)S(1)} %convert_element_type.43.refs_2_, ...), custom_call_target="tpu_custom_call" | custom-call | flops 1000 | bytes 1000 | tf_op jit(solution)/shard_map/final_images/pallas_call | solution.py:51
  (25 shorter events, 0.3 us)
Async XLA Ops:
  0.0 5.3 %copy-start.1 = (s32[8,2,1]{0,2,1:T(1,128)S(1)}, s32[8,2,1]{0,2,1:T(1,128)}, u32[]{:S(2)}) copy-start(s32[8,2,1]{0,2,1:T(1,128)} %param.9) | copy-start | bytes 196
  1.7 3.6 %collective-permute-start = (bf16[1,2,2,128,128]{4,3,2,1,0:T(8,128)(2,1)S(1)}, bf16[1,2,2,128,128]{4,3,2,1,0:T(8,128)(2,1)S(1)}, u32[]{:S(2)}, u32[]{:S(2)}) collective-permute-start(bf16[1,2,2,128,128]{4,3,2,1,0:T(8,128)(2,1)S(1)} %get-tuple-element.15.refs_0_.near0), channel_id=1, source_target_pairs={{0,1},{1,0},{2,3},{3,2},{4,5},{5,4},{6,7},{7,6},{8,9},{9,8},{10,11... | collective-permute-start | bytes 393224 | tf_op jit(solution)/shard_map/ppermute | solution.py:325
  2.2 3.0 %collective-permute-start.4 = (bf16[1,2,2,128,128]{4,3,2,1,0:T(8,128)(2,1)S(1)}, bf16[1,2,2,128,128]{4,3,2,1,0:T(8,128)(2,1)S(1)}, u32[]{:S(2)}, u32[]{:S(2)}) collective-permute-start(bf16[1,2,2,128,128]{4,3,2,1,0:T(8,128)(2,1)S(1)} %get-tuple-element.16.far0.refs_0_), channel_id=1, source_target_pairs={{0,1},{1,0},{2,3},{3,2},{4,5},{5,4},{6,7},{7,6},{8,9},{9,8},{10,11... | collective-permute-start | bytes 393224 | tf_op jit(solution)/shard_map/ppermute | solution.py:325
  2.3 8.8 %collective-permute-start.7 = (bf16[1,2,2,128,128]{4,3,2,1,0:T(8,128)(2,1)S(1)}, bf16[1,2,2,128,128]{4,3,2,1,0:T(8,128)(2,1)S(1)}, u32[]{:S(2)}, u32[]{:S(2)}) collective-permute-start(bf16[1,2,2,128,128]{4,3,2,1,0:T(8,128)(2,1)S(1)} %get-tuple-element.15.refs_0_.near0), channel_id=1, source_target_pairs={{0,2},{1,3},{2,0},{3,1},{4,6},{5,7},{6,4},{7,5},{8,10},{9,11},{10,... | collective-permute-start | bytes 393224 | tf_op jit(solution)/shard_map/ppermute | solution.py:325
  5.2 7.8 %collective-permute-start.1 = (bf16[1,2,2,128,128]{4,3,2,1,0:T(8,128)(2,1)S(1)}, bf16[1,2,2,128,128]{4,3,2,1,0:T(8,128)(2,1)S(1)}, u32[]{:S(2)}, u32[]{:S(2)}) collective-permute-start(bf16[1,2,2,128,128]{4,3,2,1,0:T(8,128)(2,1)S(1)} %get-tuple-element.16.far0.refs_0_), channel_id=1, source_target_pairs={{0,2},{1,3},{2,0},{3,1},{4,6},{5,7},{6,4},{7,5},{8,10},{9,11},{10,... | collective-permute-start | bytes 393224 | tf_op jit(solution)/shard_map/ppermute | solution.py:325
  5.9 8.5 %collective-permute-start.5 = (bf16[2,1,128,128]{3,2,1,0:T(8,128)(2,1)S(1)}, bf16[2,1,128,128]{3,2,1,0:T(8,128)(2,1)S(1)}, u32[]{:S(2)}, u32[]{:S(2)}) collective-permute-start(bf16[2,1,128,128]{3,2,1,0:T(8,128)(2,1)S(1)} %get-tuple-element.17), channel_id=1, source_target_pairs={{0,4},{4,8},{8,12},{12,16},{16,20},{20,24},{24,28},{28,0},{1,5},{5... | collective-permute-start | bytes 196616 | tf_op jit(solution)/shard_map/ppermute | solution.py:339
  8.0 6.4 %collective-permute-start.6 = (bf16[2,1,128,128]{3,2,1,0:T(8,128)(2,1)S(1)}, bf16[2,1,128,128]{3,2,1,0:T(8,128)(2,1)S(1)}, u32[]{:S(2)}, u32[]{:S(2)}) collective-permute-start(bf16[2,1,128,128]{3,2,1,0:T(8,128)(2,1)S(1)} %get-tuple-element.18), channel_id=1, source_target_pairs={{4,0},{8,4},{12,8},{16,12},{20,16},{24,20},{28,24},{0,28},{5,1},{9... | collective-permute-start | bytes 196616 | tf_op jit(solution)/shard_map/ppermute | solution.py:340
  11.1 2.3 %collective-permute-start.8 = (bf16[1,2,2,128,128]{4,3,2,1,0:T(8,128)(2,1)S(1)}, bf16[1,2,2,128,128]{4,3,2,1,0:T(8,128)(2,1)S(1)}, u32[]{:S(2)}, u32[]{:S(2)}) collective-permute-start(bf16[1,2,2,128,128]{4,3,2,1,0:T(8,128)(2,1)S(1)} %collective-permute-done.7.refs_2_), channel_id=1, source_target_pairs={{0,1},{1,0},{2,3},{3,2},{4,5},{5,4},{6,7},{7,6},{8,9},{9,8},{10,11... | collective-permute-start | bytes 393224 | tf_op jit(solution)/shard_map/ppermute | solution.py:325
  11.1 2.3 %copy-start = (s32[64]{0:T(128)S(1)}, s32[64]{0:T(128)}, u32[]{:S(2)}) copy-start(s32[64]{0:T(128)} %colour.3) | copy-start | bytes 772
  11.1 6.8 %collective-permute-start.11 = (f16[2,2,128,128]{3,2,1,0:T(8,128)(2,1)S(1)}, f16[2,2,128,128]{3,2,1,0:T(8,128)(2,1)S(1)}, u32[]{:S(2)}, u32[]{:S(2)}) collective-permute-start(f16[2,2,128,128]{3,2,1,0:T(8,128)(2,1)S(1)} %get-tuple-element.23), channel_id=1, source_target_pairs={{0,2},{1,3},{2,0},{3,1},{4,6},{5,7},{6,4},{7,5},{8,10},{9,11},{10,... | collective-permute-start | bytes 393224 | tf_op jit(solution)/shard_map/ppermute | solution.py:325
  13.1 3.2 %collective-permute-start.2 = (bf16[1,2,2,128,128]{4,3,2,1,0:T(8,128)(2,1)S(1)}, bf16[1,2,2,128,128]{4,3,2,1,0:T(8,128)(2,1)S(1)}, u32[]{:S(2)}, u32[]{:S(2)}) collective-permute-start(bf16[1,2,2,128,128]{4,3,2,1,0:T(8,128)(2,1)S(1)} %collective-permute-done.1.refs_2_), channel_id=1, source_target_pairs={{0,1},{1,0},{2,3},{3,2},{4,5},{5,4},{6,7},{7,6},{8,9},{9,8},{10,11... | collective-permute-start | bytes 393224 | tf_op jit(solution)/shard_map/ppermute | solution.py:325
  14.6 6.6 %collective-permute-start.9 = (f16[4,128,128]{2,1,0:T(8,128)(2,1)S(1)}, f16[4,128,128]{2,1,0:T(8,128)(2,1)S(1)}, u32[]{:S(2)}, u32[]{:S(2)}) collective-permute-start(f16[4,128,128]{2,1,0:T(8,128)(2,1)S(1)} %pad_maximum_fusion.1), channel_id=1, source_target_pairs={{0,2},{1,3},{2,0},{3,1},{4,6},{5,7},{6,4},{7,5},{8,10},{9,11},{10,... | collective-permute-start | bytes 393224 | tf_op jit(solution)/shard_map/ppermute | solution.py:325
  15.3 5.8 %collective-permute-start.10 = (f16[2,128,128]{2,1,0:T(8,128)(2,1)S(1)}, f16[2,128,128]{2,1,0:T(8,128)(2,1)S(1)}, u32[]{:S(2)}, u32[]{:S(2)}) collective-permute-start(f16[2,128,128]{2,1,0:T(8,128)(2,1)S(1)} %get-tuple-element.29), channel_id=1, source_target_pairs={{0,3},{1,2},{2,1},{3,0},{4,7},{5,6},{6,5},{7,4},{8,11},{9,10},{10,... | collective-permute-start | bytes 196616 | tf_op jit(solution)/shard_map/ppermute | solution.py:325
  17.3 3.8 %collective-permute-start.3 = (f16[2,128,128]{2,1,0:T(8,128)(2,1)S(1)}, f16[2,128,128]{2,1,0:T(8,128)(2,1)S(1)}, u32[]{:S(2)}, u32[]{:S(2)}) collective-permute-start(f16[2,128,128]{2,1,0:T(8,128)(2,1)S(1)} %fusion.1), channel_id=1, source_target_pairs={{0,1},{1,0},{2,3},{3,2},{4,5},{5,4},{6,7},{7,6},{8,9},{9,8},{10,11... | collective-permute-start | bytes 196616 | tf_op jit(solution)/shard_map/ppermute | solution.py:325
  18.0 3.2 %collective-permute-start.12 = (f16[4,2,128,128]{3,2,1,0:T(8,128)(2,1)S(1)}, f16[4,2,128,128]{3,2,1,0:T(8,128)(2,1)S(1)}, u32[]{:S(2)}, u32[]{:S(2)}) collective-permute-start(f16[4,2,128,128]{3,2,1,0:T(8,128)(2,1)S(1)} %pad_maximum_fusion), channel_id=1, source_target_pairs={{0,1},{1,0},{2,3},{3,2},{4,5},{5,4},{6,7},{7,6},{8,9},{9,8},{10,11... | collective-permute-start | bytes 786440 | tf_op jit(solution)/shard_map/ppermute | solution.py:325
